TPU v7x, 128 devices: a whole 4x4x4 slice. The times are simulated.
128 devices in a mesh: gx: 16 (over z, y_lo, core), gy: 8 (over x, y_hi).
Axes of the slice: x: 4, y: 4 (y_hi: 2, y_lo: 2; y = y_hi * 2 + y_lo), z: 4, core: 2. Of those that a mesh axis runs over, the one named last changes fastest.
Arguments:
- source_hat: float32 [2, 3, 256, 256, 256], P(None, None, 'gx', 'gy'), may hold values from -0.0014648438 to 0.0014648438
- particle_start: int32 [3, 262144], P(None, ('gx', 'gy')), may hold values from 0 to 255, as said below
- particle_offset: float32 [3, 262144], P(None, ('gx', 'gy')), may hold values from 0 to 1
- ghost_start: int32 [3, 3, 65536], P(None, None, ('gx', 'gy')), may hold values from 0 to 255, as said below
- ghost_offset: float32 [3, 3, 65536], P(None, None, ('gx', 'gy')), may hold values from 0 to 1, as said below
- ghost_slot: int32 [3, 65536], P(None, ('gx', 'gy')), may hold values from 0 to 2047, as said below
- counts: int32 [128, 4], P(('gx', 'gy')), may hold values from 0 to 2048, as said below
Outputs:
- velocity_far: float32 [3, 262144], P(None, ('gx', 'gy'))
- strain_far: float32 [5, 262144], P(None, ('gx', 'gy'))
Inputs may be any that keep to these rules, and one draw needn't show every extreme that they name: `particle_start`: on device (a, b), a its gx index and b its gy index, every slot's x start lies in [b * 32, (b + 1) * 32) and its z start in [a * 16, (a + 1) * 16). `counts`: row of a device: its live own slots (the slots below this count are live), then the live entries of ghost groups 0, 1, 2 (the entries below each count are live); each ghost count is at most 512. `ghost_slot`: group 0 of device (a, b) lists particles of device (a, b - 1), group 1 of (a - 1, b), group 2 of (a - 1, b - 1), indices modulo the axis sizes; every entry is a slot index of that owner, below 2048; its live entries name distinct live slots of that owner, and they are exactly the owner's live particles whose support reaches the device's brick. `ghost_start`: A live ghost entry repeats the start of the owner's slot that ghost_slot names. `ghost_offset`: A live ghost entry repeats the offset of the owner's slot that ghost_slot names.
All inputs are finite; a program needn't handle non-finite values.
Results may differ from a plain program's by a relative error of at most 0.008.
Values sent between devices are 32-bit elements; how exact they have to be, the bound alone decides.
No kernel may reach another device: no remote copies, remote signals or barrier semaphores. Data moves between devices by JAX's collectives and lax.ppermute only.
A program may use at most 192 MiB of HBM per device.

v0:
```python
import math

import jax
import jax.numpy as jnp
from jax import lax
from jax.sharding import PartitionSpec as P

SUPPORT = 8


TWO_PI = 2.0 * math.pi
HIGHEST = lax.Precision.HIGHEST


def passed_along(block, axis, distance):
    devices = range(lax.axis_size(axis))
    route = [((i - distance) % len(devices), i) for i in devices]
    return lax.ppermute(block, axis, route)


def signed_modes(indices, grid_size):
    return jnp.where(indices < grid_size // 2, indices, indices - grid_size).astype(jnp.float32)


def times_ik(field, wavenumber, part_axis):
    real_part = jnp.take(field, 0, axis=part_axis)
    imag_part = jnp.take(field, 1, axis=part_axis)
    return jnp.stack([-wavenumber * imag_part, wavenumber * real_part], axis=part_axis)


def phase_table(grid_size, pieces, piece_width):
    table_shape = (grid_size, pieces, piece_width)
    mode_index = lax.broadcasted_iota(jnp.int32, table_shape, 0)
    position = lax.broadcasted_iota(jnp.int32, table_shape, 1) * piece_width + lax.broadcasted_iota(
        jnp.int32, table_shape, 2
    )
    phase_angle = (mode_index * position % grid_size).astype(jnp.float32) * (TWO_PI / grid_size)
    cosine = jnp.cos(phase_angle)
    sine_part = jnp.sin(phase_angle)
    from_real = jnp.stack([cosine, sine_part], axis=-1)
    from_imag = jnp.stack([-sine_part, cosine], axis=-1)
    return jnp.stack([from_real, from_imag], axis=1)


def spread_weight(distance, offset_value, support):
    shifted = distance.astype(jnp.float32) - (support // 2 - 1) - offset_value
    inside = distance < support
    return jnp.where(inside, jnp.exp(-5.6 * shifted * shifted / support), 0.0)


def per_device(
    source_hat, particle_start, particle_offset, ghost_start, ghost_offset, ghost_slot, counts
):
    grid_size = source_hat.shape[4]
    kx_local = source_hat.shape[2]
    ky_local = source_hat.shape[3]
    pieces_gx = lax.axis_size("gx")
    pieces_gy = lax.axis_size("gy")
    z_local = grid_size // pieces_gx
    x_local = grid_size // pieces_gy
    scale_k = TWO_PI / grid_size
    mode_x = signed_modes(
        lax.axis_index("gx") * kx_local + jnp.arange(kx_local, dtype=jnp.int32), grid_size
    )[:, None, None]
    mode_y = signed_modes(
        lax.axis_index("gy") * ky_local + jnp.arange(ky_local, dtype=jnp.int32), grid_size
    )[None, :, None]
    mode_z = signed_modes(jnp.arange(grid_size, dtype=jnp.int32), grid_size)[None, None, :]
    square = jnp.maximum(mode_x * mode_x + mode_y * mode_y + mode_z * mode_z, 1.0)
    inner_product = (
        source_hat[:, 0] * mode_x + source_hat[:, 1] * mode_y + source_hat[:, 2] * mode_z
    )
    velocity = [
        source_hat[:, 0] - mode_x * inner_product / square,
        source_hat[:, 1] - mode_y * inner_product / square,
        source_hat[:, 2] - mode_z * inner_product / square,
    ]
    kx_wave = scale_k * mode_x
    ky_wave = scale_k * mode_y
    kz_wave = scale_k * mode_z
    spectrum = jnp.stack(
        [
            velocity[0],
            velocity[1],
            velocity[2],
            times_ik(velocity[0], kx_wave, 0),
            times_ik(velocity[1], ky_wave, 0),
            0.5 * (times_ik(velocity[0], ky_wave, 0) + times_ik(velocity[1], kx_wave, 0)),
            0.5 * (times_ik(velocity[0], kz_wave, 0) + times_ik(velocity[2], kx_wave, 0)),
            0.5 * (times_ik(velocity[1], kz_wave, 0) + times_ik(velocity[2], ky_wave, 0)),
        ],
        axis=1,
    )
    field_count = spectrum.shape[1]
    table_z = phase_table(grid_size, pieces_gx, z_local)
    along_z = jnp.einsum("rfxyk,krgzq->xgzqfy", spectrum, table_z, precision=HIGHEST)
    along_z = along_z.reshape(kx_local, pieces_gx, z_local * 2 * field_count * ky_local)
    rows_x = lax.all_to_all(along_z, "gx", split_axis=1, concat_axis=0, tiled=True)
    rows_x = rows_x.reshape(grid_size, z_local, 2, field_count, ky_local)
    count_x = rows_x.shape[3]
    table_x = phase_table(grid_size, pieces_gy, x_local)
    along_x = jnp.einsum("kzrfy,krgxq->gyxqfz", rows_x, table_x, precision=HIGHEST)
    along_x = along_x.reshape(pieces_gy, ky_local, x_local * 2 * count_x * z_local)
    columns = lax.all_to_all(along_x, "gy", split_axis=0, concat_axis=1, tiled=True)
    columns = columns.reshape(grid_size, x_local, 2, count_x, z_local)
    table_y = phase_table(grid_size, 1, grid_size)[:, :, 0, :, 0]
    real_fields = jnp.einsum("kxrfz,kry->xzfy", columns, table_y, precision=HIGHEST)
    field_rows = real_fields.reshape(x_local * z_local, 8 * grid_size).astype(jnp.bfloat16)
    own_rows = particle_start.shape[1]
    ghost_rows = ghost_start.shape[2]
    starts = jnp.concatenate([particle_start, ghost_start.reshape(3, 3 * ghost_rows)], axis=1)
    offsets = jnp.concatenate([particle_offset, ghost_offset.reshape(3, 3 * ghost_rows)], axis=1)
    live_rows = jnp.concatenate(
        [jnp.arange(own_rows, dtype=jnp.int32) < counts[0, 0]]
        + [
            jnp.arange(ghost_rows, dtype=jnp.int32) < counts[0, 1 + group_index]
            for group_index in range(3)
        ]
    ).astype(jnp.float32)
    total_rows = own_rows + 3 * ghost_rows
    row_block = math.gcd(total_rows, 512)
    block_count = total_rows // row_block
    cell_index = jnp.arange(x_local * z_local, dtype=jnp.int32)
    x_cells = lax.axis_index("gy") * x_local + cell_index // z_local
    z_cells = lax.axis_index("gx") * z_local + cell_index % z_local
    y_cells = jnp.arange(grid_size, dtype=jnp.int32)

    def interpolate(block_data):
        start_block, offset_block, live_block = block_data
        weight_x = spread_weight(
            (x_cells[None, :] - start_block[0][:, None]) % grid_size,
            offset_block[0][:, None],
            SUPPORT,
        )
        weight_z = spread_weight(
            (z_cells[None, :] - start_block[2][:, None]) % grid_size,
            offset_block[2][:, None],
            SUPPORT,
        )
        weight_plane = (weight_x * weight_z * live_block[:, None]).astype(jnp.bfloat16)
        summed = jnp.dot(weight_plane, field_rows, preferred_element_type=jnp.float32).reshape(
            row_block, 8, grid_size
        )
        weight_y = spread_weight(
            (y_cells[None, :] - start_block[1][:, None]) % grid_size,
            offset_block[1][:, None],
            SUPPORT,
        )
        return jnp.einsum("bfy,by->bf", summed, weight_y, precision=HIGHEST)

    values = lax.map(
        interpolate,
        (
            jnp.moveaxis(starts.reshape(3, block_count, row_block), 1, 0),
            jnp.moveaxis(offsets.reshape(3, block_count, row_block), 1, 0),
            live_rows.reshape(block_count, row_block),
        ),
    )
    values = values.reshape(total_rows, 8)
    own_values = values[:own_rows].T
    ghost_values = values[own_rows:].reshape(3, ghost_rows, 8)
    buffers = [
        jnp.zeros((8, own_rows), jnp.float32)
        .at[:, ghost_slot[group_index]]
        .add(ghost_values[group_index].T)
        for group_index in range(3)
    ]
    from_x, passing = passed_along((buffers[0], buffers[2]), "gy", -1)
    from_z, from_corner = passed_along((buffers[1], passing), "gx", -1)
    totals = own_values + from_x + from_z + from_corner
    return (totals[:3], totals[3:])


def solution(mesh):
    in_specs = (
        P(None, None, "gx", "gy", None),
        P(None, ("gx", "gy")),
        P(None, ("gx", "gy")),
        P(None, None, ("gx", "gy")),
        P(None, None, ("gx", "gy")),
        P(None, ("gx", "gy")),
        P(("gx", "gy"), None),
    )
    out_specs = (P(None, ("gx", "gy")), P(None, ("gx", "gy")))
    return jax.shard_map(
        per_device, mesh=mesh, in_specs=in_specs, out_specs=out_specs, check_vma=False
    )
```

profile of v0, /device:TPU:1, one launch (start us, length us, event | category | flops | bytes accessed | tf_op | source)
XLA Modules:
  0.0 637.2 jit_solution(5322468933388358023)
XLA Ops:
  1.0 2.6 bitcast_subtract_fusion
  8.5 56.9 %convolution_bitcast_fusion = f32[16,16,16,2,8,32]{5,2,0,4,3,1:T(8,128)} fusion(f32[2,8,16,32,256]{4,3,0,2,1:T(8,128)S(1)} %fusion.85, f32[256,2,16,16,2,1,1]{0,3,1,6,5,4,2:T(8,128)S(1)} %maximum_bitcast_fusion.18), kind=kOutput, calls=%fused_computation.91 | convolution fusion | flops 12884901888 | bytes 17825792 | tf_op jit(solution)/shard_map/rfxyk,krgzq->xgzqfy/dot_general | solution.py:96
  65.3 31.8 %copy.100 = f32[16,16,16,2,8,32]{5,4,3,2,0,1:T(8,128)} copy(f32[16,16,16,2,8,32]{5,2,0,4,3,1:T(8,128)} %convolution_bitcast_fusion) | data formatting | bytes 16777216 | tf_op jit(solution)/shard_map/reshape | solution.py:97
  97.1 24.5 %reshape.779 = f32[16,16,8192]{2,0,1:T(8,128)} reshape(f32[16,16,16,2,8,32]{5,4,3,2,0,1:T(8,128)} %copy.100) | data formatting | bytes 16777216 | tf_op jit(solution)/shard_map/reshape | solution.py:97
  121.6 7.8 %all-to-all-start = ((f32[16,16,8192]{2,0,1:T(8,128)}), f32[16,16,8192]{2,0,1:T(8,128)}, u32[]{:S(2)}, u32[]{:S(2)}) async-start(f32[16,16,8192]{2,0,1:T(8,128)} %reshape.779), calls=%async_computation | async-start | bytes 16777216 | tf_op jit(solution)/shard_map/all_to_all | solution.py:98
  131.8 92.1 %all-to-all-done = f32[16,16,8192]{2,0,1:T(8,128)} async-done(((f32[16,16,8192]{2,0,1:T(8,128)}), f32[16,16,8192]{2,0,1:T(8,128)}, u32[]{:S(2)}, u32[]{:S(2)}) %all-to-all-start) | async-done | bytes 8388640 | tf_op jit(solution)/shard_map/all_to_all | solution.py:98
  223.9 20.1 %reshape.676 = f32[256,16,2,8,32]{4,3,2,1,0:T(8,128)} reshape(f32[16,16,1,8192]{3,1,0,2:T(8,128)} %bitcast.58) | data formatting | bytes 16777216 | tf_op jit(solution)/shard_map/reshape | solution.py:99
  244.0 80.5 %fusion.63 = f32[8,32,32,2,8,16]{1,2,4,5,3,0:T(8,128)S(1)} fusion(f32[256,16,2,8,32,1,1]{4,3,2,1,0,6,5:T(8,128)} %bitcast.290, f32[256,2,8,32,2,1,1]{0,3,1,6,5,4,2:T(8,128)} %maximum_bitcast_fusion.19), kind=kOutput, calls=%fused_computation.92 | convolution fusion | flops 12884901888 | bytes 17825792 | tf_op jit(solution)/shard_map/kzrfy,krgxq->gyxqfz/dot_general | solution.py:102
  324.5 21.5 %copy.79 = f32[8,32,32,2,8,16]{1,5,4,3,2,0:T(8,128)} copy(f32[8,32,32,2,8,16]{1,2,4,5,3,0:T(8,128)S(1)} %fusion.63) | data formatting | bytes 16777216 | tf_op jit(solution)/shard_map/kzrfy,krgxq->gyxqfz/transpose | solution.py:102
  346.0 21.7 %copy.80 = f32[8,32,8192]{2,1,0:T(8,128)} copy(f32[8,32,8192]{1,2,0:T(8,128)} %bitcast.288) | data formatting | bytes 16777216 | tf_op jit(solution)/shard_map/reshape | solution.py:103
  367.8 6.7 %all-to-all-start.1 = ((f32[8,32,8192]{2,1,0:T(8,128)}), f32[8,32,8192]{2,1,0:T(8,128)}, u32[]{:S(2)}, u32[]{:S(2)}) async-start(f32[8,32,8192]{2,1,0:T(8,128)} %copy.80), calls=%async_computation.1 | async-start | bytes 16777216 | tf_op jit(solution)/shard_map/all_to_all | solution.py:104
  380.1 109.3 %all-to-all-done.1 = f32[8,32,8192]{2,1,0:T(8,128)} async-done(((f32[8,32,8192]{2,1,0:T(8,128)}), f32[8,32,8192]{2,1,0:T(8,128)}, u32[]{:S(2)}, u32[]{:S(2)}) %all-to-all-start.1) | async-done | bytes 8388640 | tf_op jit(solution)/shard_map/all_to_all | solution.py:104
  489.5 19.8 %copy.81 = f32[8,32,8192]{1,0,2:T(8,128)} copy(f32[8,32,8192]{2,1,0:T(8,128)} %all-to-all-done.1) | data formatting | bytes 16777216 | tf_op jit(solution)/shard_map/all_to_all | solution.py:104
  509.3 23.2 %reshape.678 = f32[256,32,2,8,16]{0,4,3,2,1:T(8,128)} reshape(f32[8,32,8192]{1,0,2:T(8,128)} %copy.81) | data formatting | bytes 16777216 | tf_op jit(solution)/shard_map/reshape | solution.py:105
  532.5 13.7 %fusion.71 = bf16[32,16,8,256]{3,0,1,2:T(8,128)(2,1)S(1)} fusion(f32[256,32,2,8,16]{0,4,3,2,1:T(8,128)} %reshape.678, f32[256,1,1,256,2]{3,0,1,4,2:T(8,128)S(1)} %get-tuple-element.246, f32[256,1,1,256,2]{3,0,1,4,2:T(8,128)S(1)} %get-tuple-element.245), kind=kOutput, calls=%fused_computation.97 | convolution fusion | flops 6443630592 | bytes 11534336 | tf_op jit(solution)/shard_map/kxrfz,kry->xzfy/dot_general | solution.py:107
  548.1 68.2 %while.16 = (s32[]{:T(128)}, f32[7,512,8]{1,2,0:T(8,128)S(1)}, s32[7,3,512]{2,1,0:T(4,128)S(1)}, f32[7,3,512]{2,1,0:T(4,128)S(1)}, f32[7,512]{1,0:T(8,128)S(1)},...) while((s32[]{:T(128)}, f32[7,512,8]{1,2,0:T(8,128)S(1)}, ...), condition=%wide.region_1.4_spmd.clone, body=%wide.region_0.3_spmd.clone.sunk | while | flops 1100225536 | bytes 20056244 | solution.py:151
  548.4 2.7 fusion.151
  553.5 4.4 fusion.153
  558.1 2.7 fusion.151
  563.2 4.4 fusion.153
  567.8 2.7 fusion.151
  572.9 4.4 fusion.153
  577.5 2.7 fusion.151
  582.6 4.4 fusion.153
  587.2 2.7 fusion.151
  592.4 4.4 fusion.153
  596.9 2.7 fusion.151
  602.1 4.4 fusion.153
  606.6 2.7 fusion.151
  611.8 4.4 fusion.153
  619.2 3.3 collective-permute-start.2
  629.2 2.7 collective-permute-start.1
  (139 shorter events, 47.1 us)
Async XLA Ops:
  0.6 2.9 copy-start
  121.6 102.3 %all-to-all-start = ((f32[16,16,8192]{2,0,1:T(8,128)}), f32[16,16,8192]{2,0,1:T(8,128)}, u32[]{:S(2)}, u32[]{:S(2)}) async-start(f32[16,16,8192]{2,0,1:T(8,128)} %reshape.779), calls=%async_computation | async-start | bytes 16777216 | tf_op jit(solution)/shard_map/all_to_all | solution.py:98
  367.7 6.8 %copy-start.5 = (s32[1,4]{1,0:T(1,128)S(1)}, s32[1,4]{1,0:T(1,128)}, u32[]{:S(2)}) copy-start(s32[1,4]{1,0:T(1,128)} %param.19) | copy-start | bytes 52
  367.7 10.1 %copy-start.3 = (s32[3,3,512]{2,1,0:T(4,128)S(1)}, s32[3,3,512]{2,1,0:T(4,128)}, u32[]{:S(2)}) copy-start(s32[3,3,512]{2,1,0:T(4,128)} %param.16) | copy-start | bytes 55300
  367.7 10.2 %copy-start.4 = (f32[3,3,512]{2,1,0:T(4,128)S(1)}, f32[3,3,512]{2,1,0:T(4,128)}, u32[]{:S(2)}) copy-start(f32[3,3,512]{2,1,0:T(4,128)} %param.17) | copy-start | bytes 55300
  367.7 12.3 %copy-start.6 = (s32[3,512]{1,0:T(4,128)S(1)}, s32[3,512]{1,0:T(4,128)}, u32[]{:S(2)}) copy-start(s32[3,512]{1,0:T(4,128)} %param.18) | copy-start | bytes 18436
  367.8 12.3 %copy-start.1 = (s32[3,2048]{1,0:T(4,128)S(1)}, s32[3,2048]{1,0:T(4,128)}, u32[]{:S(2)}) copy-start(s32[3,2048]{1,0:T(4,128)} %param.14) | copy-start | bytes 73732
  367.8 12.3 %copy-start.2 = (f32[3,2048]{1,0:T(4,128)S(1)}, f32[3,2048]{1,0:T(4,128)}, u32[]{:S(2)}) copy-start(f32[3,2048]{1,0:T(4,128)} %param.15) | copy-start | bytes 73732
  367.8 121.7 %all-to-all-start.1 = ((f32[8,32,8192]{2,1,0:T(8,128)}), f32[8,32,8192]{2,1,0:T(8,128)}, u32[]{:S(2)}, u32[]{:S(2)}) async-start(f32[8,32,8192]{2,1,0:T(8,128)} %copy.80), calls=%async_computation.1 | async-start | bytes 16777216 | tf_op jit(solution)/shard_map/all_to_all | solution.py:104
  619.2 12.7 %collective-permute-start.2 = (f32[8,2048]{1,0:T(8,128)S(1)}, f32[8,2048]{1,0:T(8,128)S(1)}, u32[]{:S(2)}, u32[]{:S(2)}) collective-permute-start(f32[8,2048]{1,0:T(8,128)S(1)} %copy.89), channel_id=1, source_target_pairs={{1,0},{2,1},{3,2},{4,3},{5,4},{6,5},{7,6},{0,7},{9,8},{10,9},{11,1... | collective-permute-start | bytes 196616 | tf_op jit(solution)/shard_map/ppermute | solution.py:18
  625.5 6.5 %collective-permute-start = (f32[8,2048]{1,0:T(8,128)S(1)}, f32[8,2048]{1,0:T(8,128)S(1)}, u32[]{:S(2)}, u32[]{:S(2)}) collective-permute-start(f32[8,2048]{1,0:T(8,128)S(1)} %copy.85), channel_id=1, source_target_pairs={{1,0},{2,1},{3,2},{4,3},{5,4},{6,5},{7,6},{0,7},{9,8},{10,9},{11,1... | collective-permute-start | bytes 196616 | tf_op jit(solution)/shard_map/ppermute | solution.py:18
  629.2 4.9 collective-permute-start.1
  631.9 3.7 collective-permute-start.3
where the time goes:
time: 643 us; the launch traced here: 637 us
  waiting for transfers between devices  205 us (32%)
  matrix products  201 us (31%)
  local copies, waits for them, and re-layouts  183 us (28%)
  other arithmetic  25.1 us (4%)
  starting transfers between devices  21.4 us (3%)
    all_to_all x1, waiting for transfers between devices, per_device(): lax.all_to_all(along_x, 'gy', split_axis=0, concat_axis=1, tiled=True)  109 us
    all_to_all x1, waiting for transfers between devices, per_device(): lax.all_to_all(along_z, 'gx', split_axis=1, concat_axis=0, tiled=True)  92.1 us
    dot_general x1, matrix products, per_device(): jnp.einsum('kzrfy,krgxq->gyxqfz', rows_x, table_x, precision=HIGHEST)  80.5 us
    dot_general x1, matrix products, per_device(): jnp.einsum('rfxyk,krgzq->xgzqfy', spectrum, table_z, precision=HIGHEST)  56.9 us
    reshape x2, local copies, waits for them, and re-layouts, per_device(): along_z.reshape(kx_local, pieces_gx, z_local * 2 * field_count * ky_local)  56.3 us
    dot_general x7, matrix products, interpolate(): return jnp.einsum('bfy,by->bf', summed, weight_y, precision=HIGHEST)  30.8 us
    reshape x1, local copies, waits for them, and re-layouts, per_device(): columns = columns.reshape(grid_size, x_local, 2, count_x, z_local)  23.2 us
    reshape x1, local copies, waits for them, and re-layouts, per_device(): along_x.reshape(pieces_gy, ky_local, x_local * 2 * count_x * z_local)  21.7 us
  transfers between devices with their start and end apart: 6, of which 4 were waited for; matrix products, arithmetic and copies ran while one was open for 2% of the time, Pallas kernels for 0%

commit v1 on v0

v1 whole, which is shorter than its diff:
```python
import math

import jax
import jax.numpy as jnp
import numpy as np
from jax import lax
from jax.experimental import pallas as pl
from jax.experimental.pallas import tpu as pltpu
from jax.sharding import PartitionSpec as P

F32 = jnp.float32
BF16 = jnp.bfloat16
SUPPORT = 8
GRID = 256
N_GX = 16
N_GY = 8
OWN = 2048
GHOST = 512
ROWS = OWN + GHOST
WAVE = 2.0 * math.pi / GRID
WINDOW = 48
BLOCK = 256


def numpy_halves(table):
    import ml_dtypes

    high = table.astype(ml_dtypes.bfloat16)
    low = (table - high.astype(np.float64)).astype(ml_dtypes.bfloat16)
    return high, low


def z_table():
    c, slab, part, step = np.meshgrid(
        np.arange(4), np.arange(N_GX), np.arange(2), np.arange(4), indexing="ij"
    )
    z = (16 * slab + 4 * step + c).reshape(-1, 1)
    part = part.reshape(-1, 1)
    angle = (z * np.arange(GRID)[None, :] % GRID) * (2.0 * np.pi / GRID)
    cosine, sine = np.cos(angle), np.sin(angle)
    from_real = np.where(part == 0, cosine, sine)
    from_imag = np.where(part == 0, -sine, cosine)
    return np.concatenate([from_real, from_imag], axis=1)


def x_table():
    index = np.arange(GRID)
    angle = (index[:, None] * index[None, :] % GRID) * (2.0 * np.pi / GRID)
    cosine, sine = np.cos(angle), np.sin(angle)
    return np.block([[cosine, -sine], [sine, cosine]])


def y_table():
    index = np.arange(GRID)
    angle = (index[:, None] * index[None, :] % GRID) * (2.0 * np.pi / GRID)
    cosine = np.cos(angle).reshape(N_GY, 1, GRID // N_GY, GRID)
    sine = -np.sin(angle).reshape(N_GY, 1, GRID // N_GY, GRID)
    return np.concatenate([cosine, sine], axis=1).reshape(N_GY, 2 * (GRID // N_GY), GRID)


def split(value):
    high = value.astype(BF16)
    return high, (value - high.astype(F32)).astype(BF16)


def signed(index):
    return jnp.where(index < GRID // 2, index, index - GRID).astype(F32)


NT = (((1,), (1,)), ((), ()))
NN = (((1,), (0,)), ((), ()))


def dot3(a_high, a_low, b_high, b_low, dims):
    def one(a, b):
        return lax.dot_general(a, b, dims, preferred_element_type=F32)

    return one(a_high, b_high) + (one(a_high, b_low) + one(a_low, b_high))


def z_kernel(place, source, t_high, t_low, out, x_high, x_low):
    quad = pl.program_id(0)
    row = lax.broadcasted_iota(jnp.int32, (32, GRID), 0)
    mode_y = signed(row + place[1] * 32)
    mode_z = signed(lax.broadcasted_iota(jnp.int32, (32, GRID), 1))
    wave_z = WAVE * mode_z
    partial_square = mode_y * mode_y + mode_z * mode_z
    for k in range(4):
        index_x = place[0] * 16 + quad * 4 + k
        mode_x = jnp.where(index_x < GRID // 2, index_x, index_x - GRID).astype(F32)
        square = jnp.maximum(mode_x * mode_x + partial_square, 1.0)
        inverse = 1.0 / square
        v = []
        for r in range(2):
            s1, s2, s3 = source[r, 0, k], source[r, 1, k], source[r, 2, k]
            ratio = (s1 * mode_x + s2 * mode_y + s3 * mode_z) * inverse
            v.append((s1 - mode_x * ratio, s2 - mode_y * ratio, s3 - mode_z * ratio))
        rows = [
            (v[0][0], v[1][0], k * 128),
            (v[0][1], v[1][1], k * 128 + 32),
            (v[0][2], v[1][2], k * 128 + 64),
            (-wave_z * v[1][0], wave_z * v[0][0], k * 128 + 96),
            (-wave_z * v[1][1], wave_z * v[0][1], 512 + k * 32),
        ]
        for real, imag, start in rows:
            for r, value in ((0, real), (1, imag)):
                high, low = split(value)
                x_high[start : start + 32, r * GRID : (r + 1) * GRID] = high
                x_low[start : start + 32, r * GRID : (r + 1) * GRID] = low

    def transformed(start, size):
        return dot3(
            t_high[...], t_low[...], x_high[start : start + size], x_low[start : start + size], NT
        )

    for pair in range(2):
        result = transformed(pair * 256, 256)
        for side in range(2):
            lanes = slice(side * 128, side * 128 + 128)
            for c in range(4):
                out[:, pair * 2 + side, c * 8 : c * 8 + 8, :] = result[
                    c * 128 : c * 128 + 128, lanes
                ].reshape(N_GX, 8, 128)
    last = transformed(512, 128)
    lane = lax.broadcasted_iota(jnp.int32, (128, 128), 1)
    lower64 = lane < 64
    lower32 = (lane & 32) == 0
    v = [last[c * 128 : c * 128 + 128] for c in range(4)]
    p0 = [jnp.where(lower64, v[c], pltpu.roll(v[c + 2], 64, 1)) for c in range(2)]
    p1 = [jnp.where(lower64, pltpu.roll(v[c], 64, 1), v[c + 2]) for c in range(2)]
    for k1, p in ((0, p0), (1, p1)):
        q0 = jnp.where(lower32, p[0], pltpu.roll(p[1], 32, 1))
        q1 = jnp.where(lower32, pltpu.roll(p[0], 96, 1), p[1])
        out[:, 2 * k1, 32:40, :] = q0.reshape(N_GX, 8, 128)
        out[:, 2 * k1 + 1, 32:40, :] = q1.reshape(N_GX, 8, 128)


def z_stage(place, source, t_high, t_low):
    return pl.pallas_call(
        z_kernel,
        out_shape=jax.ShapeDtypeStruct((N_GX, 16, 40, 128), F32),
        grid_spec=pltpu.PrefetchScalarGridSpec(
            num_scalar_prefetch=1,
            grid=(4,),
            in_specs=[
                pl.BlockSpec((2, 3, 4, 32, GRID), lambda i, _: (0, 0, i, 0, 0)),
                pl.BlockSpec((512, 512), lambda i, _: (0, 0)),
                pl.BlockSpec((512, 512), lambda i, _: (0, 0)),
            ],
            out_specs=pl.BlockSpec((N_GX, 4, 40, 128), lambda i, _: (0, i, 0, 0)),
            scratch_shapes=[pltpu.VMEM((640, 512), BF16), pltpu.VMEM((640, 512), BF16)],
        ),
        name="z_stage",
    )(place, source, t_high, t_low)


def weight(distance, offset):
    shifted = distance - (SUPPORT // 2 - 1) - offset
    inside = (distance >= 0.0) & (distance < SUPPORT)
    return jnp.where(inside, jnp.exp(-5.6 / SUPPORT * shifted * shifted), 0.0)


def wrapped(distance):
    return jnp.where(distance < 0.0, distance + GRID, distance)


def field_kernel(
    place, received, t_high, t_low, y_high, y_low, particles, out, field, d_high, d_low, window
):
    lane = lax.broadcasted_iota(jnp.int32, (GRID, 128), 1)
    group = lane // 32
    wave_x = WAVE * signed(lax.broadcasted_iota(jnp.int32, (GRID, 128), 0))
    wave_y = WAVE * signed(lane % 32 + place[1] * 32)
    last_group = group == 3
    on_left = jnp.where(group == 0, wave_y, 0.0)
    on_right = jnp.where((group == 1) | last_group, 0.5 * wave_y, 0.0)
    on_same = jnp.where((group == 1) | (group == 2), 0.5 * wave_x, 0.0)
    for c in range(4):

        def one_z(step, carry):
            def load(start):
                return received[pl.ds(start, GRID, stride=40), :]

            parts = []
            for q in range(2):
                value = load(c * 8 + q * 4 + step)
                extra = load(32 + q * 4 + step)
                if c != 3:
                    extra = pltpu.roll(extra, 32 * (3 - c), 1)
                parts.append((value, pltpu.roll(value, 96, 1), pltpu.roll(value, 32, 1), extra))
            (a_re, l_re, r_re, e_re), (a_im, l_im, r_im, e_im) = parts
            first_re = jnp.where(last_group, -wave_x * l_im, a_re)
            first_im = jnp.where(last_group, wave_x * l_re, a_im)
            plain_re = jnp.where(group == 2, 0.5 * l_re, jnp.where(last_group, 0.5 * e_re, 0.0))
            plain_im = jnp.where(group == 2, 0.5 * l_im, jnp.where(last_group, 0.5 * e_im, 0.0))
            second_re = plain_re - (on_left * l_im + on_right * r_im + on_same * a_im)
            second_im = plain_im + (on_left * l_re + on_right * r_re + on_same * a_re)
            for top, left, value in (
                (0, 0, first_re),
                (GRID, 0, first_im),
                (0, 128, second_re),
                (GRID, 128, second_im),
            ):
                high, low = split(value)
                d_high[top : top + GRID, left : left + 128] = high
                d_low[top : top + GRID, left : left + 128] = low
            result = dot3(t_high[...], t_low[...], d_high[...], d_low[...], NN).astype(BF16)
            z = step * 4 + c
            for q in range(2):
                field[z, 0:GRID, q * 256 : q * 256 + 256] = result[q * GRID : q * GRID + GRID]
                field[z, GRID : GRID + 16, q * 256 : q * 256 + 256] = result[
                    q * GRID : q * GRID + 16
                ]
            return carry

        lax.fori_loop(0, 4, one_z, 0)

    out[...] = jnp.zeros_like(out)
    base_z = (place[0] * 16).astype(F32)
    x_cell = lax.broadcasted_iota(jnp.int32, (WINDOW, BLOCK), 0).astype(F32)
    y_cell = lax.broadcasted_iota(jnp.int32, (GRID, BLOCK), 0).astype(F32)
    z_cell = lax.broadcasted_iota(jnp.int32, (16, BLOCK), 0).astype(F32) + base_z

    def one_owner(owner, carry):
        block = field[:, pl.ds(pl.multiple_of(owner * 32, 16), WINDOW), :]
        window[...] = block.reshape(16 * WINDOW, 512).T
        base_x = (owner * 32).astype(F32)

        def one_block(start):
            start = pl.multiple_of(start, BLOCK)
            data = particles[owner, :, pl.ds(start, BLOCK)]
            weight_x = weight(x_cell + base_x - data[0:1], data[3:4])
            weight_z = weight(wrapped(z_cell - data[2:3]), data[5:6])
            live = data[6:7]
            plane = jnp.concatenate(
                [(weight_x * weight_z[z : z + 1] * live).astype(BF16) for z in range(16)], axis=0
            )
            summed = lax.dot_general(window[...], plane, NN, preferred_element_type=F32)
            weight_y = weight(wrapped(y_cell - data[1:2]), data[4:5])
            w_high, w_low = split(weight_y)
            phases = dot3(y_high[...], y_low[...], w_high, w_low, NN)
            summed = summed.reshape(2, 8, 32, BLOCK)
            product = summed[0] * phases[None, 0:32] + summed[1] * phases[None, 32:64]
            out[owner, :, pl.ds(start, BLOCK)] = jnp.sum(product, axis=1)

        def own_block(index, carry):
            one_block(index * BLOCK)
            return carry

        def ghost_block(index, carry):
            one_block(OWN + index * BLOCK)
            return carry

        lax.fori_loop(0, (place[2 + owner] + BLOCK - 1) // BLOCK, own_block, 0)
        lax.fori_loop(0, (place[10 + owner] + BLOCK - 1) // BLOCK, ghost_block, 0)
        return carry

    lax.fori_loop(0, N_GY, one_owner, 0)


def field_stage(place, received, t_high, t_low, y_high, y_low, particles):
    def whole(shape):
        return pl.BlockSpec(
            shape, lambda i, _: (0,) * len(shape), pipeline_mode=pl.Buffered(1)
        )

    return pl.pallas_call(
        field_kernel,
        out_shape=jax.ShapeDtypeStruct((N_GY, 8, ROWS), F32),
        grid_spec=pltpu.PrefetchScalarGridSpec(
            num_scalar_prefetch=1,
            grid=(1,),
            in_specs=[
                whole((GRID * 40, 128)),
                whole((512, 512)),
                whole((512, 512)),
                whole((64, GRID)),
                whole((64, GRID)),
                whole((N_GY, 8, ROWS)),
            ],
            out_specs=whole((N_GY, 8, ROWS)),
            scratch_shapes=[
                pltpu.VMEM((16, GRID + 16, 512), BF16),
                pltpu.VMEM((512, 256), BF16),
                pltpu.VMEM((512, 256), BF16),
                pltpu.VMEM((512, 16 * WINDOW), BF16),
            ],
        ),
        name="field_stage",
    )(place, received, t_high, t_low, y_high, y_low, particles)


def ghost_kernel(values, slots, own, back):
    total = values[0]
    for source in range(1, N_GY):
        total = total + values[source]
    own[...] = total[:, :OWN]
    ghosts = total[:, OWN:]
    cell = lax.broadcasted_iota(jnp.int32, (OWN, GHOST), 0)
    chosen = (cell == slots[...]).astype(F32).astype(BF16)
    first, rest = split(ghosts)
    second, third = split(ghosts - first.astype(F32))
    parts = jnp.concatenate([first.astype(F32), second.astype(F32), third.astype(F32)], axis=0)
    placed = lax.dot_general(parts.astype(BF16), chosen, NT, preferred_element_type=F32)
    back[...] = placed[0:8] + (placed[8:16] + placed[16:24])


def ghost_stage(values, slots):
    return pl.pallas_call(
        ghost_kernel,
        out_shape=(
            jax.ShapeDtypeStruct((8, OWN), F32),
            jax.ShapeDtypeStruct((8, OWN), F32),
        ),
        name="ghost_stage",
    )(values, slots)


def per_device(
    source_hat, particle_start, particle_offset, ghost_start, ghost_offset, ghost_slot, counts
):
    index_gx = lax.axis_index("gx").astype(jnp.int32)
    index_gy = lax.axis_index("gy").astype(jnp.int32)
    index = jnp.arange(OWN, dtype=jnp.int32)
    own_live = (index < counts[0, 0]).astype(F32)
    ghost_live = (index[:GHOST] < counts[0, 2]).astype(F32)
    column = jnp.arange(ROWS, dtype=jnp.int32)
    count_row = jnp.where(
        column == 0, counts[0, 0], jnp.where(column == 1, counts[0, 2], 0)
    ).astype(F32)
    mine = jnp.concatenate(
        [
            jnp.concatenate([particle_start.astype(F32), ghost_start[:, 1].astype(F32)], axis=1),
            jnp.concatenate([particle_offset, ghost_offset[:, 1]], axis=1),
            jnp.concatenate([own_live, ghost_live])[None],
            count_row[None],
        ],
        axis=0,
    )
    copies = jnp.broadcast_to(mine[None], (N_GY, 8, ROWS))
    particles = lax.all_to_all(copies, "gy", split_axis=0, concat_axis=0, tiled=True)
    live_counts = particles[:, 7, 0:2].astype(jnp.int32)
    here = jnp.stack([index_gx, index_gy])
    place = jnp.concatenate([here, live_counts[:, 0], live_counts[:, 1]])

    z_high, z_low = numpy_halves(z_table())
    x_high, x_low = numpy_halves(x_table())
    y_high, y_low = numpy_halves(y_table())
    sent = z_stage(here, source_hat, jnp.asarray(z_high), jnp.asarray(z_low))
    received = lax.all_to_all(sent, "gx", split_axis=0, concat_axis=0, tiled=True)
    received = received.reshape(GRID * 40, 128)
    y_high = lax.dynamic_index_in_dim(jnp.asarray(y_high), index_gy, 0, keepdims=False)
    y_low = lax.dynamic_index_in_dim(jnp.asarray(y_low), index_gy, 0, keepdims=False)
    partial = field_stage(
        place, received, jnp.asarray(x_high), jnp.asarray(x_low), y_high, y_low, particles
    )
    partial = lax.all_to_all(partial, "gy", split_axis=0, concat_axis=0, tiled=True)
    own, back = ghost_stage(partial, ghost_slot[1:2])
    devices = range(lax.axis_size("gx"))
    route = [((i + 1) % len(devices), i) for i in devices]
    totals = own + lax.ppermute(back, "gx", route)
    return (totals[:3], totals[3:])


def solution(mesh):
    in_specs = (
        P(None, None, "gx", "gy", None),
        P(None, ("gx", "gy")),
        P(None, ("gx", "gy")),
        P(None, None, ("gx", "gy")),
        P(None, None, ("gx", "gy")),
        P(None, ("gx", "gy")),
        P(("gx", "gy"), None),
    )
    out_specs = (P(None, ("gx", "gy")), P(None, ("gx", "gy")))
    return jax.shard_map(
        per_device, mesh=mesh, in_specs=in_specs, out_specs=out_specs, check_vma=False
    )
```

time: 643 us -> 160 us (0.25)
  matrix products: 201 us -> 0 us
  local copies, waits for them, and re-layouts: 183 us -> 7.84 us
  waiting for transfers between devices: 205 us -> 70.3 us
  Pallas kernels: 0 us -> 47.7 us
  other arithmetic: 25.1 us -> 7.03 us
    dot_general x17 -> x0, matrix products: 201 us -> none  [the longest x1 80.5 us: per_device(): jnp.einsum('kzrfy,krgxq->gyxqfz', rows_x, table_x, precision=HIGHEST)]
    all_to_all x2 -> x3, waiting for transfers between devices: 201 us -> 68.2 us  [the longest x1 58.6 us: per_device(): lax.all_to_all(sent, 'gx', split_axis=0, concat_axis=0, tiled=True)]
    reshape x5 -> x0, local copies, waits for them, and re-layouts: 121 us -> none  [the longest x2 56.3 us: per_device(): along_z.reshape(kx_local, pieces_gx, z_local * 2 * field_count * ky_local)]
    pallas_call x0 -> x3, Pallas kernels: none -> 47.7 us  [the longest x1 35.6 us: field_stage(): pl.pallas_call(field_kernel, out_shape=jax.ShapeDtypeStruct((N_GY, 8, ROW...]
    transpose x1 -> x0, local copies, waits for them, and re-layouts: 21.5 us -> none  [per_device(): jnp.einsum('kzrfy,krgxq->gyxqfz', rows_x, table_x, precision=HIGHEST)]
    all_to_all x1 -> x0, local copies, waits for them, and re-layouts: 19.8 us -> none  [per_device(): lax.all_to_all(along_x, 'gy', split_axis=0, concat_axis=1, tiled=True)]
    while x7 -> x0, local copies, waits for them, and re-layouts: 13.7 us -> none
    scatter-add x3 -> x0, other arithmetic: 7.52 us -> none  [per_device(): buffers = [jnp.zeros((8, own_rows), jnp.float32).at[:, ghost_slot[group_i...]
  transfers between devices with their start and end apart: 6 -> 4, of which waited for: 4 -> 4; matrix products, arithmetic and copies ran while one was open for 2% -> 3% of each run, Pallas kernels for 0% -> 6%
where the time goes in v1:
time: 160 us; the launch traced here: 158 us
  waiting for transfers between devices  70.3 us (44%)
  Pallas kernels  47.7 us (30%)
  starting transfers between devices  24.8 us (16%)
  local copies, waits for them, and re-layouts  7.84 us (5%)
  other arithmetic  7.03 us (4%)
    all_to_all x1, waiting for transfers between devices, per_device(): lax.all_to_all(sent, 'gx', split_axis=0, concat_axis=0, tiled=True)  58.6 us
    pallas_call x1, Pallas kernels, field_stage(): pl.pallas_call(field_kernel, out_shape=jax.ShapeDtypeStruct((N_GY, 8, ROW...  35.6 us
    pallas_call x1, Pallas kernels, z_stage(): pl.pallas_call(z_kernel, out_shape=jax.ShapeDtypeStruct((N_GX, 16, 40, 12...  9.69 us
    all_to_all x1, waiting for transfers between devices, per_device(): lax.all_to_all(partial, 'gy', split_axis=0, concat_axis=0, tiled=True)  8.07 us
    all_to_all x1, starting transfers between devices, per_device(): lax.all_to_all(copies, 'gy', split_axis=0, concat_axis=0, tiled=True)  7.47 us
    all_to_all x1, starting transfers between devices, per_device(): lax.all_to_all(sent, 'gx', split_axis=0, concat_axis=0, tiled=True)  6.67 us
    all_to_all x1, starting transfers between devices, per_device(): lax.all_to_all(partial, 'gy', split_axis=0, concat_axis=0, tiled=True)  5.71 us
    ppermute x1, starting transfers between devices, per_device(): totals = own + lax.ppermute(back, 'gx', route)  4.92 us
  transfers between devices with their start and end apart: 4, of which 4 were waited for; matrix products, arithmetic and copies ran while one was open for 3% of the time, Pallas kernels for 6%

profile of v1, /device:TPU:1, one launch (start us, length us, event | category | flops | bytes accessed | tf_op | source)
XLA Modules:
  0.0 158.4 jit_solution(3262056045890249454)
XLA Ops:
  0.6 1.3 fusion.1
  1.9 0.6 add_compare_fusion
  2.6 1.3 fusion
  3.9 0.7 iota_compare_fusion
  4.6 0.7 slice.36
  5.3 0.7 slice_convert_fusion
  6.1 0.8 convert_element_type.27
  6.9 0.8 pad_maximum_fusion
  7.7 0.9 broadcast_in_dim.27
  8.6 7.5 %all-to-all-start = ((f32[8,8,2560]{2,1,0:T(8,128)}), f32[8,8,2560]{2,1,0:T(8,128)S(1)}, u32[]{:S(2)}, u32[]{:S(2)}) async-start(f32[8,8,2560]{2,1,0:T(8,128)} %broadcast_in_dim.27), calls=%async_computation | async-start | bytes 1310720 | tf_op jit(solution)/shard_map/all_to_all | solution.py:341
  16.0 0.6 pad_add_fusion.1.place
  16.6 9.7 %z_stage.1 = f32[16,16,40,128]{3,2,1,0:T(8,128)} custom-call(s32[2]{0:T(128)} %pad_add_fusion.1.place, f32[2,3,16,32,256]{4,3,2,1,0:T(8,128)} %source.1, bf16[512,512]{1,0:T(8,128)(2,1)} %constant.33.clone.t_high, bf16[512,512]{1,0:T(8,128)(2,1)} %constant.34.clone.t_low), custom_call_target="tpu_custom_call" | custom-call | tf_op jit(solution)/shard_map/z_stage/pallas_call | solution.py:139
  26.3 1.6 all-to-all-done.particles
  27.9 0.0 copy-start
  27.9 6.7 %all-to-all-start.1 = ((f32[16,16,40,128]{3,2,1,0:T(8,128)}), f32[16,16,40,128]{3,2,1,0:T(8,128)}, u32[]{:S(2)}, u32[]{:S(2)}) async-start(f32[16,16,40,128]{3,2,1,0:T(8,128)} %z_stage.1), calls=%async_computation.1 | async-start | bytes 10485760 | tf_op jit(solution)/shard_map/all_to_all | solution.py:350
  34.5 1.4 dynamic-slice_bitcast_fusion
  35.9 0.0 copy-done
  36.0 0.1 copy.17
  36.1 0.7 pad_add_fusion.place
  36.7 58.6 %all-to-all-done.1 = f32[16,16,40,128]{3,2,1,0:T(8,128)} async-done(((f32[16,16,40,128]{3,2,1,0:T(8,128)}), f32[16,16,40,128]{3,2,1,0:T(8,128)}, u32[]{:S(2)}, u32[]{:S(2)}) %all-to-all-start.1) | async-done | bytes 5242912 | tf_op jit(solution)/shard_map/all_to_all | solution.py:350
  95.3 35.6 %field_stage.1 = f32[8,8,2560]{2,1,0:T(8,128)} custom-call(s32[18]{0:T(128)} %pad_add_fusion.place, f32[10240,128]{1,0:T(8,128)} %bitcast.7.received, bf16[512,512]{1,0:T(8,128)(2,1)} %constant.37.clone.t_high, bf16[512,512]{1,0:T(8,128)(2,1)} %constant.38.clone.t_low, bf16[64,256]{1,0:T(8,128)(2,1)} %get-tuple-element.13.y_high, ...), custom_call_target="tpu_custom_call" | custom-call | tf_op jit(solution)/shard_map/field_stage/pallas_call | solution.py:267
  130.9 5.7 %all-to-all-start.2 = ((f32[8,8,2560]{2,1,0:T(8,128)}), f32[8,8,2560]{2,1,0:T(8,128)S(1)}, u32[]{:S(2)}, u32[]{:S(2)}) async-start(f32[8,8,2560]{2,1,0:T(8,128)} %field_stage.1), calls=%async_computation.2 | async-start | bytes 1310720 | tf_op jit(solution)/shard_map/all_to_all | solution.py:357
  136.6 1.3 slice.43.slots
  137.8 8.1 %all-to-all-done.2.values = f32[8,8,2560]{2,1,0:T(8,128)S(1)} async-done(((f32[8,8,2560]{2,1,0:T(8,128)}), f32[8,8,2560]{2,1,0:T(8,128)S(1)}, u32[]{:S(2)}, u32[]{:S(2)}) %all-to-all-start.2) | async-done | bytes 655392 | tf_op jit(solution)/shard_map/all_to_all | solution.py:357
  145.9 0.0 copy-start.1
  145.9 0.8 copy-done.1
  146.8 2.5 %ghost_stage.1 = (f32[8,2048]{1,0:T(8,128)}, f32[8,2048]{1,0:T(8,128)}) custom-call(f32[8,8,2560]{2,1,0:T(8,128)} %copy-done.1, s32[1,512]{1,0:T(1,128)} %slice.43.slots), custom_call_target="tpu_custom_call" | custom-call | tf_op jit(solution)/shard_map/ghost_stage/pallas_call | solution.py:309
  149.2 4.9 %collective-permute-start = (f32[8,2048]{1,0:T(8,128)}, f32[8,2048]{1,0:T(8,128)S(1)}, u32[]{:S(2)}, u32[]{:S(2)}) collective-permute-start(f32[8,2048]{1,0:T(8,128)} %get-tuple-element.5), channel_id=1, source_target_pairs={{8,0},{16,8},{24,16},{32,24},{40,32},{48,40},{56,48},{64,56},{72,6... | collective-permute-start | bytes 196616 | tf_op jit(solution)/shard_map/ppermute | solution.py:361
  154.2 2.1 %collective-permute-done = f32[8,2048]{1,0:T(8,128)S(1)} collective-permute-done((f32[8,2048]{1,0:T(8,128)}, f32[8,2048]{1,0:T(8,128)S(1)}, u32[]{:S(2)}, u32[]{:S(2)}) %collective-permute-start) | collective-permute-done | bytes 65568 | tf_op jit(solution)/shard_map/ppermute | solution.py:361
  156.3 0.9 add.9
  157.1 0.6 slice.47
  157.7 0.6 slice.48
  (5 shorter events, 0.0 us)
Async XLA Ops:
  8.6 19.3 %all-to-all-start = ((f32[8,8,2560]{2,1,0:T(8,128)}), f32[8,8,2560]{2,1,0:T(8,128)S(1)}, u32[]{:S(2)}, u32[]{:S(2)}) async-start(f32[8,8,2560]{2,1,0:T(8,128)} %broadcast_in_dim.27), calls=%async_computation | async-start | bytes 1310720 | tf_op jit(solution)/shard_map/all_to_all | solution.py:341
  27.9 8.1 %copy-start = (f32[8,8,2560]{2,1,0:T(8,128)}, f32[8,8,2560]{2,1,0:T(8,128)S(1)}, u32[]{:S(2)}) copy-start(f32[8,8,2560]{2,1,0:T(8,128)S(1)} %all-to-all-done.particles) | copy-start | bytes 1966084
  27.9 67.4 %all-to-all-start.1 = ((f32[16,16,40,128]{3,2,1,0:T(8,128)}), f32[16,16,40,128]{3,2,1,0:T(8,128)}, u32[]{:S(2)}, u32[]{:S(2)}) async-start(f32[16,16,40,128]{3,2,1,0:T(8,128)} %z_stage.1), calls=%async_computation.1 | async-start | bytes 10485760 | tf_op jit(solution)/shard_map/all_to_all | solution.py:350
  130.9 15.1 %all-to-all-start.2 = ((f32[8,8,2560]{2,1,0:T(8,128)}), f32[8,8,2560]{2,1,0:T(8,128)S(1)}, u32[]{:S(2)}, u32[]{:S(2)}) async-start(f32[8,8,2560]{2,1,0:T(8,128)} %field_stage.1), calls=%async_computation.2 | async-start | bytes 1310720 | tf_op jit(solution)/shard_map/all_to_all | solution.py:357
  145.9 0.9 copy-start.1
  149.2 7.0 %collective-permute-start = (f32[8,2048]{1,0:T(8,128)}, f32[8,2048]{1,0:T(8,128)S(1)}, u32[]{:S(2)}, u32[]{:S(2)}) collective-permute-start(f32[8,2048]{1,0:T(8,128)} %get-tuple-element.5), channel_id=1, source_target_pairs={{8,0},{16,8},{24,16},{32,24},{40,32},{48,40},{56,48},{64,56},{72,6... | collective-permute-start | bytes 196616 | tf_op jit(solution)/shard_map/ppermute | solution.py:361

commit v2 on v1

v2 whole, which is shorter than its diff:
```python
import math

import jax
import jax.numpy as jnp
import numpy as np
from jax import lax
from jax.experimental import pallas as pl
from jax.experimental.pallas import tpu as pltpu
from jax.sharding import PartitionSpec as P

F32 = jnp.float32
BF16 = jnp.bfloat16
SUPPORT = 8
GRID = 256
HALF = GRID // 2
N_GX = 16
N_GY = 8
OWN = 2048
GHOST = 512
ROWS = OWN + GHOST
WAVE = 2.0 * math.pi / GRID
WINDOW = 48
BLOCK = 256
CHUNKS = ((0, 1, 2, 3),)
EXTRA = 4


def numpy_halves(table):
    import ml_dtypes

    high = table.astype(ml_dtypes.bfloat16)
    low = (table - high.astype(np.float64)).astype(ml_dtypes.bfloat16)
    return high, low


def left_triple(table):
    high, low = numpy_halves(table)
    return np.concatenate([high, high, low], axis=-1)


def z_table():
    c1, slab, part, step = np.meshgrid(
        np.arange(2), np.arange(N_GX), np.arange(2), np.arange(4), indexing="ij"
    )
    position = (8 * slab + 2 * step + c1).reshape(-1, 1)
    part = part.reshape(-1, 1)
    angle = (position * np.arange(HALF)[None, :] % HALF) * (2.0 * np.pi / HALF)
    cosine, sine = np.cos(angle), np.sin(angle)
    from_real = np.where(part == 0, cosine, sine)
    from_imag = np.where(part == 0, -sine, cosine)
    return np.concatenate([from_real, from_imag], axis=1)


def x_table(parity):
    modes = 2 * np.arange(HALF) + parity
    angle = (np.arange(HALF)[:, None] * modes[None, :] % GRID) * (2.0 * np.pi / GRID)
    cosine, sine = np.cos(angle), np.sin(angle)
    return np.block([[cosine, -sine], [sine, cosine]])


def y_table():
    index = np.arange(GRID)
    angle = (index[:, None] * index[None, :] % GRID) * (2.0 * np.pi / GRID)
    cosine = np.cos(angle).reshape(N_GY, 1, GRID // N_GY, GRID)
    sine = -np.sin(angle).reshape(N_GY, 1, GRID // N_GY, GRID)
    return np.concatenate([cosine, sine], axis=1).reshape(N_GY, 2 * (GRID // N_GY), GRID)


def twiddles():
    angle = np.arange(HALF) * (2.0 * np.pi / GRID)
    table = np.stack([np.cos(angle), np.sin(angle)])
    return np.repeat(table[:, None, :], 32, axis=1).astype(np.float32)


def split(value):
    high = value.astype(BF16)
    return high, (value - high.astype(F32)).astype(BF16)


def signed(index):
    return jnp.where(index < GRID // 2, index, index - GRID).astype(F32)


NT = (((1,), (1,)), ((), ()))
NN = (((1,), (0,)), ((), ()))


def dot(a, b, dims):
    return lax.dot_general(a, b, dims, preferred_element_type=F32)


def z_kernel(pieces, place, source, table, twiddle, out, even, odd):
    quad = pl.program_id(0)
    with_extra = EXTRA in pieces
    parities = [p for p in range(2) if with_extra or any(c % 2 == p for c in pieces)]
    row = lax.broadcasted_iota(jnp.int32, (32, GRID), 0)
    mode_y = signed(row + place[1] * 32)
    mode_z = signed(lax.broadcasted_iota(jnp.int32, (32, GRID), 1))
    wave_z = WAVE * mode_z
    partial_square = mode_y * mode_y + mode_z * mode_z
    turn_re, turn_im = twiddle[0], twiddle[1]
    for k in range(4):
        index_x = place[0] * 16 + quad * 4 + k
        mode_x = jnp.where(index_x < GRID // 2, index_x, index_x - GRID).astype(F32)
        inverse = 1.0 / jnp.maximum(mode_x * mode_x + partial_square, 1.0)
        v = []
        for r in range(2):
            s1, s2, s3 = source[r, 0, k], source[r, 1, k], source[r, 2, k]
            ratio = (s1 * mode_x + s2 * mode_y + s3 * mode_z) * inverse
            v.append((s1 - mode_x * ratio, s2 - mode_y * ratio, s3 - mode_z * ratio))
        rows = [
            (v[0][0], v[1][0], k * 128),
            (v[0][1], v[1][1], k * 128 + 32),
            (v[0][2], v[1][2], k * 128 + 64),
            (-wave_z * v[1][0], wave_z * v[0][0], k * 128 + 96),
        ]
        if with_extra:
            rows.append((-wave_z * v[1][1], wave_z * v[0][1], 512 + k * 32))
        for real, imag, start in rows:
            here = slice(start, start + 32)
            for p in parities:
                if p == 0:
                    re = real[:, :HALF] + real[:, HALF:]
                    im = imag[:, :HALF] + imag[:, HALF:]
                    target = even
                else:
                    re0 = real[:, :HALF] - real[:, HALF:]
                    im0 = imag[:, :HALF] - imag[:, HALF:]
                    re = re0 * turn_re - im0 * turn_im
                    im = re0 * turn_im + im0 * turn_re
                    target = odd
                for r, value in ((0, re), (1, im)):
                    high, low = split(value)
                    target[here, r * HALF : (r + 1) * HALF] = high
                    target[here, GRID + r * HALF : GRID + (r + 1) * HALF] = low
                    target[here, 2 * GRID + r * HALF : 2 * GRID + (r + 1) * HALF] = high

    for p in parities:
        data = (even, odd)[p]
        wanted = [c for c in pieces if c != EXTRA and c % 2 == p]
        if not wanted:
            continue
        c_low, c_high = min(wanted) // 2, max(wanted) // 2 + 1
        for pair in range(2):
            result = dot(
                table[c_low * 128 : c_high * 128], data[pair * 256 : pair * 256 + 256], NT
            )
            for c in wanted:
                top = (c // 2 - c_low) * 128
                for side in range(2):
                    out[:, pieces.index(c), pair * 2 + side] = result[
                        top : top + 128, side * 128 : side * 128 + 128
                    ].reshape(N_GX, 8, 128)
    if with_extra:
        halves = [dot(table[...], data[512:640], NT) for data in (even, odd)]
        v = [halves[c % 2][(c // 2) * 128 : (c // 2) * 128 + 128] for c in range(4)]
        lane = lax.broadcasted_iota(jnp.int32, (128, 128), 1)
        lower64 = lane < 64
        lower32 = (lane & 32) == 0
        p0 = [jnp.where(lower64, v[c], pltpu.roll(v[c + 2], 64, 1)) for c in range(2)]
        p1 = [jnp.where(lower64, pltpu.roll(v[c], 64, 1), v[c + 2]) for c in range(2)]
        place_of = pieces.index(EXTRA)
        for k1, p in ((0, p0), (1, p1)):
            q0 = jnp.where(lower32, p[0], pltpu.roll(p[1], 32, 1))
            q1 = jnp.where(lower32, pltpu.roll(p[0], 96, 1), p[1])
            out[:, place_of, 2 * k1] = q0.reshape(N_GX, 8, 128)
            out[:, place_of, 2 * k1 + 1] = q1.reshape(N_GX, 8, 128)


def z_stage(pieces, place, source, table, twiddle):
    def kernel(*refs):
        z_kernel(pieces, *refs)

    return pl.pallas_call(
        kernel,
        out_shape=jax.ShapeDtypeStruct((N_GX, len(pieces), 16, 8, 128), F32),
        grid_spec=pltpu.PrefetchScalarGridSpec(
            num_scalar_prefetch=1,
            grid=(4,),
            in_specs=[
                pl.BlockSpec((2, 3, 4, 32, GRID), lambda i, _: (0, 0, i, 0, 0)),
                pl.BlockSpec((256, 768), lambda i, _: (0, 0)),
                pl.BlockSpec((2, 32, HALF), lambda i, _: (0, 0, 0)),
            ],
            out_specs=pl.BlockSpec(
                (N_GX, len(pieces), 4, 8, 128), lambda i, _: (0, 0, i, 0, 0)
            ),
            scratch_shapes=[pltpu.VMEM((640, 768), BF16), pltpu.VMEM((640, 768), BF16)],
        ),
        name="z_stage",
    )(place, source, table, twiddle)


def weight(distance, offset):
    shifted = distance - (SUPPORT // 2 - 1) - offset
    inside = (distance >= 0.0) & (distance < SUPPORT)
    return jnp.where(inside, jnp.exp(-5.6 / SUPPORT * shifted * shifted), 0.0)


def wrapped(distance):
    return jnp.where(distance < 0.0, distance + GRID, distance)


def gather_kernel(counts, after, start, offset, other_start, other_offset, out):
    own, ghosts = counts[0, 0], counts[0, 2]
    out[0:3, :OWN] = start[...].astype(F32)
    out[3:6, :OWN] = offset[...]
    out[0:3, OWN:] = other_start[...].astype(F32)
    out[3:6, OWN:] = other_offset[...]
    lane = lax.broadcasted_iota(jnp.int32, (1, ROWS), 1)
    bound = jnp.where(lane < OWN, own, OWN + ghosts)
    out[6:7, :] = jnp.where(lane < bound, 1.0, 0.0)
    out[7:8, :] = jnp.where(lane == 0, own, jnp.where(lane == 1, ghosts, 0)).astype(F32)


def gather_stage(counts, after, start, offset, other_start, other_offset):
    vmem = pl.BlockSpec(memory_space=pltpu.VMEM)
    return pl.pallas_call(
        gather_kernel,
        out_shape=jax.ShapeDtypeStruct((8, ROWS), F32),
        in_specs=[
            pl.BlockSpec(memory_space=pltpu.SMEM),
            pl.BlockSpec(memory_space=pl.ANY),
            vmem,
            vmem,
            vmem,
            vmem,
        ],
        out_specs=vmem,
        name="gather_stage",
    )(counts, after, start, offset, other_start, other_offset)


def for_live_blocks(place, owner, body):
    def own_block(index, carry):
        body(pl.multiple_of(index * BLOCK, BLOCK))
        return carry

    def ghost_block(index, carry):
        body(pl.multiple_of(OWN + index * BLOCK, BLOCK))
        return carry

    lax.fori_loop(0, (place[2 + owner] + BLOCK - 1) // BLOCK, own_block, 0)
    lax.fori_loop(0, (place[10 + owner] + BLOCK - 1) // BLOCK, ghost_block, 0)


def row_kernel(place, particles, table, phases):
    y_cell = lax.broadcasted_iota(jnp.int32, (GRID, BLOCK), 0).astype(F32)

    def one_block(start):
        data = particles[0, :, pl.ds(start, BLOCK)]
        weight_y = weight(wrapped(y_cell - data[1:2]), data[4:5])
        high, low = split(weight_y)
        phases[0, :, pl.ds(start, BLOCK)] = dot(
            table[...], jnp.concatenate([high, low, high], axis=0), NN
        )

    for_live_blocks(place, pl.program_id(0), one_block)


def row_stage(place, particles, table):
    return pl.pallas_call(
        row_kernel,
        out_shape=jax.ShapeDtypeStruct((N_GY, 64, ROWS), F32),
        grid_spec=pltpu.PrefetchScalarGridSpec(
            num_scalar_prefetch=1,
            grid=(N_GY,),
            in_specs=[
                pl.BlockSpec((1, 8, ROWS), lambda i, _: (i, 0, 0)),
                pl.BlockSpec((64, 768), lambda i, _: (0, 0)),
            ],
            out_specs=pl.BlockSpec((1, 64, ROWS), lambda i, _: (i, 0, 0)),
        ),
        name="row_stage",
    )(place, particles, table)


def field_kernel(
    steps, place, main, extra, t_even, t_odd, particles, phases_in, *rest
):
    if len(rest) == 8:
        previous, out, field, d_even, d_odd, window, phases, arrival = rest
    else:
        previous = None
        out, field, d_even, d_odd, window, phases, arrival = rest
    first_c = steps[0]
    step_c = pl.program_id(0)
    c = first_c + step_c
    copy = pltpu.make_async_copy(phases_in, phases, arrival)

    @pl.when(step_c == 0)
    def _():
        copy.start()

    lane = lax.broadcasted_iota(jnp.int32, (HALF, 128), 1)
    group = lane // 32
    row = lax.broadcasted_iota(jnp.int32, (HALF, 128), 0)
    wave_y = WAVE * signed(lane % 32 + place[1] * 32)
    last_group = group == 3
    on_left = jnp.where(group == 0, wave_y, 0.0)
    on_right = jnp.where((group == 1) | last_group, 0.5 * wave_y, 0.0)
    half_same = jnp.where((group == 1) | (group == 2), 0.5, 0.0)
    half_left = jnp.where(group == 2, 0.5, 0.0)
    half_extra = jnp.where(last_group, 0.5, 0.0)
    flat_main = main.reshape(GRID * 8, 128)
    flat_extra = extra.reshape(GRID * 8, 128)

    def one_z(step, carry):
        for parity, target in ((0, d_even), (1, d_odd)):
            wave_x = WAVE * signed(2 * row + parity)

            def load(flat, q):
                return flat[pl.ds(parity * 8 + q * 4 + step, HALF, stride=16), :]

            parts = []
            for q in range(2):
                value = load(flat_main, q)
                moved = pltpu.roll(load(flat_extra, q), 32 * (3 - c), 1)
                parts.append((value, pltpu.roll(value, 96, 1), pltpu.roll(value, 32, 1), moved))
            (a_re, l_re, r_re, e_re), (a_im, l_im, r_im, e_im) = parts
            on_same = half_same * wave_x
            first_re = jnp.where(last_group, -wave_x * l_im, a_re)
            first_im = jnp.where(last_group, wave_x * l_re, a_im)
            second_re = (half_left * l_re + half_extra * e_re) - (
                on_left * l_im + on_right * r_im + on_same * a_im
            )
            second_im = (half_left * l_im + half_extra * e_im) + (
                on_left * l_re + on_right * r_re + on_same * a_re
            )
            for top, left, value in (
                (0, 0, first_re),
                (HALF, 0, first_im),
                (0, 128, second_re),
                (HALF, 128, second_im),
            ):
                high, low = split(value)
                lanes = slice(left, left + 128)
                target[top : top + HALF, lanes] = high
                target[GRID + top : GRID + top + HALF, lanes] = low
                target[2 * GRID + top : 2 * GRID + top + HALF, lanes] = high
        from_even = dot(t_even[...], d_even[...], NN)
        from_odd = dot(t_odd[...], d_odd[...], NN)
        near = (from_even + from_odd).astype(BF16)
        far = (from_even - from_odd).astype(BF16)
        z = step_c * 4 + step
        for q in range(2):
            lanes = slice(q * 256, q * 256 + 256)
            field[z, 0:HALF, lanes] = near[q * HALF : q * HALF + HALF]
            field[z, HALF:GRID, lanes] = far[q * HALF : q * HALF + HALF]
            field[z, GRID : GRID + 16, lanes] = near[q * HALF : q * HALF + 16]
        return carry

    lax.fori_loop(0, 4, one_z, 0)

    @pl.when(step_c == len(steps) - 1)
    def _():
        if previous is None:
            out[...] = jnp.zeros_like(out)
        else:
            out[...] = previous[...]
        copy.wait()
        planes = 4 * len(steps)
        x_cell = lax.broadcasted_iota(jnp.int32, (WINDOW, BLOCK), 0).astype(F32)
        local_z = lax.broadcasted_iota(jnp.int32, (planes, BLOCK), 0)
        z_cell = (place[0] * 16 + first_c + 4 * (local_z % 4) + local_z // 4).astype(F32)

        def one_owner(index, carry):
            owner = (place[1] - index) & (N_GY - 1)
            block = field[:, pl.ds(pl.multiple_of(owner * 32, 16), WINDOW), :]
            window[...] = block.reshape(planes * WINDOW, 512).T
            base_x = (owner * 32).astype(F32)

            def one_block(start):
                data = particles[index, :, pl.ds(start, BLOCK)]
                weight_x = weight(x_cell + base_x - data[0:1], data[3:4])
                weight_z = weight(wrapped(z_cell - data[2:3]), data[5:6]) * data[6:7]
                plane = jnp.concatenate(
                    [(weight_x * weight_z[z : z + 1]).astype(BF16) for z in range(planes)], axis=0
                )
                summed = dot(window[...], plane, NN).reshape(2, 8, 32, BLOCK)
                phase = phases[index, :, pl.ds(start, BLOCK)]
                product = summed[0] * phase[None, 0:32] + summed[1] * phase[None, 32:64]
                value = jnp.sum(product, axis=1)
                if previous is not None:
                    value = value + out[owner, :, pl.ds(start, BLOCK)]
                out[owner, :, pl.ds(start, BLOCK)] = value

            for_live_blocks(place, index, one_block)
            return carry

        lax.fori_loop(0, N_GY, one_owner, 0)


def field_stage(steps, first, place, main, extra, extra_at, t_even, t_odd, particles, phases, previous):
    def whole(shape):
        return pl.BlockSpec(
            shape, lambda i, _: (0,) * len(shape), pipeline_mode=pl.Buffered(1)
        )

    def kernel(*refs):
        field_kernel(steps, *refs)

    piece = (N_GX, None, 16, 8, 128)
    in_specs = [
        pl.BlockSpec(piece, lambda i, _: (0, first + i, 0, 0, 0)),
        pl.BlockSpec(piece, lambda i, _: (0, extra_at, 0, 0, 0)),
        whole((256, 768)),
        whole((256, 768)),
        whole((N_GY, 8, ROWS)),
        pl.BlockSpec(memory_space=pl.ANY),
    ]
    operands = [place, main, extra, t_even, t_odd, particles, phases]
    if previous is not None:
        in_specs.append(whole((N_GY, 8, ROWS)))
        operands.append(previous)
    planes = 4 * len(steps)
    return pl.pallas_call(
        kernel,
        out_shape=jax.ShapeDtypeStruct((N_GY, 8, ROWS), F32),
        grid_spec=pltpu.PrefetchScalarGridSpec(
            num_scalar_prefetch=1,
            grid=(len(steps),),
            in_specs=in_specs,
            out_specs=whole((N_GY, 8, ROWS)),
            scratch_shapes=[
                pltpu.VMEM((planes, GRID + 16, 512), BF16),
                pltpu.VMEM((768, 256), BF16),
                pltpu.VMEM((768, 256), BF16),
                pltpu.VMEM((512, planes * WINDOW), BF16),
                pltpu.VMEM((N_GY, 64, ROWS), F32),
                pltpu.SemaphoreType.DMA,
            ],
        ),
        name="field_stage",
    )(*operands)


def ghost_kernel(values, slots, own, back):
    total = values[0]
    for source in range(1, N_GY):
        total = total + values[source]
    own[...] = total[:, :OWN]
    ghosts = total[:, OWN:]
    cell = lax.broadcasted_iota(jnp.int32, (OWN, GHOST), 0)
    chosen = (cell == slots[...]).astype(F32).astype(BF16)
    first, rest = split(ghosts)
    second, third = split(ghosts - first.astype(F32))
    parts = jnp.concatenate([first.astype(F32), second.astype(F32), third.astype(F32)], axis=0)
    placed = dot(parts.astype(BF16), chosen, NT)
    back[...] = placed[0:8] + (placed[8:16] + placed[16:24])


def ghost_stage(values, slots):
    return pl.pallas_call(
        ghost_kernel,
        out_shape=(
            jax.ShapeDtypeStruct((8, OWN), F32),
            jax.ShapeDtypeStruct((8, OWN), F32),
        ),
        name="ghost_stage",
    )(values, slots)


def final_kernel(own, arrived, velocity, strain):
    total = own[...] + arrived[...]
    velocity[...] = total[:3]
    strain[...] = total[3:]


def final_stage(own, arrived):
    return pl.pallas_call(
        final_kernel,
        out_shape=(
            jax.ShapeDtypeStruct((3, OWN), F32),
            jax.ShapeDtypeStruct((5, OWN), F32),
        ),
        name="final_stage",
    )(own, arrived)


def per_device(
    source_hat, particle_start, particle_offset, ghost_start, ghost_offset, ghost_slot, counts
):
    index_gx = lax.axis_index("gx").astype(jnp.int32)
    index_gy = lax.axis_index("gy").astype(jnp.int32)
    here = jnp.stack([index_gx, index_gy])

    table_z = jnp.asarray(left_triple(z_table()))
    twiddle = jnp.asarray(twiddles())
    sent = [
        z_stage(chunk + ((EXTRA,) if number == 0 else ()), here, source_hat, table_z, twiddle)
        for number, chunk in enumerate(CHUNKS)
    ]
    received = [
        lax.all_to_all(piece, "gx", split_axis=0, concat_axis=0, tiled=True) for piece in sent
    ]

    mine = gather_stage(
        counts, sent[0], particle_start, particle_offset, ghost_start[:, 1], ghost_offset[:, 1]
    )
    members = range(N_GY)
    particles = jnp.stack(
        [mine]
        + [
            lax.ppermute(mine, "gy", [(i, (i + shift) % N_GY) for i in members])
            for shift in range(1, N_GY)
        ]
    )
    live_counts = particles[:, 7, 0:2].astype(jnp.int32)
    place = jnp.concatenate([here, live_counts[:, 0], live_counts[:, 1]])
    table_y = jnp.asarray(left_triple(y_table()))
    table_y = lax.dynamic_index_in_dim(table_y, index_gy, 0, keepdims=False)
    phases = row_stage(place, particles, table_y)

    t_even = jnp.asarray(left_triple(x_table(0)))
    t_odd = jnp.asarray(left_triple(x_table(1)))
    partial = None
    for number, chunk in enumerate(CHUNKS):
        partial = field_stage(
            chunk, 0, place, received[number], received[0], len(CHUNKS[0]),
            t_even, t_odd, particles, phases, partial,
        )
    partial = lax.all_to_all(partial, "gy", split_axis=0, concat_axis=0, tiled=True)
    own, back = ghost_stage(partial, ghost_slot[1:2])
    devices = range(N_GX)
    route = [((i + 1) % N_GX, i) for i in devices]
    return final_stage(own, lax.ppermute(back, "gx", route))


def solution(mesh):
    in_specs = (
        P(None, None, "gx", "gy", None),
        P(None, ("gx", "gy")),
        P(None, ("gx", "gy")),
        P(None, None, ("gx", "gy")),
        P(None, None, ("gx", "gy")),
        P(None, ("gx", "gy")),
        P(("gx", "gy"), None),
    )
    out_specs = (P(None, ("gx", "gy")), P(None, ("gx", "gy")))
    return jax.shard_map(
        per_device, mesh=mesh, in_specs=in_specs, out_specs=out_specs, check_vma=False
    )
```

time: 160 us -> 167 us (1.044)
  Pallas kernels: 47.7 us -> 56.6 us
  other arithmetic: 7.03 us -> 1.22 us
  starting transfers between devices: 24.8 us -> 29.9 us
    ppermute x1 -> x8, waiting for transfers between devices: 2.1 us -> 62.3 us  [the longest x7 57.4 us: per_device(): lax.ppermute(mine, 'gy', [(i, (i + shift) % N_GY) for i in members])]
    all_to_all x2 -> x1, waiting for transfers between devices: 60.1 us -> 0.01 us  [per_device(): lax.all_to_all(piece, 'gx', split_axis=0, concat_axis=0, tiled=True)]
    ppermute x1 -> x8, starting transfers between devices: 4.92 us -> 18.9 us  [the longest x7 14.9 us: per_device(): lax.ppermute(mine, 'gy', [(i, (i + shift) % N_GY) for i in members])]
    pallas_call x2 -> x5, Pallas kernels: 45.3 us -> 54.1 us  [the longest x1 29.7 us: field_stage(): pl.pallas_call(kernel, out_shape=jax.ShapeDtypeStruct((N_GY, 8, ROWS), F3...]
    all_to_all x2 -> x1, starting transfers between devices: 14.1 us -> 7.51 us  [per_device(): lax.all_to_all(piece, 'gx', split_axis=0, concat_axis=0, tiled=True)]
    convert_element_type x3 -> x0, other arithmetic: 2.81 us -> none  [the longest x1 1.3 us: per_device(): count_row = jnp.where(column == 0, counts[0, 0], jnp.where(column == 1, c...]
    all_to_all x1, starting transfers between devices: 5.71 us -> 3.55 us  [per_device(): lax.all_to_all(partial, 'gy', split_axis=0, concat_axis=0, tiled=True)]
    unnamed x5 -> x17, local copies, waits for them, and re-layouts: 0.86 us -> 2.87 us
  transfers between devices with their start and end apart: 4 -> 10, of which waited for: 4 -> 4; matrix products, arithmetic and copies ran while one was open for 3% -> 2% of each run, Pallas kernels for 6% -> 8%
where the time goes in v2:
time: 167 us; the launch traced here: 166 us
  waiting for transfers between devices  70.4 us (42%)
  Pallas kernels  56.6 us (34%)
  starting transfers between devices  29.9 us (18%)
  local copies, waits for them, and re-layouts  7.28 us (4%)
    ppermute x7, waiting for transfers between devices, per_device(): lax.ppermute(mine, 'gy', [(i, (i + shift) % N_GY) for i in members])  57.4 us
    pallas_call x1, Pallas kernels, field_stage(): pl.pallas_call(kernel, out_shape=jax.ShapeDtypeStruct((N_GY, 8, ROWS), F3...  29.7 us
    ppermute x7, starting transfers between devices, per_device(): lax.ppermute(mine, 'gy', [(i, (i + shift) % N_GY) for i in members])  14.9 us
    pallas_call x1, Pallas kernels, row_stage(): pl.pallas_call(row_kernel, out_shape=jax.ShapeDtypeStruct((N_GY, 64, ROWS...  12.9 us
    pallas_call x1, Pallas kernels, z_stage(): pl.pallas_call(kernel, out_shape=jax.ShapeDtypeStruct((N_GX, len(pieces),...  8.46 us
    all_to_all x1, waiting for transfers between devices, per_device(): lax.all_to_all(partial, 'gy', split_axis=0, concat_axis=0, tiled=True)  8.1 us
    all_to_all x1, starting transfers between devices, per_device(): lax.all_to_all(piece, 'gx', split_axis=0, concat_axis=0, tiled=True)  7.51 us
    ppermute x1, waiting for transfers between devices, per_device(): return final_stage(own, lax.ppermute(back, 'gx', route))  4.86 us
  transfers between devices with their start and end apart: 10, of which 4 were waited for; matrix products, arithmetic and copies ran while one was open for 2% of the time, Pallas kernels for 8%

profile of v2, /device:TPU:1, one launch (start us, length us, event | category | flops | bytes accessed | tf_op | source)
XLA Modules:
  0.0 166.1 jit_solution(12533555475120759778)
XLA Ops:
  0.6 0.7 slice.18
  1.4 0.6 copy.25
  2.0 0.7 slice.19
  2.7 0.6 copy.24
  3.3 0.6 pad_add_fusion.refs_0_
  3.9 8.5 %z_stage.1.after = f32[16,5,16,8,128]{4,3,2,1,0:T(8,128)} custom-call(s32[2]{0:T(128)} %pad_add_fusion.refs_0_, f32[2,3,16,32,256]{4,3,2,1,0:T(8,128)} %refs_1_.1, bf16[256,768]{1,0:T(8,128)(2,1)} %constant.25.clone.refs_2_, f32[2,32,128]{2,1,0:T(8,128)} %constant.26.clone.refs_3_), custom_call_target="tpu_custom_call" | custom-call | tf_op jit(solution)/shard_map/z_stage/pallas_call | solution.py:174
  12.4 1.5 gather_stage.1
  13.8 3.7 %collective-permute-start = (f32[8,2560]{1,0:T(8,128)}, f32[8,2560]{1,0:T(8,128)S(1)}, u32[]{:S(2)}, u32[]{:S(2)}) collective-permute-start(f32[8,2560]{1,0:T(8,128)} %gather_stage.1), channel_id=1, source_target_pairs={{0,1},{1,2},{2,3},{3,4},{4,5},{5,6},{6,7},{7,0},{8,9},{9,10},{10,1... | collective-permute-start | bytes 245768 | tf_op jit(solution)/shard_map/ppermute | solution.py:505
  17.6 1.2 collective-permute-start.1
  18.8 1.6 collective-permute-start.2
  20.4 1.7 %collective-permute-start.3 = (f32[8,2560]{1,0:T(8,128)}, f32[8,2560]{1,0:T(8,128)S(1)}, u32[]{:S(2)}, u32[]{:S(2)}) collective-permute-start(f32[8,2560]{1,0:T(8,128)} %gather_stage.1), channel_id=1, source_target_pairs={{0,4},{1,5},{2,6},{3,7},{4,0},{5,1},{6,2},{7,3},{8,12},{9,13},{10,... | collective-permute-start | bytes 245768 | tf_op jit(solution)/shard_map/ppermute | solution.py:505
  22.1 4.5 %collective-permute-start.4 = (f32[8,2560]{1,0:T(8,128)}, f32[8,2560]{1,0:T(8,128)S(1)}, u32[]{:S(2)}, u32[]{:S(2)}) collective-permute-start(f32[8,2560]{1,0:T(8,128)} %gather_stage.1), channel_id=1, source_target_pairs={{0,5},{1,6},{2,7},{3,0},{4,1},{5,2},{6,3},{7,4},{8,13},{9,14},{10,... | collective-permute-start | bytes 245768 | tf_op jit(solution)/shard_map/ppermute | solution.py:505
  26.6 7.5 %all-to-all-start = ((f32[16,5,16,8,128]{4,3,2,1,0:T(8,128)}), f32[16,5,16,8,128]{4,3,2,1,0:T(8,128)}, u32[]{:S(2)}, u32[]{:S(2)}) async-start(f32[16,5,16,8,128]{4,3,2,1,0:T(8,128)} %z_stage.1.after), calls=%async_computation | async-start | bytes 10485760 | tf_op jit(solution)/shard_map/all_to_all | solution.py:495
  34.2 1.5 dynamic-slice_bitcast_fusion.table
  35.7 1.2 collective-permute-start.5
  36.9 1.0 collective-permute-start.6
  38.0 1.7 %collective-permute-done.5 = f32[8,2560]{1,0:T(8,128)S(1)} collective-permute-done((f32[8,2560]{1,0:T(8,128)S(1)}, f32[8,2560]{1,0:T(8,128)S(1)}, u32[]{:S(2)}, u32[]{:S(2)}) %collective-permute-start.5) | collective-permute-done | bytes 81952 | tf_op jit(solution)/shard_map/ppermute | solution.py:505
  39.7 55.7 %collective-permute-done.6 = f32[8,2560]{1,0:T(8,128)S(1)} collective-permute-done((f32[8,2560]{1,0:T(8,128)S(1)}, f32[8,2560]{1,0:T(8,128)S(1)}, u32[]{:S(2)}, u32[]{:S(2)}) %collective-permute-start.6) | collective-permute-done | bytes 81952 | tf_op jit(solution)/shard_map/ppermute | solution.py:505
  95.4 0.1 copy.19
  95.5 0.6 pad_add_fusion.1.place.refs_0_
  96.1 0.1 copy-done
  96.2 12.9 %row_stage.1.refs_6_ = f32[8,64,2560]{2,1,0:T(8,128)} custom-call(s32[18]{0:T(128)} %pad_add_fusion.1.place.refs_0_, f32[8,8,2560]{2,1,0:T(8,128)} %copy-done, bf16[64,768]{1,0:T(8,128)(2,1)} %dynamic-slice_bitcast_fusion.table), custom_call_target="tpu_custom_call" | custom-call | tf_op jit(solution)/shard_map/row_stage/pallas_call | solution.py:262
  109.2 29.7 %field_stage.1 = f32[8,8,2560]{2,1,0:T(8,128)} custom-call(s32[18]{0:T(128)} %pad_add_fusion.1.place.refs_0_, f32[16,5,16,8,128]{4,3,2,1,0:T(8,128)} %all-to-all-done.refs_1_.refs_2_, f32[16,5,16,8,128]{4,3,2,1,0:T(8,128)} %all-to-all-done.refs_1_.refs_2_, bf16[256,768]{1,0:T(8,128)(2,1)} %constant.28.clone.refs_3_, ...), custom_call_target="tpu_custom_call" | custom-call | tf_op jit(solution)/shard_map/field_stage/pallas_call | solution.py:417
  138.9 3.6 %all-to-all-start.1 = ((f32[8,8,2560]{2,1,0:T(8,128)}), f32[8,8,2560]{2,1,0:T(8,128)S(1)}, u32[]{:S(2)}, u32[]{:S(2)}) async-start(f32[8,8,2560]{2,1,0:T(8,128)} %field_stage.1), calls=%async_computation.1 | async-start | bytes 1310720 | tf_op jit(solution)/shard_map/all_to_all | solution.py:523
  142.5 1.3 slice.23.slots
  143.7 8.1 %all-to-all-done.1.values = f32[8,8,2560]{2,1,0:T(8,128)S(1)} async-done(((f32[8,8,2560]{2,1,0:T(8,128)}), f32[8,8,2560]{2,1,0:T(8,128)S(1)}, u32[]{:S(2)}, u32[]{:S(2)}) %all-to-all-start.1) | async-done | bytes 655392 | tf_op jit(solution)/shard_map/all_to_all | solution.py:523
  151.8 0.8 copy-done.1
  152.7 2.5 %ghost_stage.1 = (f32[8,2048]{1,0:T(8,128)}, f32[8,2048]{1,0:T(8,128)}) custom-call(f32[8,8,2560]{2,1,0:T(8,128)} %copy-done.1, s32[1,512]{1,0:T(1,128)} %slice.23.slots), custom_call_target="tpu_custom_call" | custom-call | tf_op jit(solution)/shard_map/ghost_stage/pallas_call | solution.py:454
  155.2 3.9 %collective-permute-start.7 = (f32[8,2048]{1,0:T(8,128)}, f32[8,2048]{1,0:T(8,128)S(1)}, u32[]{:S(2)}, u32[]{:S(2)}) collective-permute-start(f32[8,2048]{1,0:T(8,128)} %get-tuple-element.5), channel_id=1, source_target_pairs={{8,0},{16,8},{24,16},{32,24},{40,32},{48,40},{56,48},{64,56},{72,6... | collective-permute-start | bytes 196616 | tf_op jit(solution)/shard_map/ppermute | solution.py:527
  159.1 4.9 %collective-permute-done.7.arrived = f32[8,2048]{1,0:T(8,128)S(1)} collective-permute-done((f32[8,2048]{1,0:T(8,128)}, f32[8,2048]{1,0:T(8,128)S(1)}, u32[]{:S(2)}, u32[]{:S(2)}) %collective-permute-start.7) | collective-permute-done | bytes 65568 | tf_op jit(solution)/shard_map/ppermute | solution.py:527
  163.9 0.6 copy-done.3
  164.6 1.5 final_stage.1
  (21 shorter events, 0.1 us)
Async XLA Ops:
  13.8 20.3 %copy-start.2 = (f32[8,2560]{1,0:T(8,128)S(1)}, f32[8,2560]{1,0:T(8,128)}, u32[]{:S(2)}) copy-start(f32[8,2560]{1,0:T(8,128)} %gather_stage.1) | copy-start | bytes 245764
  13.8 21.9 %collective-permute-start = (f32[8,2560]{1,0:T(8,128)}, f32[8,2560]{1,0:T(8,128)S(1)}, u32[]{:S(2)}, u32[]{:S(2)}) collective-permute-start(f32[8,2560]{1,0:T(8,128)} %gather_stage.1), channel_id=1, source_target_pairs={{0,1},{1,2},{2,3},{3,4},{4,5},{5,6},{6,7},{7,0},{8,9},{9,10},{10,1... | collective-permute-start | bytes 245768 | tf_op jit(solution)/shard_map/ppermute | solution.py:505
  17.6 19.3 %collective-permute-start.1 = (f32[8,2560]{1,0:T(8,128)}, f32[8,2560]{1,0:T(8,128)S(1)}, u32[]{:S(2)}, u32[]{:S(2)}) collective-permute-start(f32[8,2560]{1,0:T(8,128)} %gather_stage.1), channel_id=1, source_target_pairs={{0,2},{1,3},{2,4},{3,5},{4,6},{5,7},{6,0},{7,1},{8,10},{9,11},{10,... | collective-permute-start | bytes 245768 | tf_op jit(solution)/shard_map/ppermute | solution.py:505
  18.8 19.1 %collective-permute-start.2 = (f32[8,2560]{1,0:T(8,128)}, f32[8,2560]{1,0:T(8,128)S(1)}, u32[]{:S(2)}, u32[]{:S(2)}) collective-permute-start(f32[8,2560]{1,0:T(8,128)} %gather_stage.1), channel_id=1, source_target_pairs={{0,3},{1,4},{2,5},{3,6},{4,7},{5,0},{6,1},{7,2},{8,11},{9,12},{10,... | collective-permute-start | bytes 245768 | tf_op jit(solution)/shard_map/ppermute | solution.py:505
  20.4 17.5 %collective-permute-start.3 = (f32[8,2560]{1,0:T(8,128)}, f32[8,2560]{1,0:T(8,128)S(1)}, u32[]{:S(2)}, u32[]{:S(2)}) collective-permute-start(f32[8,2560]{1,0:T(8,128)} %gather_stage.1), channel_id=1, source_target_pairs={{0,4},{1,5},{2,6},{3,7},{4,0},{5,1},{6,2},{7,3},{8,12},{9,13},{10,... | collective-permute-start | bytes 245768 | tf_op jit(solution)/shard_map/ppermute | solution.py:505
  22.1 15.8 %collective-permute-start.4 = (f32[8,2560]{1,0:T(8,128)}, f32[8,2560]{1,0:T(8,128)S(1)}, u32[]{:S(2)}, u32[]{:S(2)}) collective-permute-start(f32[8,2560]{1,0:T(8,128)} %gather_stage.1), channel_id=1, source_target_pairs={{0,5},{1,6},{2,7},{3,0},{4,1},{5,2},{6,3},{7,4},{8,13},{9,14},{10,... | collective-permute-start | bytes 245768 | tf_op jit(solution)/shard_map/ppermute | solution.py:505
  26.6 82.5 %all-to-all-start = ((f32[16,5,16,8,128]{4,3,2,1,0:T(8,128)}), f32[16,5,16,8,128]{4,3,2,1,0:T(8,128)}, u32[]{:S(2)}, u32[]{:S(2)}) async-start(f32[16,5,16,8,128]{4,3,2,1,0:T(8,128)} %z_stage.1.after), calls=%async_computation | async-start | bytes 10485760 | tf_op jit(solution)/shard_map/all_to_all | solution.py:495
  35.7 4.0 %collective-permute-start.5 = (f32[8,2560]{1,0:T(8,128)S(1)}, f32[8,2560]{1,0:T(8,128)S(1)}, u32[]{:S(2)}, u32[]{:S(2)}) collective-permute-start(f32[8,2560]{1,0:T(8,128)S(1)} %copy-done.2), channel_id=1, source_target_pairs={{0,6},{1,7},{2,0},{3,1},{4,2},{5,3},{6,4},{7,5},{8,14},{9,15},{10,... | collective-permute-start | bytes 245768 | tf_op jit(solution)/shard_map/ppermute | solution.py:505
  36.9 58.5 %collective-permute-start.6 = (f32[8,2560]{1,0:T(8,128)S(1)}, f32[8,2560]{1,0:T(8,128)S(1)}, u32[]{:S(2)}, u32[]{:S(2)}) collective-permute-start(f32[8,2560]{1,0:T(8,128)S(1)} %copy-done.2), channel_id=1, source_target_pairs={{0,7},{1,0},{2,1},{3,2},{4,3},{5,4},{6,5},{7,6},{8,15},{9,8},{10,9... | collective-permute-start | bytes 245768 | tf_op jit(solution)/shard_map/ppermute | solution.py:505
  95.4 0.9 copy-start
  138.9 12.9 %all-to-all-start.1 = ((f32[8,8,2560]{2,1,0:T(8,128)}), f32[8,8,2560]{2,1,0:T(8,128)S(1)}, u32[]{:S(2)}, u32[]{:S(2)}) async-start(f32[8,8,2560]{2,1,0:T(8,128)} %field_stage.1), calls=%async_computation.1 | async-start | bytes 1310720 | tf_op jit(solution)/shard_map/all_to_all | solution.py:523
  151.8 0.8 copy-start.1
  155.2 8.8 %collective-permute-start.7 = (f32[8,2048]{1,0:T(8,128)}, f32[8,2048]{1,0:T(8,128)S(1)}, u32[]{:S(2)}, u32[]{:S(2)}) collective-permute-start(f32[8,2048]{1,0:T(8,128)} %get-tuple-element.5), channel_id=1, source_target_pairs={{8,0},{16,8},{24,16},{32,24},{40,32},{48,40},{56,48},{64,56},{72,6... | collective-permute-start | bytes 196616 | tf_op jit(solution)/shard_map/ppermute | solution.py:527
  163.9 0.6 copy-start.3

commit v3 on v2

--- a/solution.py
+++ b/solution.py
@@ -89,18 +89,18 @@
     return lax.dot_general(a, b, dims, preferred_element_type=F32)
 
 
-def z_kernel(pieces, place, source, table, twiddle, out, even, odd):
+def z_kernel(pieces, source, table, twiddle, out, even, odd):
     quad = pl.program_id(0)
     with_extra = EXTRA in pieces
     parities = [p for p in range(2) if with_extra or any(c % 2 == p for c in pieces)]
     row = lax.broadcasted_iota(jnp.int32, (32, GRID), 0)
-    mode_y = signed(row + place[1] * 32)
+    mode_y = signed(row + lax.axis_index("gy") * 32)
     mode_z = signed(lax.broadcasted_iota(jnp.int32, (32, GRID), 1))
-    wave_z = WAVE * mode_z
+    half_wave_z = 0.5 * WAVE * mode_z
     partial_square = mode_y * mode_y + mode_z * mode_z
     turn_re, turn_im = twiddle[0], twiddle[1]
     for k in range(4):
-        index_x = place[0] * 16 + quad * 4 + k
+        index_x = lax.axis_index("gx") * 16 + quad * 4 + k
         mode_x = jnp.where(index_x < GRID // 2, index_x, index_x - GRID).astype(F32)
         inverse = 1.0 / jnp.maximum(mode_x * mode_x + partial_square, 1.0)
         v = []
@@ -112,10 +112,10 @@
             (v[0][0], v[1][0], k * 128),
             (v[0][1], v[1][1], k * 128 + 32),
             (v[0][2], v[1][2], k * 128 + 64),
-            (-wave_z * v[1][0], wave_z * v[0][0], k * 128 + 96),
+            (-half_wave_z * v[1][0], half_wave_z * v[0][0], k * 128 + 96),
         ]
         if with_extra:
-            rows.append((-wave_z * v[1][1], wave_z * v[0][1], 512 + k * 32))
+            rows.append((-half_wave_z * v[1][1], half_wave_z * v[0][1], 512 + k * 32))
         for real, imag, start in rows:
             here = slice(start, start + 32)
             for p in parities:
@@ -167,28 +167,23 @@
             out[:, place_of, 2 * k1 + 1] = q1.reshape(N_GX, 8, 128)
 
 
-def z_stage(pieces, place, source, table, twiddle):
+def z_stage(pieces, source, table, twiddle):
     def kernel(*refs):
         z_kernel(pieces, *refs)
 
     return pl.pallas_call(
         kernel,
         out_shape=jax.ShapeDtypeStruct((N_GX, len(pieces), 16, 8, 128), F32),
-        grid_spec=pltpu.PrefetchScalarGridSpec(
-            num_scalar_prefetch=1,
-            grid=(4,),
-            in_specs=[
-                pl.BlockSpec((2, 3, 4, 32, GRID), lambda i, _: (0, 0, i, 0, 0)),
-                pl.BlockSpec((256, 768), lambda i, _: (0, 0)),
-                pl.BlockSpec((2, 32, HALF), lambda i, _: (0, 0, 0)),
-            ],
-            out_specs=pl.BlockSpec(
-                (N_GX, len(pieces), 4, 8, 128), lambda i, _: (0, 0, i, 0, 0)
-            ),
-            scratch_shapes=[pltpu.VMEM((640, 768), BF16), pltpu.VMEM((640, 768), BF16)],
-        ),
+        grid=(4,),
+        in_specs=[
+            pl.BlockSpec((2, 3, 4, 32, GRID), lambda i: (0, 0, i, 0, 0)),
+            pl.BlockSpec((256, 768), lambda i: (0, 0)),
+            pl.BlockSpec((2, 32, HALF), lambda i: (0, 0, 0)),
+        ],
+        out_specs=pl.BlockSpec((N_GX, len(pieces), 4, 8, 128), lambda i: (0, 0, i, 0, 0)),
+        scratch_shapes=[pltpu.VMEM((640, 768), BF16), pltpu.VMEM((640, 768), BF16)],
         name="z_stage",
-    )(place, source, table, twiddle)
+    )(source, table, twiddle)
 
 
 def weight(distance, offset):
@@ -201,26 +196,25 @@
     return jnp.where(distance < 0.0, distance + GRID, distance)
 
 
-def gather_kernel(counts, after, start, offset, other_start, other_offset, out):
+def gather_kernel(counts, start, offset, other_start, other_offset, out):
     own, ghosts = counts[0, 0], counts[0, 2]
     out[0:3, :OWN] = start[...].astype(F32)
     out[3:6, :OWN] = offset[...]
-    out[0:3, OWN:] = other_start[...].astype(F32)
-    out[3:6, OWN:] = other_offset[...]
+    out[0:3, OWN:] = other_start[:, 1].astype(F32)
+    out[3:6, OWN:] = other_offset[:, 1]
     lane = lax.broadcasted_iota(jnp.int32, (1, ROWS), 1)
     bound = jnp.where(lane < OWN, own, OWN + ghosts)
     out[6:7, :] = jnp.where(lane < bound, 1.0, 0.0)
     out[7:8, :] = jnp.where(lane == 0, own, jnp.where(lane == 1, ghosts, 0)).astype(F32)
 
 
-def gather_stage(counts, after, start, offset, other_start, other_offset):
+def gather_stage(counts, start, offset, other_start, other_offset):
     vmem = pl.BlockSpec(memory_space=pltpu.VMEM)
     return pl.pallas_call(
         gather_kernel,
         out_shape=jax.ShapeDtypeStruct((8, ROWS), F32),
         in_specs=[
             pl.BlockSpec(memory_space=pltpu.SMEM),
-            pl.BlockSpec(memory_space=pl.ANY),
             vmem,
             vmem,
             vmem,
@@ -228,7 +222,7 @@
         ],
         out_specs=vmem,
         name="gather_stage",
-    )(counts, after, start, offset, other_start, other_offset)
+    )(counts, start, offset, other_start, other_offset)
 
 
 def for_live_blocks(place, owner, body):
@@ -278,11 +272,9 @@
 def field_kernel(
     steps, place, main, extra, t_even, t_odd, particles, phases_in, *rest
 ):
-    if len(rest) == 8:
-        previous, out, field, d_even, d_odd, window, phases, arrival = rest
-    else:
-        previous = None
-        out, field, d_even, d_odd, window, phases, arrival = rest
+    previous = rest[0] if len(rest) == 10 else None
+    out, field, work0, work1, work2, work3, window, phases, arrival = rest[-9:]
+    work = (work0, work1, work2, work3)
     first_c = steps[0]
     step_c = pl.program_id(0)
     c = first_c + step_c
@@ -296,18 +288,20 @@
     group = lane // 32
     row = lax.broadcasted_iota(jnp.int32, (HALF, 128), 0)
     wave_y = WAVE * signed(lane % 32 + place[1] * 32)
-    last_group = group == 3
-    on_left = jnp.where(group == 0, wave_y, 0.0)
-    on_right = jnp.where((group == 1) | last_group, 0.5 * wave_y, 0.0)
+    cross_y = jnp.where(group == 0, wave_y, jnp.where(group == 2, 0.0, 0.5 * wave_y))
     half_same = jnp.where((group == 1) | (group == 2), 0.5, 0.0)
-    half_left = jnp.where(group == 2, 0.5, 0.0)
-    half_extra = jnp.where(last_group, 0.5, 0.0)
+    plain_left = group == 2
+    plain_extra = group == 3
+    cross_left = group == 0
     flat_main = main.reshape(GRID * 8, 128)
     flat_extra = extra.reshape(GRID * 8, 128)
-
-    def one_z(step, carry):
-        for parity, target in ((0, d_even), (1, d_odd)):
-            wave_x = WAVE * signed(2 * row + parity)
+    waves = [WAVE * signed(2 * row + parity) for parity in range(2)]
+    for step in range(4):
+        results = []
+        for parity in range(2):
+            target = work[2 * (step % 2) + parity]
+            wave_x = waves[parity]
+            cross_x = half_same * wave_x
 
             def load(flat, q):
                 return flat[pl.ds(parity * 8 + q * 4 + step, HALF, stride=16), :]
@@ -316,30 +310,25 @@
             for q in range(2):
                 value = load(flat_main, q)
                 moved = pltpu.roll(load(flat_extra, q), 32 * (3 - c), 1)
-                parts.append((value, pltpu.roll(value, 96, 1), pltpu.roll(value, 32, 1), moved))
-            (a_re, l_re, r_re, e_re), (a_im, l_im, r_im, e_im) = parts
-            on_same = half_same * wave_x
-            first_re = jnp.where(last_group, -wave_x * l_im, a_re)
-            first_im = jnp.where(last_group, wave_x * l_re, a_im)
-            second_re = (half_left * l_re + half_extra * e_re) - (
-                on_left * l_im + on_right * r_im + on_same * a_im
-            )
-            second_im = (half_left * l_im + half_extra * e_im) + (
-                on_left * l_re + on_right * r_re + on_same * a_re
-            )
+                left = pltpu.roll(value, 96, 1)
+                right = pltpu.roll(value, 32, 1)
+                cross = cross_y * jnp.where(cross_left, left, right) + cross_x * value
+                plain = jnp.where(plain_left, left, jnp.where(plain_extra, moved, 0.0))
+                parts.append((value, wave_x * left, cross, plain))
+            (a_re, x_re, c_re, p_re), (a_im, x_im, c_im, p_im) = parts
             for top, left, value in (
-                (0, 0, first_re),
-                (HALF, 0, first_im),
-                (0, 128, second_re),
-                (HALF, 128, second_im),
+                (0, 0, jnp.where(plain_extra, -x_im, a_re)),
+                (HALF, 0, jnp.where(plain_extra, x_re, a_im)),
+                (0, 128, p_re - c_im),
+                (HALF, 128, p_im + c_re),
             ):
                 high, low = split(value)
                 lanes = slice(left, left + 128)
                 target[top : top + HALF, lanes] = high
                 target[GRID + top : GRID + top + HALF, lanes] = low
                 target[2 * GRID + top : 2 * GRID + top + HALF, lanes] = high
-        from_even = dot(t_even[...], d_even[...], NN)
-        from_odd = dot(t_odd[...], d_odd[...], NN)
+            results.append(dot((t_even, t_odd)[parity][...], target[...], NN))
+        from_even, from_odd = results
         near = (from_even + from_odd).astype(BF16)
         far = (from_even - from_odd).astype(BF16)
         z = step_c * 4 + step
@@ -348,9 +337,6 @@
             field[z, 0:HALF, lanes] = near[q * HALF : q * HALF + HALF]
             field[z, HALF:GRID, lanes] = far[q * HALF : q * HALF + HALF]
             field[z, GRID : GRID + 16, lanes] = near[q * HALF : q * HALF + 16]
-        return carry
-
-    lax.fori_loop(0, 4, one_z, 0)
 
     @pl.when(step_c == len(steps) - 1)
     def _():
@@ -365,7 +351,7 @@
         z_cell = (place[0] * 16 + first_c + 4 * (local_z % 4) + local_z // 4).astype(F32)
 
         def one_owner(index, carry):
-            owner = (place[1] - index) & (N_GY - 1)
+            owner = index
             block = field[:, pl.ds(pl.multiple_of(owner * 32, 16), WINDOW), :]
             window[...] = block.reshape(planes * WINDOW, 512).T
             base_x = (owner * 32).astype(F32)
@@ -426,6 +412,8 @@
                 pltpu.VMEM((planes, GRID + 16, 512), BF16),
                 pltpu.VMEM((768, 256), BF16),
                 pltpu.VMEM((768, 256), BF16),
+                pltpu.VMEM((768, 256), BF16),
+                pltpu.VMEM((768, 256), BF16),
                 pltpu.VMEM((512, planes * WINDOW), BF16),
                 pltpu.VMEM((N_GY, 64, ROWS), F32),
                 pltpu.SemaphoreType.DMA,
@@ -442,7 +430,7 @@
     own[...] = total[:, :OWN]
     ghosts = total[:, OWN:]
     cell = lax.broadcasted_iota(jnp.int32, (OWN, GHOST), 0)
-    chosen = (cell == slots[...]).astype(F32).astype(BF16)
+    chosen = (cell == slots[1:2]).astype(F32).astype(BF16)
     first, rest = split(ghosts)
     second, third = split(ghosts - first.astype(F32))
     parts = jnp.concatenate([first.astype(F32), second.astype(F32), third.astype(F32)], axis=0)
@@ -483,31 +471,24 @@
 ):
     index_gx = lax.axis_index("gx").astype(jnp.int32)
     index_gy = lax.axis_index("gy").astype(jnp.int32)
-    here = jnp.stack([index_gx, index_gy])
+    mine = gather_stage(counts, particle_start, particle_offset, ghost_start, ghost_offset)
+    copies = jnp.broadcast_to(mine[None], (N_GY, 8, ROWS))
+    particles = lax.all_to_all(copies, "gy", split_axis=0, concat_axis=0, tiled=True)
 
     table_z = jnp.asarray(left_triple(z_table()))
     twiddle = jnp.asarray(twiddles())
     sent = [
-        z_stage(chunk + ((EXTRA,) if number == 0 else ()), here, source_hat, table_z, twiddle)
+        z_stage(chunk + ((EXTRA,) if number == 0 else ()), source_hat, table_z, twiddle)
         for number, chunk in enumerate(CHUNKS)
     ]
     received = [
         lax.all_to_all(piece, "gx", split_axis=0, concat_axis=0, tiled=True) for piece in sent
     ]
 
-    mine = gather_stage(
-        counts, sent[0], particle_start, particle_offset, ghost_start[:, 1], ghost_offset[:, 1]
+    live_counts = particles[:, 7, 0:2].astype(jnp.int32)
+    place = jnp.concatenate(
+        [jnp.stack([index_gx, index_gy]), live_counts[:, 0], live_counts[:, 1]]
     )
-    members = range(N_GY)
-    particles = jnp.stack(
-        [mine]
-        + [
-            lax.ppermute(mine, "gy", [(i, (i + shift) % N_GY) for i in members])
-            for shift in range(1, N_GY)
-        ]
-    )
-    live_counts = particles[:, 7, 0:2].astype(jnp.int32)
-    place = jnp.concatenate([here, live_counts[:, 0], live_counts[:, 1]])
     table_y = jnp.asarray(left_triple(y_table()))
     table_y = lax.dynamic_index_in_dim(table_y, index_gy, 0, keepdims=False)
     phases = row_stage(place, particles, table_y)
@@ -521,7 +502,7 @@
             t_even, t_odd, particles, phases, partial,
         )
     partial = lax.all_to_all(partial, "gy", split_axis=0, concat_axis=0, tiled=True)
-    own, back = ghost_stage(partial, ghost_slot[1:2])
+    own, back = ghost_stage(partial, ghost_slot)
     devices = range(N_GX)
     route = [((i + 1) % N_GX, i) for i in devices]
     return final_stage(own, lax.ppermute(back, "gx", route))

time: 167 us -> 144 us (0.86)
  waiting for transfers between devices: 70.4 us -> 50.7 us
  blocking collectives: 0 us -> 16.9 us
  starting transfers between devices: 29.9 us -> 15.1 us
  local copies, waits for them, and re-layouts: 7.28 us -> 4.02 us
    ppermute x7 -> x0, waiting for transfers between devices: 57.4 us -> none  [per_device(): lax.ppermute(mine, 'gy', [(i, (i + shift) % N_GY) for i in members])]
    all_to_all x1, waiting for transfers between devices: 0.01 us -> 43.6 us  [per_device(): lax.all_to_all(piece, 'gx', split_axis=0, concat_axis=0, tiled=True)]
    all_to_all x0 -> x1, blocking collectives: none -> 16.9 us  [per_device(): lax.all_to_all(partial, 'gy', split_axis=0, concat_axis=0, tiled=True)]
    ppermute x7 -> x0, starting transfers between devices: 14.9 us -> none  [per_device(): lax.ppermute(mine, 'gy', [(i, (i + shift) % N_GY) for i in members])]
    all_to_all x1, waiting for transfers between devices: 8.1 us -> 4.09 us  [per_device(): lax.all_to_all(copies, 'gy', split_axis=0, concat_axis=0, tiled=True)]
    all_to_all x1, starting transfers between devices: 3.55 us -> 7.47 us  [per_device(): lax.all_to_all(copies, 'gy', split_axis=0, concat_axis=0, tiled=True)]
    ppermute x1, starting transfers between devices: 3.91 us -> 0.93 us  [per_device(): return final_stage(own, lax.ppermute(back, 'gx', route))]
    slice x3 -> x0, local copies, waits for them, and re-layouts: 2.77 us -> none  [the longest x1 1.28 us: per_device(): own, back = ghost_stage(partial, ghost_slot[1:2])]
  transfers between devices with their start and end apart: 10 -> 3, of which waited for: 4 -> 3; matrix products, arithmetic and copies ran while one was open for 2% -> 2% of each run, Pallas kernels for 8% -> 16%
where the time goes in v3:
time: 144 us
  Pallas kernels  55.7 us (39%)
  waiting for transfers between devices  50.7 us (35%)
  blocking collectives  16.9 us (12%)
  starting transfers between devices  15.1 us (10%)
  local copies, waits for them, and re-layouts  4.02 us (3%)
    all_to_all x1, waiting for transfers between devices, per_device(): lax.all_to_all(piece, 'gx', split_axis=0, concat_axis=0, tiled=True)  43.6 us
    pallas_call x1, Pallas kernels, field_stage(): pl.pallas_call(kernel, out_shape=jax.ShapeDtypeStruct((N_GY, 8, ROWS), F3...  27.6 us
    all_to_all x1, blocking collectives, per_device(): lax.all_to_all(partial, 'gy', split_axis=0, concat_axis=0, tiled=True)  16.9 us
    pallas_call x1, Pallas kernels, row_stage(): pl.pallas_call(row_kernel, out_shape=jax.ShapeDtypeStruct((N_GY, 64, ROWS...  14.9 us
    pallas_call x1, Pallas kernels, z_stage(): pl.pallas_call(kernel, out_shape=jax.ShapeDtypeStruct((N_GX, len(pieces),...  7.74 us
    all_to_all x1, starting transfers between devices, per_device(): lax.all_to_all(copies, 'gy', split_axis=0, concat_axis=0, tiled=True)  7.47 us
    all_to_all x1, starting transfers between devices, per_device(): lax.all_to_all(piece, 'gx', split_axis=0, concat_axis=0, tiled=True)  6.67 us
    all_to_all x1, waiting for transfers between devices, per_device(): lax.all_to_all(copies, 'gy', split_axis=0, concat_axis=0, tiled=True)  4.09 us
  transfers between devices with their start and end apart: 3, of which 3 were waited for; matrix products, arithmetic and copies ran while one was open for 2% of the time, Pallas kernels for 16%

profile of v3, /device:TPU:1, one launch (start us, length us, event | category | flops | bytes accessed | tf_op | source)
XLA Modules:
  0.0 143.6 jit_solution(4948083455443041589)
XLA Ops:
  0.6 1.5 %gather_stage.1 = f32[8,2560]{1,0:T(8,128)} custom-call(s32[1,4]{1,0:T(1,128)} %counts.1, s32[3,2048]{1,0:T(4,128)} %start.1, f32[3,2048]{1,0:T(4,128)} %offset.1, s32[3,3,512]{2,1,0:T(4,128)} %other_start.1, f32[3,3,512]{2,1,0:T(4,128)} %other_offset.1), custom_call_target="tpu_custom_call" | custom-call | tf_op jit(solution)/shard_map/gather_stage/pallas_call | solution.py:213
  2.1 1.8 %broadcast_in_dim.2 = f32[8,8,2560]{2,1,0:T(8,128)} broadcast(f32[8,2560]{1,0:T(8,128)} %gather_stage.1), dimensions={1,2} | broadcast | bytes 737280 | tf_op jit(solution)/shard_map/broadcast_in_dim | solution.py:475
  3.9 7.5 %all-to-all-start = ((f32[8,8,2560]{2,1,0:T(8,128)}), f32[8,8,2560]{2,1,0:T(8,128)S(1)}, u32[]{:S(2)}, u32[]{:S(2)}) async-start(f32[8,8,2560]{2,1,0:T(8,128)} %broadcast_in_dim.2), calls=%async_computation | async-start | bytes 1310720 | tf_op jit(solution)/shard_map/all_to_all | solution.py:476
  11.3 7.7 %z_stage.1 = f32[16,5,16,8,128]{4,3,2,1,0:T(8,128)} custom-call(f32[2,3,16,32,256]{4,3,2,1,0:T(8,128)} %refs_0_.1, bf16[256,768]{1,0:T(8,128)(2,1)} %constant.25.clone.refs_1_, f32[2,32,128]{2,1,0:T(8,128)} %constant.26.clone.refs_2_), custom_call_target="tpu_custom_call" | custom-call | tf_op jit(solution)/shard_map/z_stage/pallas_call | solution.py:174
  19.1 4.1 %all-to-all-done.particles.refs_5_ = f32[8,8,2560]{2,1,0:T(8,128)S(1)} async-done(((f32[8,8,2560]{2,1,0:T(8,128)}), f32[8,8,2560]{2,1,0:T(8,128)S(1)}, u32[]{:S(2)}, u32[]{:S(2)}) %all-to-all-start) | async-done | bytes 655392 | tf_op jit(solution)/shard_map/all_to_all | solution.py:476
  23.2 0.0 copy-start
  23.2 6.7 %all-to-all-start.1 = ((f32[16,5,16,8,128]{4,3,2,1,0:T(8,128)}), f32[16,5,16,8,128]{4,3,2,1,0:T(8,128)}, u32[]{:S(2)}, u32[]{:S(2)}) async-start(f32[16,5,16,8,128]{4,3,2,1,0:T(8,128)} %z_stage.1), calls=%async_computation.1 | async-start | bytes 10485760 | tf_op jit(solution)/shard_map/all_to_all | solution.py:485
  29.8 1.5 %dynamic-slice_bitcast_fusion.table = bf16[64,768]{1,0:T(8,128)(2,1)} fusion(bf16[8,64,768]{2,1,0:T(8,128)(2,1)} %constant.27.clone, s32[]{:T(128)S(6)} %select_n.4), kind=kLoop, calls=%fused_computation | loop fusion | bytes 196612 | tf_op jit(solution)/shard_map/jit(dynamic_index_in_dim)/squeeze | solution.py:493
  31.4 0.0 copy-done
  31.4 0.1 copy.15
  31.5 0.6 pad_add_fusion.place.refs_0_
  32.1 14.9 %row_stage.1.refs_6_ = f32[8,64,2560]{2,1,0:T(8,128)} custom-call(s32[18]{0:T(128)} %pad_add_fusion.place.refs_0_, f32[8,8,2560]{2,1,0:T(8,128)} %copy-done, bf16[64,768]{1,0:T(8,128)(2,1)} %dynamic-slice_bitcast_fusion.table), custom_call_target="tpu_custom_call" | custom-call | tf_op jit(solution)/shard_map/row_stage/pallas_call | solution.py:256
  47.0 43.6 %all-to-all-done.1.refs_1_.refs_2_ = f32[16,5,16,8,128]{4,3,2,1,0:T(8,128)} async-done(((f32[16,5,16,8,128]{4,3,2,1,0:T(8,128)}), f32[16,5,16,8,128]{4,3,2,1,0:T(8,128)}, u32[]{:S(2)}, u32[]{:S(2)}) %all-to-all-start.1) | async-done | bytes 5242912 | tf_op jit(solution)/shard_map/all_to_all | solution.py:485
  90.6 27.6 %field_stage.1 = f32[8,8,2560]{2,1,0:T(8,128)} custom-call(s32[18]{0:T(128)} %pad_add_fusion.place.refs_0_, f32[16,5,16,8,128]{4,3,2,1,0:T(8,128)} %all-to-all-done.1.refs_1_.refs_2_, f32[16,5,16,8,128]{4,3,2,1,0:T(8,128)} %all-to-all-done.1.refs_1_.refs_2_, bf16[256,768]{1,0:T(8,128)(2,1)} %constant.28.clone.refs_3_, ...), custom_call_target="tpu_custom_call" | custom-call | tf_op jit(solution)/shard_map/field_stage/pallas_call | solution.py:403
  118.2 16.9 %all_to_all.15.values = f32[8,8,2560]{2,1,0:T(8,128)} all-to-all(f32[8,8,2560]{2,1,0:T(8,128)} %field_stage.1), channel_id=1, replica_groups=mesh['gx'=16,'gy'=8] {'gy'}, dimensions={0} | all-to-all | bytes 1310720 | tf_op jit(solution)/shard_map/all_to_all | solution.py:504
  135.1 2.5 %ghost_stage.1 = (f32[8,2048]{1,0:T(8,128)}, f32[8,2048]{1,0:T(8,128)}) custom-call(f32[8,8,2560]{2,1,0:T(8,128)} %all_to_all.15.values, s32[3,512]{1,0:T(4,128)} %slots.1), custom_call_target="tpu_custom_call" | custom-call | tf_op jit(solution)/shard_map/ghost_stage/pallas_call | solution.py:442
  137.6 0.9 collective-permute-start
  138.5 3.0 %collective-permute-done.arrived = f32[8,2048]{1,0:T(8,128)S(1)} collective-permute-done((f32[8,2048]{1,0:T(8,128)}, f32[8,2048]{1,0:T(8,128)S(1)}, u32[]{:S(2)}, u32[]{:S(2)}) %collective-permute-start) | collective-permute-done | bytes 65568 | tf_op jit(solution)/shard_map/ppermute | solution.py:508
  141.5 0.0 copy-start.1
  141.5 0.6 copy-done.1
  142.1 1.5 %final_stage.1 = (f32[3,2048]{1,0:T(4,128)}, f32[5,2048]{1,0:T(8,128)}) custom-call(f32[8,2048]{1,0:T(8,128)} %get-tuple-element.4.own, f32[8,2048]{1,0:T(8,128)} %copy-done.1), custom_call_target="tpu_custom_call" | custom-call | tf_op jit(solution)/shard_map/final_stage/pallas_call | solution.py:459
  (2 shorter events, 0.0 us)
Async XLA Ops:
  3.9 19.3 %all-to-all-start = ((f32[8,8,2560]{2,1,0:T(8,128)}), f32[8,8,2560]{2,1,0:T(8,128)S(1)}, u32[]{:S(2)}, u32[]{:S(2)}) async-start(f32[8,8,2560]{2,1,0:T(8,128)} %broadcast_in_dim.2), calls=%async_computation | async-start | bytes 1310720 | tf_op jit(solution)/shard_map/all_to_all | solution.py:476
  23.2 8.2 %copy-start = (f32[8,8,2560]{2,1,0:T(8,128)}, f32[8,8,2560]{2,1,0:T(8,128)S(1)}, u32[]{:S(2)}) copy-start(f32[8,8,2560]{2,1,0:T(8,128)S(1)} %all-to-all-done.particles.refs_5_) | copy-start | bytes 1966084
  23.2 67.4 %all-to-all-start.1 = ((f32[16,5,16,8,128]{4,3,2,1,0:T(8,128)}), f32[16,5,16,8,128]{4,3,2,1,0:T(8,128)}, u32[]{:S(2)}, u32[]{:S(2)}) async-start(f32[16,5,16,8,128]{4,3,2,1,0:T(8,128)} %z_stage.1), calls=%async_computation.1 | async-start | bytes 10485760 | tf_op jit(solution)/shard_map/all_to_all | solution.py:485
  137.6 3.9 %collective-permute-start = (f32[8,2048]{1,0:T(8,128)}, f32[8,2048]{1,0:T(8,128)S(1)}, u32[]{:S(2)}, u32[]{:S(2)}) collective-permute-start(f32[8,2048]{1,0:T(8,128)} %get-tuple-element.5), channel_id=1, source_target_pairs={{8,0},{16,8},{24,16},{32,24},{40,32},{48,40},{56,48},{64,56},{72,6... | collective-permute-start | bytes 196616 | tf_op jit(solution)/shard_map/ppermute | solution.py:508
  141.5 0.6 copy-start.1

commit v4 on v3

--- a/solution.py
+++ b/solution.py
@@ -7,6 +7,7 @@
 from jax.experimental import pallas as pl
 from jax.experimental.pallas import tpu as pltpu
 from jax.sharding import PartitionSpec as P
+
 
 F32 = jnp.float32
 BF16 = jnp.bfloat16
@@ -23,6 +24,10 @@
 BLOCK = 256
 CHUNKS = ((0, 1, 2, 3),)
 EXTRA = 4
+BLOCKS = ROWS // BLOCK
+JOBS = N_GY * BLOCKS + 2
+HEAD = 3
+AHEAD = 8
 
 
 def numpy_halves(table):
@@ -225,64 +230,107 @@
     )(counts, start, offset, other_start, other_offset)
 
 
-def for_live_blocks(place, owner, body):
-    def own_block(index, carry):
-        body(pl.multiple_of(index * BLOCK, BLOCK))
-        return carry
-
-    def ghost_block(index, carry):
-        body(pl.multiple_of(OWN + index * BLOCK, BLOCK))
-        return carry
-
-    lax.fori_loop(0, (place[2 + owner] + BLOCK - 1) // BLOCK, own_block, 0)
-    lax.fori_loop(0, (place[10 + owner] + BLOCK - 1) // BLOCK, ghost_block, 0)
-
-
-def row_kernel(place, particles, table, phases):
+def row_kernel(place, particles, table, phases, planes, phase, plane, sent_phase, sent_plane):
     y_cell = lax.broadcasted_iota(jnp.int32, (GRID, BLOCK), 0).astype(F32)
-
-    def one_block(start):
-        data = particles[0, :, pl.ds(start, BLOCK)]
+    x_cell = lax.broadcasted_iota(jnp.int32, (WINDOW, BLOCK), 0).astype(F32)
+    local_z = lax.broadcasted_iota(jnp.int32, (16, BLOCK), 0)
+    z_cell = (place[0] * 16 + 4 * (local_z % 4) + local_z // 4).astype(F32)
+    jobs = 2 * ((place[2] + 1) // 2)
+
+    def copies(slot, job):
+        return (
+            pltpu.make_async_copy(phase.at[slot], phases.at[job], sent_phase.at[slot]),
+            pltpu.make_async_copy(plane.at[slot], planes.at[job], sent_plane.at[slot]),
+        )
+
+    def one_job(job, carry):
+        slot = job & 1
+
+        @pl.when(job >= 2)
+        def _():
+            for copy in copies(slot, job):
+                copy.wait()
+
+        entry, block = place[HEAD + job], place[HEAD + JOBS + job]
+        owner = place[HEAD + 2 * JOBS + job]
+        data = particles[entry, :, pl.ds(pl.multiple_of(block * BLOCK, BLOCK), BLOCK)]
         weight_y = weight(wrapped(y_cell - data[1:2]), data[4:5])
         high, low = split(weight_y)
-        phases[0, :, pl.ds(start, BLOCK)] = dot(
-            table[...], jnp.concatenate([high, low, high], axis=0), NN
-        )
-
-    for_live_blocks(place, pl.program_id(0), one_block)
+        phase[slot] = dot(table[...], jnp.concatenate([high, low, high], axis=0), NN)
+        weight_x = weight(x_cell + (owner * 32).astype(F32) - data[0:1], data[3:4])
+        weight_z = weight(wrapped(z_cell - data[2:3]), data[5:6]) * data[6:7]
+        for z in range(16):
+            plane[slot, z * WINDOW : (z + 1) * WINDOW] = (weight_x * weight_z[z : z + 1]).astype(
+                BF16
+            )
+        for copy in copies(slot, job):
+            copy.start()
+        return carry
+
+    lax.fori_loop(0, jobs, one_job, 0)
+    for slot in range(2):
+
+        @pl.when(jobs > slot)
+        def _():
+            for copy in copies(slot, 0):
+                copy.wait()
 
 
 def row_stage(place, particles, table):
     return pl.pallas_call(
         row_kernel,
-        out_shape=jax.ShapeDtypeStruct((N_GY, 64, ROWS), F32),
+        out_shape=(
+            jax.ShapeDtypeStruct((JOBS, 64, BLOCK), F32),
+            jax.ShapeDtypeStruct((JOBS, 16 * WINDOW, BLOCK), BF16),
+        ),
         grid_spec=pltpu.PrefetchScalarGridSpec(
             num_scalar_prefetch=1,
-            grid=(N_GY,),
+            grid=(1,),
             in_specs=[
-                pl.BlockSpec((1, 8, ROWS), lambda i, _: (i, 0, 0)),
+                pl.BlockSpec((N_GY, 8, ROWS), lambda i, _: (0, 0, 0)),
                 pl.BlockSpec((64, 768), lambda i, _: (0, 0)),
             ],
-            out_specs=pl.BlockSpec((1, 64, ROWS), lambda i, _: (i, 0, 0)),
+            out_specs=(pl.BlockSpec(memory_space=pl.ANY), pl.BlockSpec(memory_space=pl.ANY)),
+            scratch_shapes=[
+                pltpu.VMEM((2, 64, BLOCK), F32),
+                pltpu.VMEM((2, 16 * WINDOW, BLOCK), BF16),
+                pltpu.SemaphoreType.DMA((2,)),
+                pltpu.SemaphoreType.DMA((2,)),
+            ],
         ),
         name="row_stage",
     )(place, particles, table)
 
 
-def field_kernel(
-    steps, place, main, extra, t_even, t_odd, particles, phases_in, *rest
-):
-    previous = rest[0] if len(rest) == 10 else None
-    out, field, work0, work1, work2, work3, window, phases, arrival = rest[-9:]
+def field_kernel(steps, place, main, extra, t_even, t_odd, phases, planes, *rest):
+    previous = rest[0] if len(rest) == 11 else None
+    out, field, work0, work1, work2, work3, window, phase, plane, arrived = rest[-10:]
     work = (work0, work1, work2, work3)
     first_c = steps[0]
+    depth = 4 * len(steps)
     step_c = pl.program_id(0)
     c = first_c + step_c
-    copy = pltpu.make_async_copy(phases_in, phases, arrival)
-
-    @pl.when(step_c == 0)
-    def _():
-        copy.start()
+    pairs = (place[2] + 1) // 2
+
+    def copies(pair, base):
+        found = []
+        for side in range(2):
+            job, slot = 2 * pair + side, base + side
+            rows = pl.ds(first_c * 4 * WINDOW, depth * WINDOW)
+            found.append(
+                pltpu.make_async_copy(phases.at[job], phase.at[slot], arrived.at[0, slot])
+            )
+            found.append(
+                pltpu.make_async_copy(planes.at[job, rows], plane.at[slot], arrived.at[1, slot])
+            )
+        return found
+
+    for ahead in range(AHEAD - 1):
+
+        @pl.when((step_c == 0) & (pairs > ahead))
+        def _():
+            for copy in copies(ahead, 2 * ahead):
+                copy.start()
 
     lane = lax.broadcasted_iota(jnp.int32, (HALF, 128), 1)
     group = lane // 32
@@ -344,40 +392,38 @@
             out[...] = jnp.zeros_like(out)
         else:
             out[...] = previous[...]
-        copy.wait()
-        planes = 4 * len(steps)
-        x_cell = lax.broadcasted_iota(jnp.int32, (WINDOW, BLOCK), 0).astype(F32)
-        local_z = lax.broadcasted_iota(jnp.int32, (planes, BLOCK), 0)
-        z_cell = (place[0] * 16 + first_c + 4 * (local_z % 4) + local_z // 4).astype(F32)
-
-        def one_owner(index, carry):
-            owner = index
-            block = field[:, pl.ds(pl.multiple_of(owner * 32, 16), WINDOW), :]
-            window[...] = block.reshape(planes * WINDOW, 512).T
-            base_x = (owner * 32).astype(F32)
-
-            def one_block(start):
-                data = particles[index, :, pl.ds(start, BLOCK)]
-                weight_x = weight(x_cell + base_x - data[0:1], data[3:4])
-                weight_z = weight(wrapped(z_cell - data[2:3]), data[5:6]) * data[6:7]
-                plane = jnp.concatenate(
-                    [(weight_x * weight_z[z : z + 1]).astype(BF16) for z in range(planes)], axis=0
-                )
-                summed = dot(window[...], plane, NN).reshape(2, 8, 32, BLOCK)
-                phase = phases[index, :, pl.ds(start, BLOCK)]
-                product = summed[0] * phase[None, 0:32] + summed[1] * phase[None, 32:64]
+
+        for owner in range(N_GY):
+            block = field[:, owner * 32 : owner * 32 + WINDOW, :]
+            window[owner] = block.reshape(depth * WINDOW, 512).T
+
+        def one_pair(pair, carry):
+            base = 2 * (pair & (AHEAD - 1))
+            for copy in copies(pair, base):
+                copy.wait()
+
+            @pl.when(pair + AHEAD - 1 < pairs)
+            def _():
+                for copy in copies(pair + AHEAD - 1, 2 * ((pair + AHEAD - 1) & (AHEAD - 1))):
+                    copy.start()
+
+            for side in range(2):
+                job = 2 * pair + side
+                owner, block = place[HEAD + 2 * JOBS + job], place[HEAD + JOBS + job]
+                lanes = pl.ds(pl.multiple_of(block * BLOCK, BLOCK), BLOCK)
+                summed = dot(window[owner], plane[base + side], NN).reshape(2, 8, 32, BLOCK)
+                turn = phase[base + side]
+                product = summed[0] * turn[None, 0:32] + summed[1] * turn[None, 32:64]
                 value = jnp.sum(product, axis=1)
                 if previous is not None:
-                    value = value + out[owner, :, pl.ds(start, BLOCK)]
-                out[owner, :, pl.ds(start, BLOCK)] = value
-
-            for_live_blocks(place, index, one_block)
+                    value = value + previous[owner, :, lanes]
+                out[owner, :, lanes] = value
             return carry
 
-        lax.fori_loop(0, N_GY, one_owner, 0)
-
-
-def field_stage(steps, first, place, main, extra, extra_at, t_even, t_odd, particles, phases, previous):
+        lax.fori_loop(0, pairs, one_pair, 0)
+
+
+def field_stage(steps, first, place, main, extra, extra_at, t_even, t_odd, rows, previous):
     def whole(shape):
         return pl.BlockSpec(
             shape, lambda i, _: (0,) * len(shape), pipeline_mode=pl.Buffered(1)
@@ -392,14 +438,14 @@
         pl.BlockSpec(piece, lambda i, _: (0, extra_at, 0, 0, 0)),
         whole((256, 768)),
         whole((256, 768)),
-        whole((N_GY, 8, ROWS)),
+        pl.BlockSpec(memory_space=pl.ANY),
         pl.BlockSpec(memory_space=pl.ANY),
     ]
-    operands = [place, main, extra, t_even, t_odd, particles, phases]
+    operands = [place, main, extra, t_even, t_odd, *rows]
     if previous is not None:
         in_specs.append(whole((N_GY, 8, ROWS)))
         operands.append(previous)
-    planes = 4 * len(steps)
+    depth = 4 * len(steps)
     return pl.pallas_call(
         kernel,
         out_shape=jax.ShapeDtypeStruct((N_GY, 8, ROWS), F32),
@@ -409,14 +455,15 @@
             in_specs=in_specs,
             out_specs=whole((N_GY, 8, ROWS)),
             scratch_shapes=[
-                pltpu.VMEM((planes, GRID + 16, 512), BF16),
+                pltpu.VMEM((depth, GRID + 16, 512), BF16),
                 pltpu.VMEM((768, 256), BF16),
                 pltpu.VMEM((768, 256), BF16),
                 pltpu.VMEM((768, 256), BF16),
                 pltpu.VMEM((768, 256), BF16),
-                pltpu.VMEM((512, planes * WINDOW), BF16),
-                pltpu.VMEM((N_GY, 64, ROWS), F32),
-                pltpu.SemaphoreType.DMA,
+                pltpu.VMEM((N_GY, 512, depth * WINDOW), BF16),
+                pltpu.VMEM((2 * AHEAD, 64, BLOCK), F32),
+                pltpu.VMEM((2 * AHEAD, depth * WINDOW, BLOCK), BF16),
+                pltpu.SemaphoreType.DMA((2, 2 * AHEAD)),
             ],
         ),
         name="field_stage",
@@ -431,7 +478,7 @@
     ghosts = total[:, OWN:]
     cell = lax.broadcasted_iota(jnp.int32, (OWN, GHOST), 0)
     chosen = (cell == slots[1:2]).astype(F32).astype(BF16)
-    first, rest = split(ghosts)
+    first, _ = split(ghosts)
     second, third = split(ghosts - first.astype(F32))
     parts = jnp.concatenate([first.astype(F32), second.astype(F32), third.astype(F32)], axis=0)
     placed = dot(parts.astype(BF16), chosen, NT)
@@ -466,14 +513,34 @@
     )(own, arrived)
 
 
+def job_list(live, owners, index_gx, index_gy):
+    needed = (live + BLOCK - 1) // BLOCK
+    block = jnp.arange(BLOCKS, dtype=jnp.int32)[None, :]
+    own = OWN // BLOCK
+    valid = jnp.where(block < own, block < needed[:, 0:1], block - own < needed[:, 1:2])
+    valid = valid.reshape(-1).astype(jnp.int32)
+    item = jnp.arange(N_GY * BLOCKS, dtype=jnp.int32)
+    before = jnp.sum(jnp.where(item[None, :] < item[:, None], valid[None, :], 0), axis=1)
+    jobs = jnp.sum(valid)
+    wanted = jnp.minimum(jnp.arange(JOBS, dtype=jnp.int32), jobs - 1)
+    chosen = (before[None, :] == wanted[:, None]) & (valid[None, :] > 0)
+    found = jnp.sum(jnp.where(chosen, item[None, :], 0), axis=1)
+    entry = found // BLOCKS
+    at_entry = entry[:, None] == jnp.arange(N_GY, dtype=jnp.int32)[None, :]
+    owner = jnp.sum(jnp.where(at_entry, owners[None, :], 0), axis=1)
+    return jnp.concatenate(
+        [jnp.stack([index_gx, index_gy, jobs]), entry, found % BLOCKS, owner]
+    )
+
+
 def per_device(
     source_hat, particle_start, particle_offset, ghost_start, ghost_offset, ghost_slot, counts
 ):
     index_gx = lax.axis_index("gx").astype(jnp.int32)
     index_gy = lax.axis_index("gy").astype(jnp.int32)
+    members = range(N_GY)
     mine = gather_stage(counts, particle_start, particle_offset, ghost_start, ghost_offset)
-    copies = jnp.broadcast_to(mine[None], (N_GY, 8, ROWS))
-    particles = lax.all_to_all(copies, "gy", split_axis=0, concat_axis=0, tiled=True)
+    partner = lax.ppermute(mine, "gy", [(i, i ^ 1) for i in members])
 
     table_z = jnp.asarray(left_triple(z_table()))
     twiddle = jnp.asarray(twiddles())
@@ -482,16 +549,23 @@
         for number, chunk in enumerate(CHUNKS)
     ]
     received = [
-        lax.all_to_all(piece, "gx", split_axis=0, concat_axis=0, tiled=True) for piece in sent
+        lax.all_to_all(piece, "gx", split_axis=0, concat_axis=0, tiled=True)
+        for piece in sent
     ]
-
-    live_counts = particles[:, 7, 0:2].astype(jnp.int32)
-    place = jnp.concatenate(
-        [jnp.stack([index_gx, index_gy]), live_counts[:, 0], live_counts[:, 1]]
+    pair = jnp.stack([mine, partner])
+    pairs = [pair]
+    for shift in (2, 6, 4):
+        route = [(i, (i + shift) % N_GY) for i in members]
+        pairs.append(lax.ppermute(pair, "gy", route))
+    particles = jnp.concatenate(pairs, axis=0)
+    shifts = jnp.array([0, 0, 2, 2, 6, 6, 4, 4], jnp.int32)
+    owners = jnp.bitwise_xor(
+        (index_gy - shifts) & (N_GY - 1), jnp.arange(N_GY, dtype=jnp.int32) & 1
     )
+    place = job_list(particles[:, 7, 0:2].astype(jnp.int32), owners, index_gx, index_gy)
     table_y = jnp.asarray(left_triple(y_table()))
     table_y = lax.dynamic_index_in_dim(table_y, index_gy, 0, keepdims=False)
-    phases = row_stage(place, particles, table_y)
+    rows = row_stage(place, particles, table_y)
 
     t_even = jnp.asarray(left_triple(x_table(0)))
     t_odd = jnp.asarray(left_triple(x_table(1)))
@@ -499,7 +573,7 @@
     for number, chunk in enumerate(CHUNKS):
         partial = field_stage(
             chunk, 0, place, received[number], received[0], len(CHUNKS[0]),
-            t_even, t_odd, particles, phases, partial,
+            t_even, t_odd, rows, partial,
         )
     partial = lax.all_to_all(partial, "gy", split_axis=0, concat_axis=0, tiled=True)
     own, back = ghost_stage(partial, ghost_slot)

time: 144 us -> 132 us (0.917)
  waiting for transfers between devices: 50.7 us -> 36.6 us
  starting transfers between devices: 15.1 us -> 17.6 us
    all_to_all x1, waiting for transfers between devices: 43.6 us -> 26.3 us  [per_device(): lax.all_to_all(piece, 'gx', split_axis=0, concat_axis=0, tiled=True)]
    ppermute x0 -> x4, starting transfers between devices: none -> 8.02 us  [the longest x3 4.29 us: per_device(): pairs.append(lax.ppermute(pair, 'gy', route))]
    all_to_all x1 -> x0, starting transfers between devices: 7.47 us -> none  [per_device(): lax.all_to_all(copies, 'gy', split_axis=0, concat_axis=0, tiled=True)]
    ppermute x0 -> x4, waiting for transfers between devices: none -> 6.62 us  [the longest x3 6.62 us: per_device(): pairs.append(lax.ppermute(pair, 'gy', route))]
    pallas_call x1, Pallas kernels: 27.6 us -> 23.2 us  [field_stage(): pl.pallas_call(kernel, out_shape=jax.ShapeDtypeStruct((N_GY, 8, ROWS), F3...]
    all_to_all x1 -> x0, waiting for transfers between devices: 4.09 us -> none  [per_device(): lax.all_to_all(copies, 'gy', split_axis=0, concat_axis=0, tiled=True)]
    pallas_call x1, Pallas kernels: 14.9 us -> 18.6 us  [row_stage(): pl.pallas_call(row_kernel, out_shape=(jax.ShapeDtypeStruct((JOBS, 64, BLO...]
    ppermute x1, starting transfers between devices: 0.93 us -> 3.08 us  [per_device(): return final_stage(own, lax.ppermute(back, 'gx', route))]
  transfers between devices with their start and end apart: 3 -> 6, of which waited for: 3 -> 4; matrix products, arithmetic and copies ran while one was open for 2% -> 3% of each run, Pallas kernels for 16% -> 20%
where the time goes in v4:
time: 132 us
  Pallas kernels  55.1 us (42%)
  waiting for transfers between devices  36.6 us (28%)
  starting transfers between devices  17.6 us (13%)
  blocking collectives  16.1 us (12%)
  local copies, waits for them, and re-layouts  3.66 us (3%)
  between operations  1.39 us (1%)
    all_to_all x1, waiting for transfers between devices, per_device(): lax.all_to_all(piece, 'gx', split_axis=0, concat_axis=0, tiled=True)  26.3 us
    pallas_call x1, Pallas kernels, field_stage(): pl.pallas_call(kernel, out_shape=jax.ShapeDtypeStruct((N_GY, 8, ROWS), F3...  23.2 us
    pallas_call x1, Pallas kernels, row_stage(): pl.pallas_call(row_kernel, out_shape=(jax.ShapeDtypeStruct((JOBS, 64, BLO...  18.6 us
    all_to_all x1, blocking collectives, per_device(): lax.all_to_all(partial, 'gy', split_axis=0, concat_axis=0, tiled=True)  16.1 us
    pallas_call x1, Pallas kernels, z_stage(): pl.pallas_call(kernel, out_shape=jax.ShapeDtypeStruct((N_GX, len(pieces),...  7.73 us
    ppermute x3, waiting for transfers between devices, per_device(): pairs.append(lax.ppermute(pair, 'gy', route))  6.62 us
    all_to_all x1, starting transfers between devices, per_device(): lax.all_to_all(piece, 'gx', split_axis=0, concat_axis=0, tiled=True)  6.53 us
    ppermute x3, starting transfers between devices, per_device(): pairs.append(lax.ppermute(pair, 'gy', route))  4.29 us
  transfers between devices with their start and end apart: 6, of which 4 were waited for; matrix products, arithmetic and copies ran while one was open for 3% of the time, Pallas kernels for 20%

profile of v4, /device:TPU:1, one launch (start us, length us, event | category | flops | bytes accessed | tf_op | source)
XLA Modules:
  0.0 131.6 jit_solution(4656900223059256473)
XLA Ops:
  0.6 1.5 %gather_stage.1 = f32[8,2560]{1,0:T(8,128)} custom-call(s32[1,4]{1,0:T(1,128)} %counts.1, s32[3,2048]{1,0:T(4,128)} %start.1, f32[3,2048]{1,0:T(4,128)} %offset.1, s32[3,3,512]{2,1,0:T(4,128)} %other_start.1, f32[3,3,512]{2,1,0:T(4,128)} %other_offset.1), custom_call_target="tpu_custom_call" | custom-call | tf_op jit(solution)/shard_map/gather_stage/pallas_call | solution.py:218
  2.1 3.7 %collective-permute-start = (f32[8,2560]{1,0:T(8,128)}, f32[8,2560]{1,0:T(8,128)S(1)}, u32[]{:S(2)}, u32[]{:S(2)}) collective-permute-start(f32[8,2560]{1,0:T(8,128)} %gather_stage.1), channel_id=1, source_target_pairs={{0,1},{1,0},{2,3},{3,2},{4,5},{5,4},{6,7},{7,6},{8,9},{9,8},{10,11... | collective-permute-start | bytes 245768 | tf_op jit(solution)/shard_map/ppermute | solution.py:543
  5.8 7.7 %z_stage.1 = f32[16,5,16,8,128]{4,3,2,1,0:T(8,128)} custom-call(f32[2,3,16,32,256]{4,3,2,1,0:T(8,128)} %refs_0_.1, bf16[256,768]{1,0:T(8,128)(2,1)} %constant.72.clone.refs_1_, f32[2,32,128]{2,1,0:T(8,128)} %constant.73.clone.refs_2_), custom_call_target="tpu_custom_call" | custom-call | tf_op jit(solution)/shard_map/z_stage/pallas_call | solution.py:179
  13.6 6.5 %all-to-all-start = ((f32[16,5,16,8,128]{4,3,2,1,0:T(8,128)}), f32[16,5,16,8,128]{4,3,2,1,0:T(8,128)}, u32[]{:S(2)}, u32[]{:S(2)}) async-start(f32[16,5,16,8,128]{4,3,2,1,0:T(8,128)} %z_stage.1), calls=%async_computation | async-start | bytes 10485760 | tf_op jit(solution)/shard_map/all_to_all | solution.py:552
  20.1 0.0 copy-done.3
  20.1 1.5 %dynamic-slice_bitcast_fusion.table = bf16[64,768]{1,0:T(8,128)(2,1)} fusion(bf16[8,64,768]{2,1,0:T(8,128)(2,1)} %constant.75.clone, s32[]{:T(128)S(6)} %select_n.58), kind=kLoop, calls=%fused_computation.1 | loop fusion | bytes 196612 | tf_op jit(solution)/shard_map/jit(dynamic_index_in_dim)/squeeze | solution.py:567
  21.7 0.0 copy-done.1
  21.7 0.0 collective-permute-done
  21.7 2.8 %collective-permute-start.3 = (f32[2,8,2560]{2,1,0:T(8,128)S(1)}, f32[2,8,2560]{2,1,0:T(8,128)S(1)}, u32[]{:S(2)}, u32[]{:S(2)}) collective-permute-start(f32[2,8,2560]{2,1,0:T(8,128)S(1)} %pad_maximum_fusion), channel_id=1, source_target_pairs={{0,4},{1,5},{2,6},{3,7},{4,0},{5,1},{6,2},{7,3},{8,12},{9,13},{10,... | collective-permute-start | bytes 491528 | tf_op jit(solution)/shard_map/ppermute | solution.py:559
  24.6 0.9 collective-permute-start.2
  25.4 0.6 collective-permute-start.1
  26.0 6.6 %collective-permute-done.1 = f32[2,8,2560]{2,1,0:T(8,128)S(1)} collective-permute-done((f32[2,8,2560]{2,1,0:T(8,128)S(1)}, f32[2,8,2560]{2,1,0:T(8,128)S(1)}, u32[]{:S(2)}, u32[]{:S(2)}) %collective-permute-start.1) | collective-permute-done | bytes 163872 | tf_op jit(solution)/shard_map/ppermute | solution.py:559
  32.6 0.1 collective-permute-done.2
  32.7 0.0 collective-permute-done.3
  32.7 0.0 copy-start
  32.7 0.1 copy.17
  32.8 0.1 fusion.2
  32.9 0.1 reshape.85
  33.0 0.7 fusion.4
  34.3 0.1 select_reduce_fusion.1
  34.5 0.1 select_reduce_fusion
  34.6 0.1 select_reduce_fusion.2
  34.7 1.3 concatenate.8.place.refs_0_
  36.0 18.6 %row_stage.1 = (f32[82,64,256]{2,1,0:T(8,128)}, bf16[82,768,256]{2,1,0:T(8,128)(2,1)}) custom-call(s32[249]{0:T(256)} %concatenate.8.place.refs_0_, f32[8,8,2560]{2,1,0:T(8,128)} %copy-done, bf16[64,768]{1,0:T(8,128)(2,1)} %dynamic-slice_bitcast_fusion.table), custom_call_target="tpu_custom_call" | custom-call | tf_op jit(solution)/shard_map/row_stage/pallas_call | solution.py:280
  54.6 26.3 %all-to-all-done.refs_1_.refs_2_ = f32[16,5,16,8,128]{4,3,2,1,0:T(8,128)} async-done(((f32[16,5,16,8,128]{4,3,2,1,0:T(8,128)}), f32[16,5,16,8,128]{4,3,2,1,0:T(8,128)}, u32[]{:S(2)}, u32[]{:S(2)}) %all-to-all-start) | async-done | bytes 5242912 | tf_op jit(solution)/shard_map/all_to_all | solution.py:552
  80.9 23.2 %field_stage.1 = f32[8,8,2560]{2,1,0:T(8,128)} custom-call(s32[249]{0:T(256)} %concatenate.8.place.refs_0_, f32[16,5,16,8,128]{4,3,2,1,0:T(8,128)} %all-to-all-done.refs_1_.refs_2_, f32[16,5,16,8,128]{4,3,2,1,0:T(8,128)} %all-to-all-done.refs_1_.refs_2_, bf16[256,768]{1,0:T(8,128)(2,1)} %constant.76.clone.refs_3_, bf16[256,768]{1,0:T(8,128)(2,1)} %constant.77.clone.refs_4_, ...), custom_call_target="tpu_custom_call" | custom-call | tf_op jit(solution)/shard_map/field_stage/pallas_call | solution.py:449
  104.1 16.1 %all_to_all.10.values = f32[8,8,2560]{2,1,0:T(8,128)} all-to-all(f32[8,8,2560]{2,1,0:T(8,128)} %field_stage.1), channel_id=1, replica_groups=mesh['gx'=16,'gy'=8] {'gy'}, dimensions={0} | all-to-all | bytes 1310720 | tf_op jit(solution)/shard_map/all_to_all | solution.py:578
  120.2 2.5 %ghost_stage.1 = (f32[8,2048]{1,0:T(8,128)}, f32[8,2048]{1,0:T(8,128)}) custom-call(f32[8,8,2560]{2,1,0:T(8,128)} %all_to_all.10.values, s32[3,512]{1,0:T(4,128)} %slots.1), custom_call_target="tpu_custom_call" | custom-call | tf_op jit(solution)/shard_map/ghost_stage/pallas_call | solution.py:489
  122.7 3.1 %collective-permute-start.4 = (f32[8,2048]{1,0:T(8,128)}, f32[8,2048]{1,0:T(8,128)S(1)}, u32[]{:S(2)}, u32[]{:S(2)}) collective-permute-start(f32[8,2048]{1,0:T(8,128)} %get-tuple-element.9), channel_id=1, source_target_pairs={{8,0},{16,8},{24,16},{32,24},{40,32},{48,40},{56,48},{64,56},{72,6... | collective-permute-start | bytes 196616 | tf_op jit(solution)/shard_map/ppermute | solution.py:582
  125.8 3.7 %collective-permute-done.4.arrived = f32[8,2048]{1,0:T(8,128)S(1)} collective-permute-done((f32[8,2048]{1,0:T(8,128)}, f32[8,2048]{1,0:T(8,128)S(1)}, u32[]{:S(2)}, u32[]{:S(2)}) %collective-permute-start.4) | collective-permute-done | bytes 65568 | tf_op jit(solution)/shard_map/ppermute | solution.py:582
  129.5 0.6 copy-done.2
  130.1 1.5 %final_stage.1 = (f32[3,2048]{1,0:T(4,128)}, f32[5,2048]{1,0:T(8,128)}) custom-call(f32[8,2048]{1,0:T(8,128)} %get-tuple-element.8.own, f32[8,2048]{1,0:T(8,128)} %copy-done.2), custom_call_target="tpu_custom_call" | custom-call | tf_op jit(solution)/shard_map/final_stage/pallas_call | solution.py:506
  (19 shorter events, 0.1 us)
Async XLA Ops:
  2.1 19.6 %collective-permute-start = (f32[8,2560]{1,0:T(8,128)}, f32[8,2560]{1,0:T(8,128)S(1)}, u32[]{:S(2)}, u32[]{:S(2)}) collective-permute-start(f32[8,2560]{1,0:T(8,128)} %gather_stage.1), channel_id=1, source_target_pairs={{0,1},{1,0},{2,3},{3,2},{4,5},{5,4},{6,7},{7,6},{8,9},{9,8},{10,11... | collective-permute-start | bytes 245768 | tf_op jit(solution)/shard_map/ppermute | solution.py:543
  13.6 6.5 %copy-start.3 = (s32[8]{0:T(128)S(1)}, s32[8]{0:T(128)}, u32[]{:S(2)}) copy-start(s32[8]{0:T(128)} %constant.79) | copy-start | bytes 100
  13.6 8.1 %copy-start.1 = (f32[8,2560]{1,0:T(8,128)S(1)}, f32[8,2560]{1,0:T(8,128)}, u32[]{:S(2)}) copy-start(f32[8,2560]{1,0:T(8,128)} %gather_stage.1) | copy-start | bytes 245764
  13.6 67.3 %all-to-all-start = ((f32[16,5,16,8,128]{4,3,2,1,0:T(8,128)}), f32[16,5,16,8,128]{4,3,2,1,0:T(8,128)}, u32[]{:S(2)}, u32[]{:S(2)}) async-start(f32[16,5,16,8,128]{4,3,2,1,0:T(8,128)} %z_stage.1), calls=%async_computation | async-start | bytes 10485760 | tf_op jit(solution)/shard_map/all_to_all | solution.py:552
  21.7 10.9 %collective-permute-start.3 = (f32[2,8,2560]{2,1,0:T(8,128)S(1)}, f32[2,8,2560]{2,1,0:T(8,128)S(1)}, u32[]{:S(2)}, u32[]{:S(2)}) collective-permute-start(f32[2,8,2560]{2,1,0:T(8,128)S(1)} %pad_maximum_fusion), channel_id=1, source_target_pairs={{0,4},{1,5},{2,6},{3,7},{4,0},{5,1},{6,2},{7,3},{8,12},{9,13},{10,... | collective-permute-start | bytes 491528 | tf_op jit(solution)/shard_map/ppermute | solution.py:559
  24.6 8.1 %collective-permute-start.2 = (f32[2,8,2560]{2,1,0:T(8,128)S(1)}, f32[2,8,2560]{2,1,0:T(8,128)S(1)}, u32[]{:S(2)}, u32[]{:S(2)}) collective-permute-start(f32[2,8,2560]{2,1,0:T(8,128)S(1)} %pad_maximum_fusion), channel_id=1, source_target_pairs={{0,6},{1,7},{2,0},{3,1},{4,2},{5,3},{6,4},{7,5},{8,14},{9,15},{10,... | collective-permute-start | bytes 491528 | tf_op jit(solution)/shard_map/ppermute | solution.py:559
  25.4 7.2 %collective-permute-start.1 = (f32[2,8,2560]{2,1,0:T(8,128)S(1)}, f32[2,8,2560]{2,1,0:T(8,128)S(1)}, u32[]{:S(2)}, u32[]{:S(2)}) collective-permute-start(f32[2,8,2560]{2,1,0:T(8,128)S(1)} %pad_maximum_fusion), channel_id=1, source_target_pairs={{0,2},{1,3},{2,4},{3,5},{4,6},{5,7},{6,0},{7,1},{8,10},{9,11},{10,... | collective-permute-start | bytes 491528 | tf_op jit(solution)/shard_map/ppermute | solution.py:559
  32.7 3.2 %copy-start = (f32[8,8,2560]{2,1,0:T(8,128)}, f32[8,8,2560]{2,1,0:T(8,128)S(1)}, u32[]{:S(2)}) copy-start(f32[8,8,2560]{2,1,0:T(8,128)S(1)} %constant_dynamic-update-slice_fusion.particles) | copy-start | bytes 1966084
  122.7 6.8 %collective-permute-start.4 = (f32[8,2048]{1,0:T(8,128)}, f32[8,2048]{1,0:T(8,128)S(1)}, u32[]{:S(2)}, u32[]{:S(2)}) collective-permute-start(f32[8,2048]{1,0:T(8,128)} %get-tuple-element.9), channel_id=1, source_target_pairs={{8,0},{16,8},{24,16},{32,24},{40,32},{48,40},{56,48},{64,56},{72,6... | collective-permute-start | bytes 196616 | tf_op jit(solution)/shard_map/ppermute | solution.py:582
  129.5 0.6 copy-start.2

commit v5 on v4

--- a/solution.py
+++ b/solution.py
@@ -104,7 +104,8 @@
     half_wave_z = 0.5 * WAVE * mode_z
     partial_square = mode_y * mode_y + mode_z * mode_z
     turn_re, turn_im = twiddle[0], twiddle[1]
-    for k in range(4):
+
+    def build(k):
         index_x = lax.axis_index("gx") * 16 + quad * 4 + k
         mode_x = jnp.where(index_x < GRID // 2, index_x, index_x - GRID).astype(F32)
         inverse = 1.0 / jnp.maximum(mode_x * mode_x + partial_square, 1.0)
@@ -140,22 +141,27 @@
                     target[here, GRID + r * HALF : GRID + (r + 1) * HALF] = low
                     target[here, 2 * GRID + r * HALF : 2 * GRID + (r + 1) * HALF] = high
 
-    for p in parities:
-        data = (even, odd)[p]
-        wanted = [c for c in pieces if c != EXTRA and c % 2 == p]
-        if not wanted:
-            continue
-        c_low, c_high = min(wanted) // 2, max(wanted) // 2 + 1
-        for pair in range(2):
-            result = dot(
-                table[c_low * 128 : c_high * 128], data[pair * 256 : pair * 256 + 256], NT
-            )
+    def transform(pair):
+        for p in parities:
+            wanted = [c for c in pieces if c != EXTRA and c % 2 == p]
+            if not wanted:
+                continue
+            c_low, c_high = min(wanted) // 2, max(wanted) // 2 + 1
+            data = (even, odd)[p][pair * 256 : pair * 256 + 256]
+            result = dot(table[c_low * 128 : c_high * 128], data, NT)
             for c in wanted:
                 top = (c // 2 - c_low) * 128
                 for side in range(2):
-                    out[:, pieces.index(c), pair * 2 + side] = result[
+                    out[:, pieces.index(c), side, pair] = result[
                         top : top + 128, side * 128 : side * 128 + 128
                     ].reshape(N_GX, 8, 128)
+
+    build(0)
+    build(1)
+    transform(0)
+    build(2)
+    build(3)
+    transform(1)
     if with_extra:
         halves = [dot(table[...], data[512:640], NT) for data in (even, odd)]
         v = [halves[c % 2][(c // 2) * 128 : (c // 2) * 128 + 128] for c in range(4)]
@@ -168,8 +174,8 @@
         for k1, p in ((0, p0), (1, p1)):
             q0 = jnp.where(lower32, p[0], pltpu.roll(p[1], 32, 1))
             q1 = jnp.where(lower32, pltpu.roll(p[0], 96, 1), p[1])
-            out[:, place_of, 2 * k1] = q0.reshape(N_GX, 8, 128)
-            out[:, place_of, 2 * k1 + 1] = q1.reshape(N_GX, 8, 128)
+            out[:, place_of, 0, k1] = q0.reshape(N_GX, 8, 128)
+            out[:, place_of, 1, k1] = q1.reshape(N_GX, 8, 128)
 
 
 def z_stage(pieces, source, table, twiddle):
@@ -178,14 +184,16 @@
 
     return pl.pallas_call(
         kernel,
-        out_shape=jax.ShapeDtypeStruct((N_GX, len(pieces), 16, 8, 128), F32),
+        out_shape=jax.ShapeDtypeStruct((N_GX, len(pieces), 2, 8, 8, 128), F32),
         grid=(4,),
         in_specs=[
             pl.BlockSpec((2, 3, 4, 32, GRID), lambda i: (0, 0, i, 0, 0)),
             pl.BlockSpec((256, 768), lambda i: (0, 0)),
             pl.BlockSpec((2, 32, HALF), lambda i: (0, 0, 0)),
         ],
-        out_specs=pl.BlockSpec((N_GX, len(pieces), 4, 8, 128), lambda i: (0, 0, i, 0, 0)),
+        out_specs=pl.BlockSpec(
+            (N_GX, len(pieces), 2, 2, 8, 128), lambda i: (0, 0, 0, i, 0, 0)
+        ),
         scratch_shapes=[pltpu.VMEM((640, 768), BF16), pltpu.VMEM((640, 768), BF16)],
         name="z_stage",
     )(source, table, twiddle)
@@ -201,16 +209,19 @@
     return jnp.where(distance < 0.0, distance + GRID, distance)
 
 
-def gather_kernel(counts, start, offset, other_start, other_offset, out):
+def gather_kernel(counts, start, offset, other_start, other_offset, out, packed):
     own, ghosts = counts[0, 0], counts[0, 2]
-    out[0:3, :OWN] = start[...].astype(F32)
-    out[3:6, :OWN] = offset[...]
-    out[0:3, OWN:] = other_start[:, 1].astype(F32)
-    out[3:6, OWN:] = other_offset[:, 1]
-    lane = lax.broadcasted_iota(jnp.int32, (1, ROWS), 1)
-    bound = jnp.where(lane < OWN, own, OWN + ghosts)
-    out[6:7, :] = jnp.where(lane < bound, 1.0, 0.0)
-    out[7:8, :] = jnp.where(lane == 0, own, jnp.where(lane == 1, ghosts, 0)).astype(F32)
+    lane = lax.broadcasted_iota(jnp.int32, (8, ROWS), 1)
+    packed[...] = jnp.zeros_like(packed)
+    packed[0:3, :GHOST] = other_start[:, 1].astype(F32)
+    packed[3:6, :GHOST] = other_offset[:, 1]
+    moved = pltpu.roll(packed[...], own, 1)
+    packed[0:3, :OWN] = start[...].astype(F32)
+    packed[3:6, :OWN] = offset[...]
+    out[...] = jnp.where(lane < own, packed[...], moved)
+    lane = lane[0:1]
+    out[6:7, :] = jnp.where(lane < own + ghosts, 1.0, 0.0)
+    out[7:8, :] = jnp.where(lane == 0, own + ghosts, 0).astype(F32)
 
 
 def gather_stage(counts, start, offset, other_start, other_offset):
@@ -226,6 +237,7 @@
             vmem,
         ],
         out_specs=vmem,
+        scratch_shapes=[pltpu.VMEM((8, ROWS), F32)],
         name="gather_stage",
     )(counts, start, offset, other_start, other_offset)
 
@@ -352,7 +364,10 @@
             cross_x = half_same * wave_x
 
             def load(flat, q):
-                return flat[pl.ds(parity * 8 + q * 4 + step, HALF, stride=16), :]
+                top = parity * 64 + q * 4 + step
+                return jnp.concatenate(
+                    [flat[pl.ds(source * 128 + top, 8, stride=8), :] for source in range(N_GX)]
+                )
 
             parts = []
             for q in range(2):
@@ -432,10 +447,10 @@
     def kernel(*refs):
         field_kernel(steps, *refs)
 
-    piece = (N_GX, None, 16, 8, 128)
+    piece = (N_GX, None, 2, 8, 8, 128)
     in_specs = [
-        pl.BlockSpec(piece, lambda i, _: (0, first + i, 0, 0, 0)),
-        pl.BlockSpec(piece, lambda i, _: (0, extra_at, 0, 0, 0)),
+        pl.BlockSpec(piece, lambda i, _: (0, first + i, 0, 0, 0, 0)),
+        pl.BlockSpec(piece, lambda i, _: (0, extra_at, 0, 0, 0, 0)),
         whole((256, 768)),
         whole((256, 768)),
         pl.BlockSpec(memory_space=pl.ANY),
@@ -470,12 +485,13 @@
     )(*operands)
 
 
-def ghost_kernel(values, slots, own, back):
+def ghost_kernel(counts, values, slots, own, back):
     total = values[0]
     for source in range(1, N_GY):
         total = total + values[source]
-    own[...] = total[:, :OWN]
-    ghosts = total[:, OWN:]
+    lane = lax.broadcasted_iota(jnp.int32, (8, OWN), 1)
+    own[...] = jnp.where(lane < counts[0, 0], total[:, :OWN], 0.0)
+    ghosts = pltpu.roll(total, ROWS - counts[0, 0], 1)[:, :GHOST]
     cell = lax.broadcasted_iota(jnp.int32, (OWN, GHOST), 0)
     chosen = (cell == slots[1:2]).astype(F32).astype(BF16)
     first, _ = split(ghosts)
@@ -485,39 +501,23 @@
     back[...] = placed[0:8] + (placed[8:16] + placed[16:24])
 
 
-def ghost_stage(values, slots):
+def ghost_stage(counts, values, slots):
+    vmem = pl.BlockSpec(memory_space=pltpu.VMEM)
     return pl.pallas_call(
         ghost_kernel,
         out_shape=(
             jax.ShapeDtypeStruct((8, OWN), F32),
             jax.ShapeDtypeStruct((8, OWN), F32),
         ),
+        in_specs=[pl.BlockSpec(memory_space=pltpu.SMEM), vmem, vmem],
+        out_specs=(vmem, vmem),
         name="ghost_stage",
-    )(values, slots)
-
-
-def final_kernel(own, arrived, velocity, strain):
-    total = own[...] + arrived[...]
-    velocity[...] = total[:3]
-    strain[...] = total[3:]
-
-
-def final_stage(own, arrived):
-    return pl.pallas_call(
-        final_kernel,
-        out_shape=(
-            jax.ShapeDtypeStruct((3, OWN), F32),
-            jax.ShapeDtypeStruct((5, OWN), F32),
-        ),
-        name="final_stage",
-    )(own, arrived)
+    )(counts, values, slots)
 
 
 def job_list(live, owners, index_gx, index_gy):
     needed = (live + BLOCK - 1) // BLOCK
-    block = jnp.arange(BLOCKS, dtype=jnp.int32)[None, :]
-    own = OWN // BLOCK
-    valid = jnp.where(block < own, block < needed[:, 0:1], block - own < needed[:, 1:2])
+    valid = jnp.arange(BLOCKS, dtype=jnp.int32)[None, :] < needed[:, None]
     valid = valid.reshape(-1).astype(jnp.int32)
     item = jnp.arange(N_GY * BLOCKS, dtype=jnp.int32)
     before = jnp.sum(jnp.where(item[None, :] < item[:, None], valid[None, :], 0), axis=1)
@@ -562,7 +562,7 @@
     owners = jnp.bitwise_xor(
         (index_gy - shifts) & (N_GY - 1), jnp.arange(N_GY, dtype=jnp.int32) & 1
     )
-    place = job_list(particles[:, 7, 0:2].astype(jnp.int32), owners, index_gx, index_gy)
+    place = job_list(particles[:, 7, 0].astype(jnp.int32), owners, index_gx, index_gy)
     table_y = jnp.asarray(left_triple(y_table()))
     table_y = lax.dynamic_index_in_dim(table_y, index_gy, 0, keepdims=False)
     rows = row_stage(place, particles, table_y)
@@ -576,10 +576,11 @@
             t_even, t_odd, rows, partial,
         )
     partial = lax.all_to_all(partial, "gy", split_axis=0, concat_axis=0, tiled=True)
-    own, back = ghost_stage(partial, ghost_slot)
+    own, back = ghost_stage(counts, partial, ghost_slot)
     devices = range(N_GX)
     route = [((i + 1) % N_GX, i) for i in devices]
-    return final_stage(own, lax.ppermute(back, "gx", route))
+    arrived = lax.ppermute(back, "gx", route)
+    return (own[:3] + arrived[:3], own[3:] + arrived[3:])
 
 
 def solution(mesh):

time: 132 us -> 163 us (1.23)
  waiting for transfers between devices: 36.6 us -> 65.3 us
  other arithmetic: 1.17 us -> 5.21 us
  Pallas kernels: 55.1 us -> 51.3 us
  starting transfers between devices: 17.6 us -> 20.1 us
  blocking collectives: 16.1 us -> 14.3 us
    ppermute x1, waiting for transfers between devices: 0.01 us -> 56.6 us  [per_device(): partner = lax.ppermute(mine, 'gy', [(i, i ^ 1) for i in members])]
    all_to_all x1, waiting for transfers between devices: 26.3 us -> 0.01 us  [per_device(): lax.all_to_all(piece, 'gx', split_axis=0, concat_axis=0, tiled=True)]
    add x0 -> x2, other arithmetic: none -> 2.95 us  [per_device(): return (own[:3] + arrived[:3], own[3:] + arrived[3:])]
    ppermute x1, starting transfers between devices: 3.08 us -> 5.25 us  [per_device(): arrived = lax.ppermute(back, 'gx', route)]
    all_to_all x1, blocking collectives: 16.1 us -> 14.3 us  [per_device(): lax.all_to_all(partial, 'gy', split_axis=0, concat_axis=0, tiled=True)]
  transfers between devices with their start and end apart: 6 -> 6, of which waited for: 4 -> 3; matrix products, arithmetic and copies ran while one was open for 3% -> 4% of each run, Pallas kernels for 20% -> 12%
where the time goes in v5:
time: 163 us; the launch traced here: 161 us
  waiting for transfers between devices  65.3 us (40%)
  Pallas kernels  51.3 us (31%)
  starting transfers between devices  20.1 us (12%)
  blocking collectives  14.3 us (9%)
  other arithmetic  5.21 us (3%)
  local copies, waits for them, and re-layouts  3.8 us (2%)
    ppermute x1, waiting for transfers between devices, per_device(): partner = lax.ppermute(mine, 'gy', [(i, i ^ 1) for i in members])  56.6 us
    pallas_call x1, Pallas kernels, field_stage(): pl.pallas_call(kernel, out_shape=jax.ShapeDtypeStruct((N_GY, 8, ROWS), F3...  22.2 us
    pallas_call x1, Pallas kernels, row_stage(): pl.pallas_call(row_kernel, out_shape=(jax.ShapeDtypeStruct((JOBS, 64, BLO...  17.6 us
    all_to_all x1, blocking collectives, per_device(): lax.all_to_all(partial, 'gy', split_axis=0, concat_axis=0, tiled=True)  14.3 us
    all_to_all x1, starting transfers between devices, per_device(): lax.all_to_all(piece, 'gx', split_axis=0, concat_axis=0, tiled=True)  7.96 us
    pallas_call x1, Pallas kernels, z_stage(): pl.pallas_call(kernel, out_shape=jax.ShapeDtypeStruct((N_GX, len(pieces),...  7.51 us
    ppermute x3, waiting for transfers between devices, per_device(): pairs.append(lax.ppermute(pair, 'gy', route))  6.46 us
    ppermute x1, starting transfers between devices, per_device(): arrived = lax.ppermute(back, 'gx', route)  5.25 us
  transfers between devices with their start and end apart: 6, of which 3 were waited for; matrix products, arithmetic and copies ran while one was open for 4% of the time, Pallas kernels for 12%

profile of v5, /device:TPU:1, one launch (start us, length us, event | category | flops | bytes accessed | tf_op | source)
XLA Modules:
  0.0 161.4 jit_solution(16636293883277541171)
XLA Ops:
  0.6 7.5 %z_stage.1 = f32[16,5,2,8,8,128]{5,4,3,2,1,0:T(8,128)} custom-call(f32[2,3,16,32,256]{4,3,2,1,0:T(8,128)} %refs_0_.1, bf16[256,768]{1,0:T(8,128)(2,1)} %constant.68.clone.refs_1_, f32[2,32,128]{2,1,0:T(8,128)} %constant.69.clone.refs_2_), custom_call_target="tpu_custom_call" | custom-call | tf_op jit(solution)/shard_map/z_stage/pallas_call | solution.py:185
  8.1 8.0 %all-to-all-start = ((f32[16,5,2,8,8,128]{5,4,3,2,1,0:T(8,128)}), f32[16,5,2,8,8,128]{5,4,3,2,1,0:T(8,128)}, u32[]{:S(2)}, u32[]{:S(2)}) async-start(f32[16,5,2,8,8,128]{5,4,3,2,1,0:T(8,128)} %z_stage.1), calls=%async_computation | async-start | bytes 10485760 | tf_op jit(solution)/shard_map/all_to_all | solution.py:552
  16.1 1.5 gather_stage.1
  17.6 2.6 %collective-permute-start = (f32[8,2560]{1,0:T(8,128)}, f32[8,2560]{1,0:T(8,128)S(1)}, u32[]{:S(2)}, u32[]{:S(2)}) collective-permute-start(f32[8,2560]{1,0:T(8,128)} %gather_stage.1), channel_id=1, source_target_pairs={{0,1},{1,0},{2,3},{3,2},{4,5},{5,4},{6,7},{7,6},{8,9},{9,8},{10,11... | collective-permute-start | bytes 245768 | tf_op jit(solution)/shard_map/ppermute | solution.py:543
  20.3 0.0 copy-done.1
  20.3 0.9 constant_dynamic-update-slice_fusion.4
  21.2 1.5 dynamic-slice_bitcast_fusion.table
  22.7 56.6 %collective-permute-done = f32[8,2560]{1,0:T(8,128)S(1)} collective-permute-done((f32[8,2560]{1,0:T(8,128)}, f32[8,2560]{1,0:T(8,128)S(1)}, u32[]{:S(2)}, u32[]{:S(2)}) %collective-permute-start) | collective-permute-done | bytes 81952 | tf_op jit(solution)/shard_map/ppermute | solution.py:543
  79.3 0.9 pad_maximum_fusion
  80.2 2.8 %collective-permute-start.3 = (f32[2,8,2560]{2,1,0:T(8,128)S(1)}, f32[2,8,2560]{2,1,0:T(8,128)S(1)}, u32[]{:S(2)}, u32[]{:S(2)}) collective-permute-start(f32[2,8,2560]{2,1,0:T(8,128)S(1)} %pad_maximum_fusion), channel_id=1, source_target_pairs={{0,4},{1,5},{2,6},{3,7},{4,0},{5,1},{6,2},{7,3},{8,12},{9,13},{10,... | collective-permute-start | bytes 491528 | tf_op jit(solution)/shard_map/ppermute | solution.py:559
  83.0 0.9 collective-permute-start.2
  83.9 0.6 collective-permute-start.1
  84.5 6.5 %collective-permute-done.1 = f32[2,8,2560]{2,1,0:T(8,128)S(1)} collective-permute-done((f32[2,8,2560]{2,1,0:T(8,128)S(1)}, f32[2,8,2560]{2,1,0:T(8,128)S(1)}, u32[]{:S(2)}, u32[]{:S(2)}) %collective-permute-start.1) | collective-permute-done | bytes 163872 | tf_op jit(solution)/shard_map/ppermute | solution.py:559
  90.9 0.0 collective-permute-done.2
  91.0 0.0 collective-permute-done.3
  91.0 0.2 fusion.1
  91.3 0.1 fusion.2
  91.4 0.1 reshape.68
  91.4 0.7 fusion.3
  92.7 0.1 select_reduce_fusion.1
  92.8 0.1 select_reduce_fusion
  93.0 0.1 select_reduce_fusion.2
  93.0 1.2 concatenate.8.place.refs_0_
  94.3 17.6 %row_stage.1 = (f32[82,64,256]{2,1,0:T(8,128)}, bf16[82,768,256]{2,1,0:T(8,128)(2,1)}) custom-call(s32[249]{0:T(256)} %concatenate.8.place.refs_0_, f32[8,8,2560]{2,1,0:T(8,128)} %copy-done, bf16[64,768]{1,0:T(8,128)(2,1)} %dynamic-slice_bitcast_fusion.table), custom_call_target="tpu_custom_call" | custom-call | tf_op jit(solution)/shard_map/row_stage/pallas_call | solution.py:292
  111.9 0.0 all-to-all-done.refs_1_.refs_2_
  111.9 22.2 %field_stage.1 = f32[8,8,2560]{2,1,0:T(8,128)} custom-call(s32[249]{0:T(256)} %concatenate.8.place.refs_0_, f32[16,5,2,8,8,128]{5,4,3,2,1,0:T(8,128)} %all-to-all-done.refs_1_.refs_2_, f32[16,5,2,8,8,128]{5,4,3,2,1,0:T(8,128)} %all-to-all-done.refs_1_.refs_2_, bf16[256,768]{1,0:T(8,128)(2,1)} %constant.72.clone.refs_3_, ...), custom_call_target="tpu_custom_call" | custom-call | tf_op jit(solution)/shard_map/field_stage/pallas_call | solution.py:464
  134.1 14.3 %all_to_all.10.values = f32[8,8,2560]{2,1,0:T(8,128)} all-to-all(f32[8,8,2560]{2,1,0:T(8,128)} %field_stage.1), channel_id=1, replica_groups=mesh['gx'=16,'gy'=8] {'gy'}, dimensions={0} | all-to-all | bytes 1310720 | tf_op jit(solution)/shard_map/all_to_all | solution.py:578
  148.4 2.5 %ghost_stage.1 = (f32[8,2048]{1,0:T(8,128)}, f32[8,2048]{1,0:T(8,128)}) custom-call(s32[1,4]{1,0:T(1,128)} %counts.3, f32[8,8,2560]{2,1,0:T(8,128)} %all_to_all.10.values, s32[3,512]{1,0:T(4,128)} %slots.1), custom_call_target="tpu_custom_call" | custom-call | tf_op jit(solution)/shard_map/ghost_stage/pallas_call | solution.py:506
  150.9 5.2 %collective-permute-start.4 = (f32[8,2048]{1,0:T(8,128)}, f32[8,2048]{1,0:T(8,128)S(1)}, u32[]{:S(2)}, u32[]{:S(2)}) collective-permute-start(f32[8,2048]{1,0:T(8,128)} %get-tuple-element.9), channel_id=1, source_target_pairs={{8,0},{16,8},{24,16},{32,24},{40,32},{48,40},{56,48},{64,56},{72,6... | collective-permute-start | bytes 196616 | tf_op jit(solution)/shard_map/ppermute | solution.py:582
  156.2 2.3 %collective-permute-done.4 = f32[8,2048]{1,0:T(8,128)S(1)} collective-permute-done((f32[8,2048]{1,0:T(8,128)}, f32[8,2048]{1,0:T(8,128)S(1)}, u32[]{:S(2)}, u32[]{:S(2)}) %collective-permute-start.4) | collective-permute-done | bytes 65568 | tf_op jit(solution)/shard_map/ppermute | solution.py:582
  158.4 1.5 slice_add_fusion.1
  159.9 1.5 slice_add_fusion
  (12 shorter events, 0.1 us)
Async XLA Ops:
  8.1 12.1 %copy-start.1 = (s32[8]{0:T(128)S(1)}, s32[8]{0:T(128)}, u32[]{:S(2)}) copy-start(s32[8]{0:T(128)} %constant.75) | copy-start | bytes 100
  8.1 103.7 %all-to-all-start = ((f32[16,5,2,8,8,128]{5,4,3,2,1,0:T(8,128)}), f32[16,5,2,8,8,128]{5,4,3,2,1,0:T(8,128)}, u32[]{:S(2)}, u32[]{:S(2)}) async-start(f32[16,5,2,8,8,128]{5,4,3,2,1,0:T(8,128)} %z_stage.1), calls=%async_computation | async-start | bytes 10485760 | tf_op jit(solution)/shard_map/all_to_all | solution.py:552
  17.6 61.6 %collective-permute-start = (f32[8,2560]{1,0:T(8,128)}, f32[8,2560]{1,0:T(8,128)S(1)}, u32[]{:S(2)}, u32[]{:S(2)}) collective-permute-start(f32[8,2560]{1,0:T(8,128)} %gather_stage.1), channel_id=1, source_target_pairs={{0,1},{1,0},{2,3},{3,2},{4,5},{5,4},{6,7},{7,6},{8,9},{9,8},{10,11... | collective-permute-start | bytes 245768 | tf_op jit(solution)/shard_map/ppermute | solution.py:543
  80.2 10.8 %collective-permute-start.3 = (f32[2,8,2560]{2,1,0:T(8,128)S(1)}, f32[2,8,2560]{2,1,0:T(8,128)S(1)}, u32[]{:S(2)}, u32[]{:S(2)}) collective-permute-start(f32[2,8,2560]{2,1,0:T(8,128)S(1)} %pad_maximum_fusion), channel_id=1, source_target_pairs={{0,4},{1,5},{2,6},{3,7},{4,0},{5,1},{6,2},{7,3},{8,12},{9,13},{10,... | collective-permute-start | bytes 491528 | tf_op jit(solution)/shard_map/ppermute | solution.py:559
  83.0 7.9 %collective-permute-start.2 = (f32[2,8,2560]{2,1,0:T(8,128)S(1)}, f32[2,8,2560]{2,1,0:T(8,128)S(1)}, u32[]{:S(2)}, u32[]{:S(2)}) collective-permute-start(f32[2,8,2560]{2,1,0:T(8,128)S(1)} %pad_maximum_fusion), channel_id=1, source_target_pairs={{0,6},{1,7},{2,0},{3,1},{4,2},{5,3},{6,4},{7,5},{8,14},{9,15},{10,... | collective-permute-start | bytes 491528 | tf_op jit(solution)/shard_map/ppermute | solution.py:559
  83.9 7.1 %collective-permute-start.1 = (f32[2,8,2560]{2,1,0:T(8,128)S(1)}, f32[2,8,2560]{2,1,0:T(8,128)S(1)}, u32[]{:S(2)}, u32[]{:S(2)}) collective-permute-start(f32[2,8,2560]{2,1,0:T(8,128)S(1)} %pad_maximum_fusion), channel_id=1, source_target_pairs={{0,2},{1,3},{2,4},{3,5},{4,6},{5,7},{6,0},{7,1},{8,10},{9,11},{10,... | collective-permute-start | bytes 491528 | tf_op jit(solution)/shard_map/ppermute | solution.py:559
  91.0 3.2 %copy-start = (f32[8,8,2560]{2,1,0:T(8,128)}, f32[8,8,2560]{2,1,0:T(8,128)S(1)}, u32[]{:S(2)}) copy-start(f32[8,8,2560]{2,1,0:T(8,128)S(1)} %constant_dynamic-update-slice_fusion.particles) | copy-start | bytes 1966084
  150.9 7.5 %collective-permute-start.4 = (f32[8,2048]{1,0:T(8,128)}, f32[8,2048]{1,0:T(8,128)S(1)}, u32[]{:S(2)}, u32[]{:S(2)}) collective-permute-start(f32[8,2048]{1,0:T(8,128)} %get-tuple-element.9), channel_id=1, source_target_pairs={{8,0},{16,8},{24,16},{32,24},{40,32},{48,40},{56,48},{64,56},{72,6... | collective-permute-start | bytes 196616 | tf_op jit(solution)/shard_map/ppermute | solution.py:582

commit v6 on v5

--- a/solution.py
+++ b/solution.py
@@ -515,6 +515,23 @@
     )(counts, values, slots)
 
 
+def final_kernel(own, arrived, velocity, strain):
+    total = own[...] + arrived[...]
+    velocity[...] = total[:3]
+    strain[...] = total[3:]
+
+
+def final_stage(own, arrived):
+    return pl.pallas_call(
+        final_kernel,
+        out_shape=(
+            jax.ShapeDtypeStruct((3, OWN), F32),
+            jax.ShapeDtypeStruct((5, OWN), F32),
+        ),
+        name="final_stage",
+    )(own, arrived)
+
+
 def job_list(live, owners, index_gx, index_gy):
     needed = (live + BLOCK - 1) // BLOCK
     valid = jnp.arange(BLOCKS, dtype=jnp.int32)[None, :] < needed[:, None]
@@ -579,8 +596,7 @@
     own, back = ghost_stage(counts, partial, ghost_slot)
     devices = range(N_GX)
     route = [((i + 1) % N_GX, i) for i in devices]
-    arrived = lax.ppermute(back, "gx", route)
-    return (own[:3] + arrived[:3], own[3:] + arrived[3:])
+    return final_stage(own, lax.ppermute(back, "gx", route))
 
 
 def solution(mesh):

time: 163 us -> 162 us (level)
  other arithmetic: 5.21 us -> 2.26 us
    add x2 -> x0, other arithmetic: 2.95 us -> none  [per_device(): return (own[:3] + arrived[:3], own[3:] + arrived[3:])]
where the time goes in v6:
time: 162 us; the launch traced here: 161 us
  waiting for transfers between devices  65.3 us (40%)
  Pallas kernels  52.9 us (33%)
  starting transfers between devices  20.1 us (12%)
  blocking collectives  14.3 us (9%)
  local copies, waits for them, and re-layouts  4.42 us (3%)
  other arithmetic  2.26 us (1%)
    ppermute x1, waiting for transfers between devices, per_device(): partner = lax.ppermute(mine, 'gy', [(i, i ^ 1) for i in members])  56.6 us
    pallas_call x1, Pallas kernels, field_stage(): pl.pallas_call(kernel, out_shape=jax.ShapeDtypeStruct((N_GY, 8, ROWS), F3...  22.2 us
    pallas_call x1, Pallas kernels, row_stage(): pl.pallas_call(row_kernel, out_shape=(jax.ShapeDtypeStruct((JOBS, 64, BLO...  17.6 us
    all_to_all x1, blocking collectives, per_device(): lax.all_to_all(partial, 'gy', split_axis=0, concat_axis=0, tiled=True)  14.3 us
    all_to_all x1, starting transfers between devices, per_device(): lax.all_to_all(piece, 'gx', split_axis=0, concat_axis=0, tiled=True)  7.96 us
    pallas_call x1, Pallas kernels, z_stage(): pl.pallas_call(kernel, out_shape=jax.ShapeDtypeStruct((N_GX, len(pieces),...  7.51 us
    ppermute x3, waiting for transfers between devices, per_device(): pairs.append(lax.ppermute(pair, 'gy', route))  6.46 us
    ppermute x1, starting transfers between devices, per_device(): return final_stage(own, lax.ppermute(back, 'gx', route))  5.25 us
  transfers between devices with their start and end apart: 6, of which 3 were waited for; matrix products, arithmetic and copies ran while one was open for 4% of the time, Pallas kernels for 12%

profile of v6, /device:TPU:1, one launch (start us, length us, event | category | flops | bytes accessed | tf_op | source)
XLA Modules:
  0.0 160.6 jit_solution(2369140239726112995)
XLA Ops:
  0.6 7.5 %z_stage.1 = f32[16,5,2,8,8,128]{5,4,3,2,1,0:T(8,128)} custom-call(f32[2,3,16,32,256]{4,3,2,1,0:T(8,128)} %refs_0_.1, bf16[256,768]{1,0:T(8,128)(2,1)} %constant.68.clone.refs_1_, f32[2,32,128]{2,1,0:T(8,128)} %constant.69.clone.refs_2_), custom_call_target="tpu_custom_call" | custom-call | tf_op jit(solution)/shard_map/z_stage/pallas_call | solution.py:185
  8.1 8.0 %all-to-all-start = ((f32[16,5,2,8,8,128]{5,4,3,2,1,0:T(8,128)}), f32[16,5,2,8,8,128]{5,4,3,2,1,0:T(8,128)}, u32[]{:S(2)}, u32[]{:S(2)}) async-start(f32[16,5,2,8,8,128]{5,4,3,2,1,0:T(8,128)} %z_stage.1), calls=%async_computation | async-start | bytes 10485760 | tf_op jit(solution)/shard_map/all_to_all | solution.py:569
  16.1 1.5 gather_stage.1
  17.6 2.6 %collective-permute-start = (f32[8,2560]{1,0:T(8,128)}, f32[8,2560]{1,0:T(8,128)S(1)}, u32[]{:S(2)}, u32[]{:S(2)}) collective-permute-start(f32[8,2560]{1,0:T(8,128)} %gather_stage.1), channel_id=1, source_target_pairs={{0,1},{1,0},{2,3},{3,2},{4,5},{5,4},{6,7},{7,6},{8,9},{9,8},{10,11... | collective-permute-start | bytes 245768 | tf_op jit(solution)/shard_map/ppermute | solution.py:560
  20.3 0.0 copy-done.2
  20.3 0.9 constant_dynamic-update-slice_fusion.4
  21.2 1.5 dynamic-slice_bitcast_fusion.table
  22.7 56.6 %collective-permute-done = f32[8,2560]{1,0:T(8,128)S(1)} collective-permute-done((f32[8,2560]{1,0:T(8,128)}, f32[8,2560]{1,0:T(8,128)S(1)}, u32[]{:S(2)}, u32[]{:S(2)}) %collective-permute-start) | collective-permute-done | bytes 81952 | tf_op jit(solution)/shard_map/ppermute | solution.py:560
  79.3 0.9 pad_maximum_fusion
  80.2 2.8 %collective-permute-start.3 = (f32[2,8,2560]{2,1,0:T(8,128)S(1)}, f32[2,8,2560]{2,1,0:T(8,128)S(1)}, u32[]{:S(2)}, u32[]{:S(2)}) collective-permute-start(f32[2,8,2560]{2,1,0:T(8,128)S(1)} %pad_maximum_fusion), channel_id=1, source_target_pairs={{0,4},{1,5},{2,6},{3,7},{4,0},{5,1},{6,2},{7,3},{8,12},{9,13},{10,... | collective-permute-start | bytes 491528 | tf_op jit(solution)/shard_map/ppermute | solution.py:576
  83.0 0.9 collective-permute-start.2
  83.9 0.6 collective-permute-start.1
  84.5 6.5 %collective-permute-done.1 = f32[2,8,2560]{2,1,0:T(8,128)S(1)} collective-permute-done((f32[2,8,2560]{2,1,0:T(8,128)S(1)}, f32[2,8,2560]{2,1,0:T(8,128)S(1)}, u32[]{:S(2)}, u32[]{:S(2)}) %collective-permute-start.1) | collective-permute-done | bytes 163872 | tf_op jit(solution)/shard_map/ppermute | solution.py:576
  90.9 0.0 collective-permute-done.2
  91.0 0.0 collective-permute-done.3
  91.0 0.2 fusion.1
  91.3 0.1 fusion.2
  91.4 0.1 reshape.68
  91.4 0.7 fusion.3
  92.7 0.1 select_reduce_fusion.1
  92.8 0.1 select_reduce_fusion
  93.0 0.1 select_reduce_fusion.2
  93.0 1.2 concatenate.8.place.refs_0_
  94.3 17.6 %row_stage.1 = (f32[82,64,256]{2,1,0:T(8,128)}, bf16[82,768,256]{2,1,0:T(8,128)(2,1)}) custom-call(s32[249]{0:T(256)} %concatenate.8.place.refs_0_, f32[8,8,2560]{2,1,0:T(8,128)} %copy-done, bf16[64,768]{1,0:T(8,128)(2,1)} %dynamic-slice_bitcast_fusion.table), custom_call_target="tpu_custom_call" | custom-call | tf_op jit(solution)/shard_map/row_stage/pallas_call | solution.py:292
  111.9 0.0 all-to-all-done.refs_1_.refs_2_
  111.9 22.2 %field_stage.1 = f32[8,8,2560]{2,1,0:T(8,128)} custom-call(s32[249]{0:T(256)} %concatenate.8.place.refs_0_, f32[16,5,2,8,8,128]{5,4,3,2,1,0:T(8,128)} %all-to-all-done.refs_1_.refs_2_, f32[16,5,2,8,8,128]{5,4,3,2,1,0:T(8,128)} %all-to-all-done.refs_1_.refs_2_, bf16[256,768]{1,0:T(8,128)(2,1)} %constant.72.clone.refs_3_, ...), custom_call_target="tpu_custom_call" | custom-call | tf_op jit(solution)/shard_map/field_stage/pallas_call | solution.py:464
  134.1 14.3 %all_to_all.10.values = f32[8,8,2560]{2,1,0:T(8,128)} all-to-all(f32[8,8,2560]{2,1,0:T(8,128)} %field_stage.1), channel_id=1, replica_groups=mesh['gx'=16,'gy'=8] {'gy'}, dimensions={0} | all-to-all | bytes 1310720 | tf_op jit(solution)/shard_map/all_to_all | solution.py:595
  148.4 2.5 %ghost_stage.1 = (f32[8,2048]{1,0:T(8,128)}, f32[8,2048]{1,0:T(8,128)}) custom-call(s32[1,4]{1,0:T(1,128)} %counts.3, f32[8,8,2560]{2,1,0:T(8,128)} %all_to_all.10.values, s32[3,512]{1,0:T(4,128)} %slots.1), custom_call_target="tpu_custom_call" | custom-call | tf_op jit(solution)/shard_map/ghost_stage/pallas_call | solution.py:506
  150.9 5.2 %collective-permute-start.4 = (f32[8,2048]{1,0:T(8,128)}, f32[8,2048]{1,0:T(8,128)S(1)}, u32[]{:S(2)}, u32[]{:S(2)}) collective-permute-start(f32[8,2048]{1,0:T(8,128)} %get-tuple-element.9), channel_id=1, source_target_pairs={{8,0},{16,8},{24,16},{32,24},{40,32},{48,40},{56,48},{64,56},{72,6... | collective-permute-start | bytes 196616 | tf_op jit(solution)/shard_map/ppermute | solution.py:599
  156.2 2.3 %collective-permute-done.4.arrived = f32[8,2048]{1,0:T(8,128)S(1)} collective-permute-done((f32[8,2048]{1,0:T(8,128)}, f32[8,2048]{1,0:T(8,128)S(1)}, u32[]{:S(2)}, u32[]{:S(2)}) %collective-permute-start.4) | collective-permute-done | bytes 65568 | tf_op jit(solution)/shard_map/ppermute | solution.py:599
  158.4 0.6 copy-done.1
  159.1 1.5 final_stage.1
  (13 shorter events, 0.1 us)
Async XLA Ops:
  8.1 12.1 %copy-start.2 = (s32[8]{0:T(128)S(1)}, s32[8]{0:T(128)}, u32[]{:S(2)}) copy-start(s32[8]{0:T(128)} %constant.75) | copy-start | bytes 100
  8.1 103.7 %all-to-all-start = ((f32[16,5,2,8,8,128]{5,4,3,2,1,0:T(8,128)}), f32[16,5,2,8,8,128]{5,4,3,2,1,0:T(8,128)}, u32[]{:S(2)}, u32[]{:S(2)}) async-start(f32[16,5,2,8,8,128]{5,4,3,2,1,0:T(8,128)} %z_stage.1), calls=%async_computation | async-start | bytes 10485760 | tf_op jit(solution)/shard_map/all_to_all | solution.py:569
  17.6 61.6 %collective-permute-start = (f32[8,2560]{1,0:T(8,128)}, f32[8,2560]{1,0:T(8,128)S(1)}, u32[]{:S(2)}, u32[]{:S(2)}) collective-permute-start(f32[8,2560]{1,0:T(8,128)} %gather_stage.1), channel_id=1, source_target_pairs={{0,1},{1,0},{2,3},{3,2},{4,5},{5,4},{6,7},{7,6},{8,9},{9,8},{10,11... | collective-permute-start | bytes 245768 | tf_op jit(solution)/shard_map/ppermute | solution.py:560
  80.2 10.8 %collective-permute-start.3 = (f32[2,8,2560]{2,1,0:T(8,128)S(1)}, f32[2,8,2560]{2,1,0:T(8,128)S(1)}, u32[]{:S(2)}, u32[]{:S(2)}) collective-permute-start(f32[2,8,2560]{2,1,0:T(8,128)S(1)} %pad_maximum_fusion), channel_id=1, source_target_pairs={{0,4},{1,5},{2,6},{3,7},{4,0},{5,1},{6,2},{7,3},{8,12},{9,13},{10,... | collective-permute-start | bytes 491528 | tf_op jit(solution)/shard_map/ppermute | solution.py:576
  83.0 7.9 %collective-permute-start.2 = (f32[2,8,2560]{2,1,0:T(8,128)S(1)}, f32[2,8,2560]{2,1,0:T(8,128)S(1)}, u32[]{:S(2)}, u32[]{:S(2)}) collective-permute-start(f32[2,8,2560]{2,1,0:T(8,128)S(1)} %pad_maximum_fusion), channel_id=1, source_target_pairs={{0,6},{1,7},{2,0},{3,1},{4,2},{5,3},{6,4},{7,5},{8,14},{9,15},{10,... | collective-permute-start | bytes 491528 | tf_op jit(solution)/shard_map/ppermute | solution.py:576
  83.9 7.1 %collective-permute-start.1 = (f32[2,8,2560]{2,1,0:T(8,128)S(1)}, f32[2,8,2560]{2,1,0:T(8,128)S(1)}, u32[]{:S(2)}, u32[]{:S(2)}) collective-permute-start(f32[2,8,2560]{2,1,0:T(8,128)S(1)} %pad_maximum_fusion), channel_id=1, source_target_pairs={{0,2},{1,3},{2,4},{3,5},{4,6},{5,7},{6,0},{7,1},{8,10},{9,11},{10,... | collective-permute-start | bytes 491528 | tf_op jit(solution)/shard_map/ppermute | solution.py:576
  91.0 3.2 %copy-start = (f32[8,8,2560]{2,1,0:T(8,128)}, f32[8,8,2560]{2,1,0:T(8,128)S(1)}, u32[]{:S(2)}) copy-start(f32[8,8,2560]{2,1,0:T(8,128)S(1)} %constant_dynamic-update-slice_fusion.particles) | copy-start | bytes 1966084
  150.9 7.5 %collective-permute-start.4 = (f32[8,2048]{1,0:T(8,128)}, f32[8,2048]{1,0:T(8,128)S(1)}, u32[]{:S(2)}, u32[]{:S(2)}) collective-permute-start(f32[8,2048]{1,0:T(8,128)} %get-tuple-element.9), channel_id=1, source_target_pairs={{8,0},{16,8},{24,16},{32,24},{40,32},{48,40},{56,48},{64,56},{72,6... | collective-permute-start | bytes 196616 | tf_op jit(solution)/shard_map/ppermute | solution.py:599
  158.4 0.6 copy-start.1

commit v7 on v6

--- a/solution.py
+++ b/solution.py
@@ -22,7 +22,9 @@
 WAVE = 2.0 * math.pi / GRID
 WINDOW = 48
 BLOCK = 256
-CHUNKS = ((0, 1, 2, 3),)
+CHUNKS = ((0, 2), (1, 3))
+ORDER = (0, 2, 1, 3)
+FIELDS = 7
 EXTRA = 4
 BLOCKS = ROWS // BLOCK
 JOBS = N_GY * BLOCKS + 2
@@ -97,7 +99,7 @@
 def z_kernel(pieces, source, table, twiddle, out, even, odd):
     quad = pl.program_id(0)
     with_extra = EXTRA in pieces
-    parities = [p for p in range(2) if with_extra or any(c % 2 == p for c in pieces)]
+    parities = [p for p in range(2) if any(c != EXTRA and c % 2 == p for c in pieces)]
     row = lax.broadcasted_iota(jnp.int32, (32, GRID), 0)
     mode_y = signed(row + lax.axis_index("gy") * 32)
     mode_z = signed(lax.broadcasted_iota(jnp.int32, (32, GRID), 1))
@@ -124,7 +126,7 @@
             rows.append((-half_wave_z * v[1][1], half_wave_z * v[0][1], 512 + k * 32))
         for real, imag, start in rows:
             here = slice(start, start + 32)
-            for p in parities:
+            for p in parities if start < 512 else range(2):
                 if p == 0:
                     re = real[:, :HALF] + real[:, HALF:]
                     im = imag[:, :HALF] + imag[:, HALF:]
@@ -246,7 +248,9 @@
     y_cell = lax.broadcasted_iota(jnp.int32, (GRID, BLOCK), 0).astype(F32)
     x_cell = lax.broadcasted_iota(jnp.int32, (WINDOW, BLOCK), 0).astype(F32)
     local_z = lax.broadcasted_iota(jnp.int32, (16, BLOCK), 0)
-    z_cell = (place[0] * 16 + 4 * (local_z % 4) + local_z // 4).astype(F32)
+    turn_of = local_z // 4
+    c = 2 * (turn_of & 1) + turn_of // 2
+    z_cell = (place[0] * 16 + 4 * (local_z % 4) + c).astype(F32)
     jobs = 2 * ((place[2] + 1) // 2)
 
     def copies(slot, job):
@@ -318,10 +322,11 @@
     previous = rest[0] if len(rest) == 11 else None
     out, field, work0, work1, work2, work3, window, phase, plane, arrived = rest[-10:]
     work = (work0, work1, work2, work3)
-    first_c = steps[0]
+    first_c = ORDER.index(steps[0])
     depth = 4 * len(steps)
     step_c = pl.program_id(0)
-    c = first_c + step_c
+    turn_of = first_c + step_c
+    c = 2 * (turn_of & 1) + turn_of // 2
     pairs = (place[2] + 1) // 2
 
     def copies(pair, base):
@@ -348,11 +353,10 @@
     group = lane // 32
     row = lax.broadcasted_iota(jnp.int32, (HALF, 128), 0)
     wave_y = WAVE * signed(lane % 32 + place[1] * 32)
-    cross_y = jnp.where(group == 0, wave_y, jnp.where(group == 2, 0.0, 0.5 * wave_y))
+    cross_y = jnp.where((group == 1) | (group == 3), 0.5 * wave_y, 0.0)
     half_same = jnp.where((group == 1) | (group == 2), 0.5, 0.0)
     plain_left = group == 2
     plain_extra = group == 3
-    cross_left = group == 0
     flat_main = main.reshape(GRID * 8, 128)
     flat_extra = extra.reshape(GRID * 8, 128)
     waves = [WAVE * signed(2 * row + parity) for parity in range(2)]
@@ -375,7 +379,7 @@
                 moved = pltpu.roll(load(flat_extra, q), 32 * (3 - c), 1)
                 left = pltpu.roll(value, 96, 1)
                 right = pltpu.roll(value, 32, 1)
-                cross = cross_y * jnp.where(cross_left, left, right) + cross_x * value
+                cross = cross_y * right + cross_x * value
                 plain = jnp.where(plain_left, left, jnp.where(plain_extra, moved, 0.0))
                 parts.append((value, wave_x * left, cross, plain))
             (a_re, x_re, c_re, p_re), (a_im, x_im, c_im, p_im) = parts
@@ -410,7 +414,14 @@
 
         for owner in range(N_GY):
             block = field[:, owner * 32 : owner * 32 + WINDOW, :]
-            window[owner] = block.reshape(depth * WINDOW, 512).T
+            turned = block.reshape(depth * WINDOW, 512).T
+            for q in range(2):
+                top = q * 32 * FIELDS
+                window[owner, top : top + 128] = turned[q * 256 : q * 256 + 128]
+                window[owner, top + 128 : top + 224] = turned[q * 256 + 160 : q * 256 + 256]
+        wave_rows = WAVE * signed(
+            lax.broadcasted_iota(jnp.int32, (32, BLOCK), 0) + place[1] * 32
+        )
 
         def one_pair(pair, carry):
             base = 2 * (pair & (AHEAD - 1))
@@ -426,10 +437,14 @@
                 job = 2 * pair + side
                 owner, block = place[HEAD + 2 * JOBS + job], place[HEAD + JOBS + job]
                 lanes = pl.ds(pl.multiple_of(block * BLOCK, BLOCK), BLOCK)
-                summed = dot(window[owner], plane[base + side], NN).reshape(2, 8, 32, BLOCK)
-                turn = phase[base + side]
-                product = summed[0] * turn[None, 0:32] + summed[1] * turn[None, 32:64]
-                value = jnp.sum(product, axis=1)
+                summed = dot(window[owner], plane[base + side], NN)
+                summed = summed.reshape(2, FIELDS, 32, BLOCK)
+                turn_re, turn_im = phase[base + side, 0:32], phase[base + side, 32:64]
+                product = summed[0] * turn_re[None] + summed[1] * turn_im[None]
+                along_y = wave_rows * (summed[0, 1] * turn_im - summed[1, 1] * turn_re)
+                value = jnp.concatenate(
+                    [jnp.sum(product, axis=1), jnp.sum(along_y, axis=0, keepdims=True)], axis=0
+                )
                 if previous is not None:
                     value = value + previous[owner, :, lanes]
                 out[owner, :, lanes] = value
@@ -475,7 +490,7 @@
                 pltpu.VMEM((768, 256), BF16),
                 pltpu.VMEM((768, 256), BF16),
                 pltpu.VMEM((768, 256), BF16),
-                pltpu.VMEM((N_GY, 512, depth * WINDOW), BF16),
+                pltpu.VMEM((N_GY, 64 * FIELDS, depth * WINDOW), BF16),
                 pltpu.VMEM((2 * AHEAD, 64, BLOCK), F32),
                 pltpu.VMEM((2 * AHEAD, depth * WINDOW, BLOCK), BF16),
                 pltpu.SemaphoreType.DMA((2, 2 * AHEAD)),
@@ -518,7 +533,9 @@
 def final_kernel(own, arrived, velocity, strain):
     total = own[...] + arrived[...]
     velocity[...] = total[:3]
-    strain[...] = total[3:]
+    strain[0:1] = total[3:4]
+    strain[1:2] = total[7:8]
+    strain[2:5] = total[4:7]
 
 
 def final_stage(own, arrived):
@@ -565,10 +582,9 @@
         z_stage(chunk + ((EXTRA,) if number == 0 else ()), source_hat, table_z, twiddle)
         for number, chunk in enumerate(CHUNKS)
     ]
-    received = [
-        lax.all_to_all(piece, "gx", split_axis=0, concat_axis=0, tiled=True)
-        for piece in sent
-    ]
+    received = []
+    for piece in sent:
+        received.append(lax.all_to_all(piece, "gx", split_axis=0, concat_axis=0, tiled=True))
     pair = jnp.stack([mine, partner])
     pairs = [pair]
     for shift in (2, 6, 4):

time: 162 us -> 156 us (0.963); the launches traced: 161 us -> 153 us
  waiting for transfers between devices: 65.3 us -> 35.9 us
  Pallas kernels: 52.9 us -> 64.6 us
  starting transfers between devices: 20.1 us -> 25.8 us
  local copies, waits for them, and re-layouts: 4.42 us -> 8.64 us
    ppermute x1, waiting for transfers between devices: 56.6 us -> 28.8 us  [per_device(): partner = lax.ppermute(mine, 'gy', [(i, i ^ 1) for i in members])]
    pallas_call x1 -> x2, Pallas kernels: 22.2 us -> 29.3 us  [field_stage(): pl.pallas_call(kernel, out_shape=jax.ShapeDtypeStruct((N_GY, 8, ROWS), F3...]
    all_to_all x1 -> x2, starting transfers between devices: 7.96 us -> 13.4 us  [per_device(): lax.all_to_all(piece, 'gx', split_axis=0, concat_axis=0, tiled=True)]
    pallas_call x1 -> x2, Pallas kernels: 7.51 us -> 12.1 us  [z_stage(): pl.pallas_call(kernel, out_shape=jax.ShapeDtypeStruct((N_GX, len(pieces),...]
    unnamed x10 -> x12, local copies, waits for them, and re-layouts: 1.58 us -> 4.16 us
  transfers between devices with their start and end apart: 6 -> 7, of which waited for: 3 -> 3; matrix products, arithmetic and copies ran while one was open for 4% -> 7% of each run, Pallas kernels for 12% -> 26%
where the time goes in v7:
time: 156 us; the launch traced here: 153 us
  Pallas kernels  64.6 us (41%)
  waiting for transfers between devices  35.9 us (23%)
  starting transfers between devices  25.8 us (17%)
  blocking collectives  14.2 us (9%)
  local copies, waits for them, and re-layouts  8.64 us (6%)
  other arithmetic  2.15 us (1%)
    pallas_call x2, Pallas kernels, field_stage(): pl.pallas_call(kernel, out_shape=jax.ShapeDtypeStruct((N_GY, 8, ROWS), F3...  29.3 us
    ppermute x1, waiting for transfers between devices, per_device(): partner = lax.ppermute(mine, 'gy', [(i, i ^ 1) for i in members])  28.8 us
    pallas_call x1, Pallas kernels, row_stage(): pl.pallas_call(row_kernel, out_shape=(jax.ShapeDtypeStruct((JOBS, 64, BLO...  17.6 us
    all_to_all x1, blocking collectives, per_device(): lax.all_to_all(partial, 'gy', split_axis=0, concat_axis=0, tiled=True)  14.2 us
    all_to_all x2, starting transfers between devices, per_device(): lax.all_to_all(piece, 'gx', split_axis=0, concat_axis=0, tiled=True)  13.4 us
    pallas_call x2, Pallas kernels, z_stage(): pl.pallas_call(kernel, out_shape=jax.ShapeDtypeStruct((N_GX, len(pieces),...  12.1 us
    ppermute x3, waiting for transfers between devices, per_device(): pairs.append(lax.ppermute(pair, 'gy', route))  5.83 us
    ppermute x1, starting transfers between devices, per_device(): return final_stage(own, lax.ppermute(back, 'gx', route))  5.48 us
  transfers between devices with their start and end apart: 7, of which 3 were waited for; matrix products, arithmetic and copies ran while one was open for 7% of the time, Pallas kernels for 26%

profile of v7, /device:TPU:1, one launch (start us, length us, event | category | flops | bytes accessed | tf_op | source)
XLA Modules:
  0.0 152.7 jit_solution(18104599287492995680)
XLA Ops:
  0.6 6.6 %z_stage.3 = f32[16,3,2,8,8,128]{5,4,3,2,1,0:T(8,128)} custom-call(f32[2,3,16,32,256]{4,3,2,1,0:T(8,128)} %refs_0_.3, bf16[256,768]{1,0:T(8,128)(2,1)} %constant.68.clone.refs_1_, f32[2,32,128]{2,1,0:T(8,128)} %constant.69.clone.refs_2_), custom_call_target="tpu_custom_call" | custom-call | tf_op jit(solution)/shard_map/z_stage/pallas_call | solution.py:187
  7.2 7.8 %all-to-all-start.1 = ((f32[16,3,2,8,8,128]{5,4,3,2,1,0:T(8,128)}), f32[16,3,2,8,8,128]{5,4,3,2,1,0:T(8,128)S(1)}, u32[]{:S(2)}, u32[]{:S(2)}) async-start(f32[16,3,2,8,8,128]{5,4,3,2,1,0:T(8,128)} %z_stage.3), calls=%async_computation.1 | async-start | bytes 6291456 | tf_op jit(solution)/shard_map/all_to_all | solution.py:587
  15.1 1.5 %gather_stage.1 = f32[8,2560]{1,0:T(8,128)} custom-call(s32[1,4]{1,0:T(1,128)} %counts.3, s32[3,2048]{1,0:T(4,128)} %start.1, f32[3,2048]{1,0:T(4,128)} %offset.1, s32[3,3,512]{2,1,0:T(4,128)} %other_start.1, f32[3,3,512]{2,1,0:T(4,128)} %other_offset.1), custom_call_target="tpu_custom_call" | custom-call | tf_op jit(solution)/shard_map/gather_stage/pallas_call | solution.py:231
  16.6 2.6 %collective-permute-start = (f32[8,2560]{1,0:T(8,128)}, f32[8,2560]{1,0:T(8,128)S(1)}, u32[]{:S(2)}, u32[]{:S(2)}) collective-permute-start(f32[8,2560]{1,0:T(8,128)} %gather_stage.1), channel_id=1, source_target_pairs={{0,1},{1,0},{2,3},{3,2},{4,5},{5,4},{6,7},{7,6},{8,9},{9,8},{10,11... | collective-permute-start | bytes 245768 | tf_op jit(solution)/shard_map/ppermute | solution.py:577
  19.2 5.5 %z_stage.2 = f32[16,2,2,8,8,128]{5,4,3,2,1,0:T(8,128)} custom-call(f32[2,3,16,32,256]{4,3,2,1,0:T(8,128)} %refs_0_.3, bf16[256,768]{1,0:T(8,128)(2,1)} %constant.68.clone.refs_1_, f32[2,32,128]{2,1,0:T(8,128)} %constant.69.clone.refs_2_), custom_call_target="tpu_custom_call" | custom-call | tf_op jit(solution)/shard_map/z_stage/pallas_call | solution.py:187
  24.8 0.6 constant_dynamic-update-slice_fusion.4
  25.4 1.5 dynamic-slice_bitcast_fusion.table
  26.9 28.8 %collective-permute-done = f32[8,2560]{1,0:T(8,128)S(1)} collective-permute-done((f32[8,2560]{1,0:T(8,128)}, f32[8,2560]{1,0:T(8,128)S(1)}, u32[]{:S(2)}, u32[]{:S(2)}) %collective-permute-start) | collective-permute-done | bytes 81952 | tf_op jit(solution)/shard_map/ppermute | solution.py:577
  55.8 2.8 %collective-permute-start.3 = (f32[2,8,2560]{2,1,0:T(8,128)S(1)}, f32[2,8,2560]{2,1,0:T(8,128)}, u32[]{:S(2)}, u32[]{:S(2)}) collective-permute-start(f32[2,8,2560]{2,1,0:T(8,128)S(1)} %pad_maximum_fusion), channel_id=1, source_target_pairs={{0,4},{1,5},{2,6},{3,7},{4,0},{5,1},{6,2},{7,3},{8,12},{9,13},{10,... | collective-permute-start | bytes 491528 | tf_op jit(solution)/shard_map/ppermute | solution.py:592
  58.6 0.9 collective-permute-start.2
  59.5 0.6 collective-permute-start.1
  60.1 0.6 constant_dynamic-update-slice_fusion.3
  60.7 5.8 %collective-permute-done.1 = f32[2,8,2560]{2,1,0:T(8,128)S(1)} collective-permute-done((f32[2,8,2560]{2,1,0:T(8,128)S(1)}, f32[2,8,2560]{2,1,0:T(8,128)S(1)}, u32[]{:S(2)}, u32[]{:S(2)}) %collective-permute-start.1) | collective-permute-done | bytes 163872 | tf_op jit(solution)/shard_map/ppermute | solution.py:592
  66.5 0.7 constant_dynamic-update-slice_fusion.2
  67.2 5.5 %all-to-all-start = ((f32[16,2,2,8,8,128]{5,4,3,2,1,0:T(8,128)}), f32[16,2,2,8,8,128]{5,4,3,2,1,0:T(8,128)}, u32[]{:S(2)}, u32[]{:S(2)}) async-start(f32[16,2,2,8,8,128]{5,4,3,2,1,0:T(8,128)} %z_stage.2), calls=%async_computation | async-start | bytes 4194304 | tf_op jit(solution)/shard_map/all_to_all | solution.py:587
  72.7 1.6 %constant_dynamic-update-slice_fusion.1 = f32[8,8,2560]{2,1,0:T(8,128)} fusion(f32[8,8,2560]{2,1,0:T(8,128)} %constant_dynamic-update-slice_fusion.2, f32[2,8,2560]{2,1,0:T(8,128)} %collective-permute-done.2), kind=kLoop, calls=%fused_computation.6 | loop fusion | bytes 327680
  74.3 1.6 %constant_dynamic-update-slice_fusion.particles = f32[8,8,2560]{2,1,0:T(8,128)} fusion(f32[8,8,2560]{2,1,0:T(8,128)} %constant_dynamic-update-slice_fusion.1, f32[2,8,2560]{2,1,0:T(8,128)} %collective-permute-done.3), kind=kLoop, calls=%fused_computation.5 | loop fusion | bytes 327680 | tf_op jit(solution)/shard_map/concatenate | solution.py:593
  75.9 1.0 fusion.1
  77.1 0.7 fusion.3
  78.5 0.1 select_reduce_fusion.1
  78.6 0.1 select_reduce_fusion
  78.7 0.1 select_reduce_fusion.2
  78.8 1.3 concatenate.8.place.refs_0_
  80.1 17.6 %row_stage.1 = (f32[82,64,256]{2,1,0:T(8,128)}, bf16[82,768,256]{2,1,0:T(8,128)(2,1)}) custom-call(s32[249]{0:T(256)} %concatenate.8.place.refs_0_, f32[8,8,2560]{2,1,0:T(8,128)} %constant_dynamic-update-slice_fusion.particles, bf16[64,768]{1,0:T(8,128)(2,1)} %dynamic-slice_bitcast_fusion.table), custom_call_target="tpu_custom_call" | custom-call | tf_op jit(solution)/shard_map/row_stage/pallas_call | solution.py:296
  97.8 14.6 %field_stage.2.refs_7_ = f32[8,8,2560]{2,1,0:T(8,128)} custom-call(s32[249]{0:T(256)} %concatenate.8.place.refs_0_, f32[16,3,2,8,8,128]{5,4,3,2,1,0:T(8,128)} %copy-done, f32[16,3,2,8,8,128]{5,4,3,2,1,0:T(8,128)} %copy-done, bf16[256,768]{1,0:T(8,128)(2,1)} %constant.72.clone.refs_3_, bf16[256,768]{1,0:T(8,128)(2,1)} %constant.73.clone.refs_4_, ...), custom_call_target="tpu_custom_call" | custom-call | tf_op jit(solution)/shard_map/field_stage/pallas_call | solution.py:479
  112.4 14.8 %field_stage.3 = f32[8,8,2560]{2,1,0:T(8,128)} custom-call(s32[249]{0:T(256)} %concatenate.8.place.refs_0_, f32[16,2,2,8,8,128]{5,4,3,2,1,0:T(8,128)} %all-to-all-done.refs_1_, f32[16,3,2,8,8,128]{5,4,3,2,1,0:T(8,128)} %copy-done, bf16[256,768]{1,0:T(8,128)(2,1)} %constant.72.clone.refs_3_, bf16[256,768]{1,0:T(8,128)(2,1)} %constant.73.clone.refs_4_, ...), custom_call_target="tpu_custom_call" | custom-call | tf_op jit(solution)/shard_map/field_stage/pallas_call | solution.py:479
  127.1 14.2 %all_to_all.15.values = f32[8,8,2560]{2,1,0:T(8,128)} all-to-all(f32[8,8,2560]{2,1,0:T(8,128)} %field_stage.3), channel_id=1, replica_groups=mesh['gx'=16,'gy'=8] {'gy'}, dimensions={0} | all-to-all | bytes 1310720 | tf_op jit(solution)/shard_map/all_to_all | solution.py:611
  141.3 2.5 %ghost_stage.1 = (f32[8,2048]{1,0:T(8,128)}, f32[8,2048]{1,0:T(8,128)}) custom-call(s32[1,4]{1,0:T(1,128)} %counts.3, f32[8,8,2560]{2,1,0:T(8,128)} %all_to_all.15.values, s32[3,512]{1,0:T(4,128)} %slots.1), custom_call_target="tpu_custom_call" | custom-call | tf_op jit(solution)/shard_map/ghost_stage/pallas_call | solution.py:521
  143.8 5.5 %collective-permute-start.4 = (f32[8,2048]{1,0:T(8,128)}, f32[8,2048]{1,0:T(8,128)S(1)}, u32[]{:S(2)}, u32[]{:S(2)}) collective-permute-start(f32[8,2048]{1,0:T(8,128)} %get-tuple-element.9), channel_id=1, source_target_pairs={{8,0},{16,8},{24,16},{32,24},{40,32},{48,40},{56,48},{64,56},{72,6... | collective-permute-start | bytes 196616 | tf_op jit(solution)/shard_map/ppermute | solution.py:615
  149.3 1.3 collective-permute-done.4.arrived
  150.6 0.6 copy-done.2
  151.2 1.5 final_stage.1
  (19 shorter events, 0.2 us)
Async XLA Ops:
  7.2 60.0 %all-to-all-start.1 = ((f32[16,3,2,8,8,128]{5,4,3,2,1,0:T(8,128)}), f32[16,3,2,8,8,128]{5,4,3,2,1,0:T(8,128)S(1)}, u32[]{:S(2)}, u32[]{:S(2)}) async-start(f32[16,3,2,8,8,128]{5,4,3,2,1,0:T(8,128)} %z_stage.3), calls=%async_computation.1 | async-start | bytes 6291456 | tf_op jit(solution)/shard_map/all_to_all | solution.py:587
  15.1 9.7 %copy-start.3 = (s32[8]{0:T(128)S(1)}, s32[8]{0:T(128)}, u32[]{:S(2)}) copy-start(s32[8]{0:T(128)} %constant.75) | copy-start | bytes 100
  16.6 8.1 %copy-start.1 = (f32[8,2560]{1,0:T(8,128)S(1)}, f32[8,2560]{1,0:T(8,128)}, u32[]{:S(2)}) copy-start(f32[8,2560]{1,0:T(8,128)} %gather_stage.1) | copy-start | bytes 245764
  16.6 39.2 %collective-permute-start = (f32[8,2560]{1,0:T(8,128)}, f32[8,2560]{1,0:T(8,128)S(1)}, u32[]{:S(2)}, u32[]{:S(2)}) collective-permute-start(f32[8,2560]{1,0:T(8,128)} %gather_stage.1), channel_id=1, source_target_pairs={{0,1},{1,0},{2,3},{3,2},{4,5},{5,4},{6,7},{7,6},{8,9},{9,8},{10,11... | collective-permute-start | bytes 245768 | tf_op jit(solution)/shard_map/ppermute | solution.py:577
  55.8 18.6 %collective-permute-start.3 = (f32[2,8,2560]{2,1,0:T(8,128)S(1)}, f32[2,8,2560]{2,1,0:T(8,128)}, u32[]{:S(2)}, u32[]{:S(2)}) collective-permute-start(f32[2,8,2560]{2,1,0:T(8,128)S(1)} %pad_maximum_fusion), channel_id=1, source_target_pairs={{0,4},{1,5},{2,6},{3,7},{4,0},{5,1},{6,2},{7,3},{8,12},{9,13},{10,... | collective-permute-start | bytes 491528 | tf_op jit(solution)/shard_map/ppermute | solution.py:592
  58.6 14.1 %collective-permute-start.2 = (f32[2,8,2560]{2,1,0:T(8,128)S(1)}, f32[2,8,2560]{2,1,0:T(8,128)}, u32[]{:S(2)}, u32[]{:S(2)}) collective-permute-start(f32[2,8,2560]{2,1,0:T(8,128)S(1)} %pad_maximum_fusion), channel_id=1, source_target_pairs={{0,6},{1,7},{2,0},{3,1},{4,2},{5,3},{6,4},{7,5},{8,14},{9,15},{10,... | collective-permute-start | bytes 491528 | tf_op jit(solution)/shard_map/ppermute | solution.py:592
  59.5 7.1 %collective-permute-start.1 = (f32[2,8,2560]{2,1,0:T(8,128)S(1)}, f32[2,8,2560]{2,1,0:T(8,128)S(1)}, u32[]{:S(2)}, u32[]{:S(2)}) collective-permute-start(f32[2,8,2560]{2,1,0:T(8,128)S(1)} %pad_maximum_fusion), channel_id=1, source_target_pairs={{0,2},{1,3},{2,4},{3,5},{4,6},{5,7},{6,0},{7,1},{8,10},{9,11},{10,... | collective-permute-start | bytes 491528 | tf_op jit(solution)/shard_map/ppermute | solution.py:592
  67.2 30.6 %copy-start = (f32[16,3,2,8,8,128]{5,4,3,2,1,0:T(8,128)}, f32[16,3,2,8,8,128]{5,4,3,2,1,0:T(8,128)S(1)}, u32[]{:S(2)}) copy-start(f32[16,3,2,8,8,128]{5,4,3,2,1,0:T(8,128)S(1)} %all-to-all-done.1.refs_1_.refs_2_) | copy-start | bytes 9437188
  67.2 45.2 %all-to-all-start = ((f32[16,2,2,8,8,128]{5,4,3,2,1,0:T(8,128)}), f32[16,2,2,8,8,128]{5,4,3,2,1,0:T(8,128)}, u32[]{:S(2)}, u32[]{:S(2)}) async-start(f32[16,2,2,8,8,128]{5,4,3,2,1,0:T(8,128)} %z_stage.2), calls=%async_computation | async-start | bytes 4194304 | tf_op jit(solution)/shard_map/all_to_all | solution.py:587
  143.8 6.8 %collective-permute-start.4 = (f32[8,2048]{1,0:T(8,128)}, f32[8,2048]{1,0:T(8,128)S(1)}, u32[]{:S(2)}, u32[]{:S(2)}) collective-permute-start(f32[8,2048]{1,0:T(8,128)} %get-tuple-element.9), channel_id=1, source_target_pairs={{8,0},{16,8},{24,16},{32,24},{40,32},{48,40},{56,48},{64,56},{72,6... | collective-permute-start | bytes 196616 | tf_op jit(solution)/shard_map/ppermute | solution.py:615
  150.6 0.6 copy-start.2
